TPU v7x, 128 devices: a whole 4x4x4 slice. The times are simulated.
128 devices in a mesh: row: 8 (over x_hi, z), col: 16 (over y, x_lo, core).
Axes of the slice: x: 4 (x_hi: 2, x_lo: 2; x = x_hi * 2 + x_lo), y: 4, z: 4, core: 2. Of those that a mesh axis runs over, the one named last changes fastest.
Arguments:
- object_field: bfloat16 [2, 4096, 8192], P(None, 'row', 'col'), may hold values from -6 to 6
- probe_modes: float32 [2, 2, 256, 256], replicated, may hold values from -6 to 6
- measured_amp: bfloat16 [8, 16, 8, 256, 256], P('row', 'col'), may hold values from 0.25 to 8
- scan_positions: int32 [8, 16, 2, 8], P('row', 'col'), may hold values from 0 to 512
- frame_counts: int32 [8, 16], P('row', 'col'), may hold values from 1 to 8, as said below
Outputs:
- object_grad: float32 [2, 4096, 8192], P(None, 'row', 'col')
- probe_grad: float32 [2, 2, 256, 256], replicated
Inputs may be any that keep to these rules, and one draw needn't show every extreme that they name: `frame_counts`: live frames of a tile; slots at or past it are ignored; some tile has exactly 8.
All inputs are finite; a program needn't handle non-finite values.
Results may differ from a plain program's by a relative error of at most 0.0059.
The roundings to bfloat16 on the way count: a program that leaves them out, or rounds other values in their place, can miss the bound.
Values may be sent and summed in bfloat16 or wider, within the bound.
No kernel may reach another device: no remote copies, remote signals or barrier semaphores. Data moves between devices by JAX's collectives and lax.ppermute only.
A program may use at most 64 MiB of HBM per device.

v0:
```python
import math

import jax
import jax.numpy as jnp
from jax import lax
from jax.sharding import PartitionSpec as P

HALO = 128


def with_halo(value, sides, width):
    for axis, dim in sides:
        devices, length = (lax.axis_size(axis), value.shape[dim])
        up = [(i, (i + 1) % devices) for i in range(devices - 1)]
        down = [(j, i) for i, j in up]
        last = lax.slice_in_dim(value, length - width, length, axis=dim)
        leading = lax.slice_in_dim(value, 0, width, axis=dim)
        before = lax.ppermute(last, axis, up)
        after = lax.ppermute(leading, axis, down)
        value = jnp.concatenate([before, value, after], axis=dim)
    return value


def from_behind(value, axis, by):
    devices = lax.axis_size(axis)
    pairs = [(i, i + by) for i in range(devices) if 0 <= i + by < devices]
    return lax.ppermute(value, axis, pairs)


def fourier_tables(frame_side):
    indices = jnp.arange(frame_side, dtype=jnp.int32)
    product = indices[:, None] * indices[None, :] % frame_side
    angles = 2.0 * math.pi / frame_side * product.astype(jnp.float32)
    norm_scale = 1.0 / math.sqrt(frame_side)
    return (
        (jnp.cos(angles) * norm_scale).astype(jnp.bfloat16),
        (-jnp.sin(angles) * norm_scale).astype(jnp.bfloat16),
    )


def left_mul(table, data):
    return jnp.einsum("kn,mnj->mkj", table, data, preferred_element_type=jnp.float32)


def right_mul(data, table):
    return jnp.einsum("mkn,nj->mkj", data, table, preferred_element_type=jnp.float32)


def transform(real_part, imag_part, table_real, table_imag):
    first_real = (left_mul(table_real, real_part) - left_mul(table_imag, imag_part)).astype(
        jnp.bfloat16
    )
    first_imag = (left_mul(table_real, imag_part) + left_mul(table_imag, real_part)).astype(
        jnp.bfloat16
    )
    out_real = right_mul(first_real, table_real) - right_mul(first_imag, table_imag)
    out_imag = right_mul(first_real, table_imag) + right_mul(first_imag, table_real)
    return (out_real, out_imag)


def frame_terms(frame_patch, frame_amp, probe_modes, table_real, table_imag):
    probe_real = probe_modes[0]
    probe_imag = probe_modes[1]
    patch_real = frame_patch[0].astype(jnp.float32)
    patch_imag = frame_patch[1].astype(jnp.float32)
    exit_real = (probe_real * patch_real - probe_imag * patch_imag).astype(jnp.bfloat16)
    exit_imag = (probe_real * patch_imag + probe_imag * patch_real).astype(jnp.bfloat16)
    psi_real, psi_imag = transform(exit_real, exit_imag, table_real, table_imag)
    power = jnp.sum(psi_real * psi_real + psi_imag * psi_imag, axis=0)
    factor = 1.0 - frame_amp.astype(jnp.float32) / jnp.maximum(jnp.sqrt(power), 0.5)
    chi_real = (psi_real * factor).astype(jnp.bfloat16)
    chi_imag = (psi_imag * factor).astype(jnp.bfloat16)
    back_real, back_imag = transform(chi_real, chi_imag, table_real, -table_imag)
    patch_grad = jnp.stack(
        [
            jnp.sum(probe_real * back_real + probe_imag * back_imag, axis=0),
            jnp.sum(probe_real * back_imag - probe_imag * back_real, axis=0),
        ]
    )
    probe_term = jnp.stack(
        [
            patch_real * back_real + patch_imag * back_imag,
            patch_real * back_imag - patch_imag * back_real,
        ]
    )
    return (patch_grad, probe_term)


def shards(object_field, probe_modes, measured_amp, scan_positions, frame_counts):
    frame_side = probe_modes.shape[-1]
    slot_count = measured_amp.shape[2]
    tile_side = object_field.shape[1]
    extended = with_halo(object_field, (("row", 1), ("col", 2)), HALO)
    amplitudes = measured_amp[0, 0]
    row_starts = scan_positions[0, 0, 0]
    col_starts = scan_positions[0, 0, 1]
    live_count = frame_counts[0, 0]
    table_real, table_imag = fourier_tables(frame_side)

    def advance(slot_at, state_pair):
        gradient, probe_total = state_pair
        row_at = row_starts[slot_at]
        column_at = col_starts[slot_at]
        frame_patch = lax.dynamic_slice(
            extended, (0, row_at, column_at), (2, frame_side, frame_side)
        )
        frame_amp = lax.dynamic_index_in_dim(amplitudes, slot_at, 0, keepdims=False)
        patch_grad, probe_term = frame_terms(
            frame_patch, frame_amp, probe_modes, table_real, table_imag
        )
        old_block = lax.dynamic_slice(gradient, (0, row_at, column_at), (2, frame_side, frame_side))
        gradient = lax.dynamic_update_slice(
            gradient, old_block + patch_grad, (0, row_at, column_at)
        )
        return (gradient, probe_total + probe_term)

    gradient = jnp.zeros((2, tile_side + 2 * HALO, tile_side + 2 * HALO), jnp.float32)
    probe_zero = jnp.zeros(probe_modes.shape, jnp.float32)
    gradient, probe_local = lax.fori_loop(
        jnp.zeros((), jnp.int32), live_count, advance, (gradient, probe_zero)
    )
    low_end = tile_side + HALO
    from_above = from_behind(gradient[:, low_end:, :].astype(jnp.bfloat16), "row", 1).astype(
        jnp.float32
    )
    from_below = from_behind(gradient[:, :HALO, :].astype(jnp.bfloat16), "row", -1).astype(
        jnp.float32
    )
    middle = gradient[:, HALO:low_end, :]
    middle = middle.at[:, :HALO, :].add(from_above)
    middle = middle.at[:, tile_side - HALO :, :].add(from_below)
    from_left = from_behind(middle[:, :, low_end:].astype(jnp.bfloat16), "col", 1).astype(
        jnp.float32
    )
    from_right = from_behind(middle[:, :, :HALO].astype(jnp.bfloat16), "col", -1).astype(
        jnp.float32
    )
    interior = middle[:, :, HALO:low_end]
    interior = interior.at[:, :, :HALO].add(from_left)
    interior = interior.at[:, :, tile_side - HALO :].add(from_right)
    probe_total = lax.psum(probe_local, ("row", "col"))
    norm_scale = 1.0 / math.sqrt(lax.axis_size("row") * lax.axis_size("col") * slot_count)
    return (interior, probe_total * norm_scale)


def solution(mesh):
    in_specs = (
        P(None, "row", "col"),
        P(),
        P("row", "col", None, None, None),
        P("row", "col", None, None),
        P("row", "col"),
    )
    out_specs = (P(None, "row", "col"), P())
    return jax.shard_map(shards, mesh=mesh, in_specs=in_specs, out_specs=out_specs, check_vma=False)
```

profile of v0, /device:TPU:1, one launch (start us, length us, event | category | flops | bytes accessed | tf_op | source)
XLA Modules:
  0.0 501.4 jit_solution(10045798548236359964)
XLA Ops:
  8.3 4.4 collective-permute-start
  14.0 3.6 collective-permute-done
  18.9 2.9 collective-permute-done.1
  22.0 4.7 collective-permute-start.2
  26.7 1.9 collective-permute-start.3
  28.6 2.7 collective-permute-done.2
  31.4 5.9 %collective-permute-done.3 = bf16[2,768,128]{2,1,0:T(8,128)(2,1)S(1)} collective-permute-done((bf16[2,768,128]{2,1,0:T(8,128)(2,1)S(1)}, bf16[2,768,128]{2,1,0:T(8,128)(2,1)S(1)}, u32[]{:S(2)}, u32[]{:S(2)}) %collective-permute-start.3) | collective-permute-done | bytes 393248 | tf_op jit(solution)/shard_map/ppermute | solution.py:19
  39.0 2.4 broadcast_in_dim.4
  41.5 143.7 %while.19 = (s32[]{:T(128)}, f32[2,768,768]{2,1,0:T(8,128)}, f32[2,2,256,256]{3,2,1,0:T(8,128)S(1)}, s32[]{:T(128)}, s32[8]{0:T(128)S(1)}, /*index=5*/s32[8]{0:T...) while((s32[]{:T(128)}, f32[2,768,768]{2,1,0:T(8,128)}, ...), condition=%wide.region_4.5_spmd.clone.clone, body=%wide.region_0.4_spmd.clone.clone.sunk | while | flops 1098842112 | bytes 31064372 | solution.py:119
  70.6 6.5 %dynamic_update_slice.7 = f32[2,768,768]{2,1,0:T(8,128)} dynamic-update-slice(f32[2,768,768]{2,1,0:T(8,128)} %get-tuple-element.399, f32[2,256,256]{2,1,0:T(8,128)S(1)} %maximum_add_fusion.4, s32[]{:T(128)} %constant.148.clone.1..sunk, s32[]{:T(128)S(6)} %select_n.158, s32[]{:T(128)S(6)} %select_n.159) | dynamic-update-slice | bytes 1048580 | tf_op jit(solution)/shard_map/while/body/dynamic_update_slice | solution.py:112
  106.3 6.8 %dynamic_update_slice.7 = f32[2,768,768]{2,1,0:T(8,128)} dynamic-update-slice(f32[2,768,768]{2,1,0:T(8,128)} %get-tuple-element.399, f32[2,256,256]{2,1,0:T(8,128)S(1)} %maximum_add_fusion.4, s32[]{:T(128)} %constant.148.clone.1..sunk, s32[]{:T(128)S(6)} %select_n.158, s32[]{:T(128)S(6)} %select_n.159) | dynamic-update-slice | bytes 1048580 | tf_op jit(solution)/shard_map/while/body/dynamic_update_slice | solution.py:112
  142.3 6.5 %dynamic_update_slice.7 = f32[2,768,768]{2,1,0:T(8,128)} dynamic-update-slice(f32[2,768,768]{2,1,0:T(8,128)} %get-tuple-element.399, f32[2,256,256]{2,1,0:T(8,128)S(1)} %maximum_add_fusion.4, s32[]{:T(128)} %constant.148.clone.1..sunk, s32[]{:T(128)S(6)} %select_n.158, s32[]{:T(128)S(6)} %select_n.159) | dynamic-update-slice | bytes 1048580 | tf_op jit(solution)/shard_map/while/body/dynamic_update_slice | solution.py:112
  178.0 6.5 %dynamic_update_slice.7 = f32[2,768,768]{2,1,0:T(8,128)} dynamic-update-slice(f32[2,768,768]{2,1,0:T(8,128)} %get-tuple-element.399, f32[2,256,256]{2,1,0:T(8,128)S(1)} %maximum_add_fusion.4, s32[]{:T(128)} %constant.148.clone.1..sunk, s32[]{:T(128)S(6)} %select_n.158, s32[]{:T(128)S(6)} %select_n.159) | dynamic-update-slice | bytes 1048580 | tf_op jit(solution)/shard_map/while/body/dynamic_update_slice | solution.py:112
  185.2 3.0 convert.10
  188.2 146.3 %collective-permute-start.4 = (bf16[2,128,768]{2,1,0:T(8,128)(2,1)S(1)}, bf16[2,128,768]{2,1,0:T(8,128)(2,1)S(1)}, u32[]{:S(2)}, u32[]{:S(2)}) collective-permute-start(bf16[2,128,768]{2,1,0:T(8,128)(2,1)S(1)} %get-tuple-element.299), channel_id=1, source_target_pairs={{0,16},{16,32},{32,48},{48,64},{64,80},{80,96},{96,112},{1,17},{17... | collective-permute-start | bytes 1179656 | tf_op jit(solution)/shard_map/ppermute | solution.py:27
  335.8 1.8 slice.160
  339.2 2.1 add_dynamic-update-slice_fusion
  341.3 2.0 collective-permute-done.5
  343.3 2.1 fusion.142
  345.4 2.2 convert.11
  348.5 1.9 collective-permute-start.7
  350.5 3.6 collective-permute-start.6
  354.1 135.5 %all-reduce.2.cloned.1.call-done = f32[2,2,256,256]{3,2,1,0:T(8,128)} async-done(((f32[2,2,256,256]{3,2,1,0:T(8,128)}), f32[2,2,256,256]{3,2,1,0:T(8,128)}) %all-reduce.2.cloned.1.call-update) | async-done | bytes 1048592 | tf_op jit(solution)/shard_map/psum | solution.py:141
  489.7 2.3 broadcast_multiply_fusion
  (124 shorter events, 110.1 us)
Async XLA Ops:
  7.2 482.5 %all-reduce.2.cloned.1.call-start = ((), (), s32[]{:S(2)}) async-start(), calls=%async_computation | async-start | bytes 2097152 | tf_op jit(solution)/shard_map/psum | solution.py:141
  8.3 9.3 %collective-permute-start = (bf16[2,128,512]{2,1,0:T(8,128)(2,1)S(1)}, bf16[2,128,512]{2,1,0:T(8,128)(2,1)S(1)}, u32[]{:S(2)}, u32[]{:S(2)}) collective-permute-start(bf16[2,128,512]{2,1,0:T(8,128)(2,1)S(1)} %get-tuple-element.305), channel_id=1, source_target_pairs={{0,16},{16,32},{32,48},{48,64},{64,80},{80,96},{96,112},{1,17},{17... | collective-permute-start | bytes 786440 | tf_op jit(solution)/shard_map/ppermute | solution.py:18
  12.7 15.9 %copy-start.5 = (s32[1,1,2,8]{3,2,1,0:T(2,128)S(1)}, s32[1,1,2,8]{3,2,1,0:T(2,128)}, u32[]{:S(2)}) copy-start(s32[1,1,2,8]{3,2,1,0:T(2,128)} %param.18) | copy-start | bytes 196
  12.7 9.1 %collective-permute-start.1 = (bf16[2,128,512]{2,1,0:T(8,128)(2,1)S(1)}, bf16[2,128,512]{2,1,0:T(8,128)(2,1)S(1)}, u32[]{:S(2)}, u32[]{:S(2)}) collective-permute-start(bf16[2,128,512]{2,1,0:T(8,128)(2,1)S(1)} %get-tuple-element.304), channel_id=1, source_target_pairs={{16,0},{32,16},{48,32},{64,48},{80,64},{96,80},{112,96},{17,1},{33... | collective-permute-start | bytes 786440 | tf_op jit(solution)/shard_map/ppermute | solution.py:19
  22.0 9.4 %collective-permute-start.2 = (bf16[2,768,128]{2,1,0:T(8,128)(2,1)S(1)}, bf16[2,768,128]{2,1,0:T(8,128)(2,1)S(1)}, u32[]{:S(2)}, u32[]{:S(2)}) collective-permute-start(bf16[2,768,128]{2,1,0:T(8,128)(2,1)S(1)} %get-tuple-element.302), channel_id=1, source_target_pairs={{0,1},{1,2},{2,3},{3,4},{4,5},{5,6},{6,7},{7,8},{8,9},{9,10},{10,1... | collective-permute-start | bytes 1179656 | tf_op jit(solution)/shard_map/ppermute | solution.py:18
  26.7 10.6 %collective-permute-start.3 = (bf16[2,768,128]{2,1,0:T(8,128)(2,1)S(1)}, bf16[2,768,128]{2,1,0:T(8,128)(2,1)S(1)}, u32[]{:S(2)}, u32[]{:S(2)}) collective-permute-start(bf16[2,768,128]{2,1,0:T(8,128)(2,1)S(1)} %get-tuple-element.303), channel_id=1, source_target_pairs={{1,0},{2,1},{3,2},{4,3},{5,4},{6,5},{7,6},{8,7},{9,8},{10,9},{11,1... | collective-permute-start | bytes 1179656 | tf_op jit(solution)/shard_map/ppermute | solution.py:19
  39.0 2.4 copy-start
  185.1 3.0 copy-start.2
  185.1 150.6 %copy-start.1 = (f32[2,768,768]{2,1,0:T(8,128)S(1)}, f32[2,768,768]{2,1,0:T(8,128)}, u32[]{:S(2)}) copy-start(f32[2,768,768]{2,1,0:T(8,128)} %get-tuple-element.198) | copy-start | bytes 14155780
  188.2 151.0 %collective-permute-start.4 = (bf16[2,128,768]{2,1,0:T(8,128)(2,1)S(1)}, bf16[2,128,768]{2,1,0:T(8,128)(2,1)S(1)}, u32[]{:S(2)}, u32[]{:S(2)}) collective-permute-start(bf16[2,128,768]{2,1,0:T(8,128)(2,1)S(1)} %get-tuple-element.299), channel_id=1, source_target_pairs={{0,16},{16,32},{32,48},{48,64},{64,80},{80,96},{96,112},{1,17},{17... | collective-permute-start | bytes 1179656 | tf_op jit(solution)/shard_map/ppermute | solution.py:27
  334.5 8.8 %collective-permute-start.5 = (bf16[2,128,768]{2,1,0:T(8,128)(2,1)S(1)}, bf16[2,128,768]{2,1,0:T(8,128)(2,1)S(1)}, u32[]{:S(2)}, u32[]{:S(2)}) collective-permute-start(bf16[2,128,768]{2,1,0:T(8,128)(2,1)S(1)} %get-tuple-element.298), channel_id=1, source_target_pairs={{16,0},{32,16},{48,32},{64,48},{80,64},{96,80},{112,96},{17,1},{33... | collective-permute-start | bytes 1179656 | tf_op jit(solution)/shard_map/ppermute | solution.py:27
  345.4 2.8 copy-start.3
  348.5 144.5 %collective-permute-start.7 = (bf16[2,512,128]{2,1,0:T(8,128)(2,1)S(1)}, bf16[2,512,128]{2,1,0:T(8,128)(2,1)S(1)}, u32[]{:S(2)}, u32[]{:S(2)}) collective-permute-start(bf16[2,512,128]{2,1,0:T(8,128)(2,1)S(1)} %get-tuple-element.300), channel_id=1, source_target_pairs={{1,0},{2,1},{3,2},{4,3},{5,4},{6,5},{7,6},{8,7},{9,8},{10,9},{11,1... | collective-permute-start | bytes 786440 | tf_op jit(solution)/shard_map/ppermute | solution.py:27
  350.5 141.5 %collective-permute-start.6 = (bf16[2,512,128]{2,1,0:T(8,128)(2,1)S(1)}, bf16[2,512,128]{2,1,0:T(8,128)(2,1)S(1)}, u32[]{:S(2)}, u32[]{:S(2)}) collective-permute-start(bf16[2,512,128]{2,1,0:T(8,128)(2,1)S(1)} %get-tuple-element.301), channel_id=1, source_target_pairs={{0,1},{1,2},{2,3},{3,4},{4,5},{5,6},{6,7},{7,8},{8,9},{9,10},{10,1... | collective-permute-start | bytes 786440 | tf_op jit(solution)/shard_map/ppermute | solution.py:27
  493.2 1.3 copy-start.4
Sparse Core Ops, SparseCore 0:
  337.8 151.8 all-reduce.1
where the time goes:
time: 504 us; the launch traced here: 501 us
  starting transfers between devices  165 us (33%)
  waiting for transfers between devices  154 us (31%)
  matrix products  77.3 us (15%)
  local copies, waits for them, and re-layouts  40.3 us (8%)
  other arithmetic  30.5 us (6%)
  loops' own time  19.2 us (4%)
  between operations  14.3 us (3%)
    ppermute x4, starting transfers between devices, from_behind(): return lax.ppermute(value, axis, pairs)  153 us
    psum x1, waiting for transfers between devices, shards(): probe_total = lax.psum(probe_local, ('row', 'col'))  136 us
    dot_general x32, matrix products, right_mul(): jnp.einsum('mkn,nj->mkj', data, table, preferred_element_type=jnp.float32)  39.1 us
    dot_general x32, matrix products, left_mul(): jnp.einsum('kn,mnj->mkj', table, data, preferred_element_type=jnp.float32)  38.2 us
    dynamic_update_slice x4, local copies, waits for them, and re-layouts, advance(): lax.dynamic_update_slice(gradient, old_block + patch_grad, (0, row_at, co...  26.4 us
    another operation x1, loops' own time, shards(): lax.fori_loop(jnp.zeros((), jnp.int32), live_count, advance, (gradient, p...  19.2 us
  transfers between devices with their start and end apart: 9, of which 7 were waited for; matrix products, arithmetic and copies ran while one was open for 3% of the time, Pallas kernels for 0%

commit v1 on v0

v1 whole, which is shorter than its diff:
```python
import math

import jax
import jax.numpy as jnp
import numpy as np
from jax import lax
from jax.experimental import pallas as pl
from jax.experimental.pallas import tpu as pltpu
from jax.sharding import Mesh
from jax.sharding import PartitionSpec as P

HALO = 128
LANES = 128
CHUNK = 16
BF16 = jnp.bfloat16
F32 = jnp.float32
COL = ("colc", "core")
PEERS = ("row", "colc")
VM = pl.BlockSpec(memory_space=pltpu.VMEM)
SM = pl.BlockSpec(memory_space=pltpu.SMEM)


def fourier_tables(side):
    indices = np.arange(side)
    angles = 2.0 * math.pi / side * (indices[:, None] * indices[None, :] % side)
    real = jnp.asarray((np.cos(angles) / math.sqrt(side)).astype(np.float32)).astype(BF16)
    imag = jnp.asarray((-np.sin(angles) / math.sqrt(side)).astype(np.float32)).astype(BF16)
    return jnp.block([[real, -imag], [imag, real]]), jnp.block([[real, imag], [-imag, real]])


def matmul(a, b):
    return jnp.dot(a, b, preferred_element_type=F32)


def frames_kernel(
    meta_ref, pos_ref, mid_ref, row_a_ref, row_b_ref, col_a_ref, col_b_ref, probe_ref, amp_ref, lt_ref, rt_ref,
    main_ref, out_a_ref, out_b_ref, keep_ref, send_ref,
    ext, grad, pgrad, stage, firsts,
):
    side = probe_ref.shape[-1]
    modes = probe_ref.shape[1]
    tile = mid_ref.shape[1]
    nblk = tile // LANES
    count, row_odd, core = meta_ref[0], meta_ref[1], meta_ref[2]
    row_a = pl.multiple_of((1 - row_odd) * (HALO + tile), HALO)
    row_b = pl.multiple_of(row_odd * (HALO + tile), HALO)
    col_a = (1 - core) * (nblk + 1)
    col_b = core * (nblk + 1)
    for c in range(2):
        for b in range(nblk):
            cols = slice(b * LANES, (b + 1) * LANES)
            ext[c, b + 1, pl.ds(row_a, HALO), :] = row_a_ref[c, :, cols].astype(F32)
            ext[c, b + 1, HALO : HALO + tile, :] = mid_ref[c, :, cols].astype(F32)
            ext[c, b + 1, pl.ds(row_b, HALO), :] = row_b_ref[c, :, cols].astype(F32)
        ext[c, col_a] = col_a_ref[c].astype(F32)
        ext[c, col_b] = col_b_ref[c].astype(F32)
    grad[...] = jnp.zeros_like(grad)
    pgrad[...] = jnp.zeros_like(pgrad)
    lane = lax.broadcasted_iota(jnp.int32, (side, LANES), 1)

    def step(s, carry):
        row = pos_ref[0, s]
        col = pos_ref[1, s]
        cq = col // LANES
        cr = col % LANES
        back_shift = (LANES - cr) % LANES
        keep = lane < LANES - cr
        patch = []
        for c in range(2):
            rolled = [
                pltpu.roll(ext[c, jnp.minimum(cq + j, nblk + 1), pl.ds(row, side), :], back_shift, 1)
                for j in range(side // LANES + 1)
            ]
            patch.append([jnp.where(keep, rolled[j], rolled[j + 1]) for j in range(side // LANES)])
        patch_r = jnp.concatenate(patch[0], axis=1)
        patch_i = jnp.concatenate(patch[1], axis=1)
        for m in range(modes):
            pr = probe_ref[0, m]
            pi = probe_ref[1, m]
            stage[m, 0:side, :] = (pr * patch_r - pi * patch_i).astype(BF16)
            stage[m, side:, :] = (pr * patch_i + pi * patch_r).astype(BF16)
        for m in range(modes):
            f = matmul(lt_ref[...], stage[m]).astype(BF16)
            firsts[m * side : (m + 1) * side, 0:side] = f[:side]
            firsts[m * side : (m + 1) * side, side:] = f[side:]
        psi = matmul(firsts[...], rt_ref[...])
        psi_r = [psi[m * side : (m + 1) * side, :side] for m in range(modes)]
        psi_i = [psi[m * side : (m + 1) * side, side:] for m in range(modes)]
        power = sum(psi_r[m] * psi_r[m] + psi_i[m] * psi_i[m] for m in range(modes))
        factor = 1.0 - amp_ref[s].astype(F32) * lax.rsqrt(jnp.maximum(power, 0.25))
        for m in range(modes):
            stage[m, 0:side, :] = (psi_r[m] * factor).astype(BF16)
            stage[m, side:, :] = (psi_i[m] * factor).astype(BF16)
        for m in range(modes):
            f = matmul(rt_ref[...], stage[m]).astype(BF16)
            firsts[m * side : (m + 1) * side, 0:side] = f[:side]
            firsts[m * side : (m + 1) * side, side:] = f[side:]
        back = matmul(firsts[...], lt_ref[...])
        sum_r = jnp.zeros((side, side), F32)
        sum_i = jnp.zeros((side, side), F32)
        for m in range(modes):
            pr = probe_ref[0, m]
            pi = probe_ref[1, m]
            g_r = back[m * side : (m + 1) * side, :side]
            g_i = back[m * side : (m + 1) * side, side:]
            sum_r = sum_r + (pr * g_r + pi * g_i)
            sum_i = sum_i + (pr * g_i - pi * g_r)
            pgrad[0, m] += patch_r * g_r + patch_i * g_i
            pgrad[1, m] += patch_r * g_i - patch_i * g_r
        for c, v in enumerate((sum_r, sum_i)):
            parts = [pltpu.roll(v[:, j * LANES : (j + 1) * LANES], cr, 1) for j in range(side // LANES)]
            for j in range(side // LANES + 1):
                low = parts[j - 1] if j > 0 else jnp.zeros((side, LANES), F32)
                high = parts[j] if j < side // LANES else jnp.zeros((side, LANES), F32)
                grad[c, cq + j, pl.ds(row, side), :] += jnp.where(lane >= cr, high, low)
        return carry

    lax.fori_loop(0, count, step, 0)
    main_ref[...] = grad[:, 1 : nblk + 1]
    for c in range(2):
        out_a_ref[c] = grad[c, col_a].astype(BF16)
        out_b_ref[c] = grad[c, col_b].astype(BF16)
    for m in range(modes):
        for i in range(side // CHUNK):
            for j in range(side // LANES):
                k = (m * (side // CHUNK) + i) * (side // LANES) + j
                at = (slice(i * CHUNK, (i + 1) * CHUNK), slice(j * LANES, (j + 1) * LANES))
                keep_ref[k] = pgrad[core, m, at[0], at[1]]
                send_ref[k] = pgrad[1 - core, m, at[0], at[1]].astype(BF16)


def run_frames(meta, pos, mid, row_a, row_b, col_a, col_b, probe, amp, lt, rt):
    side = probe.shape[-1]
    modes = probe.shape[1]
    tile = mid.shape[1]
    nblk = tile // LANES
    rows = tile + 2 * HALO
    chunks = modes * side * side // (CHUNK * LANES)
    return pl.pallas_call(
        frames_kernel,
        out_shape=(
            jax.ShapeDtypeStruct((2, nblk, rows, LANES), F32),
            jax.ShapeDtypeStruct((2, rows, LANES), BF16),
            jax.ShapeDtypeStruct((2, rows, LANES), BF16),
            jax.ShapeDtypeStruct((chunks, CHUNK, LANES), F32),
            jax.ShapeDtypeStruct((chunks, CHUNK, LANES), BF16),
        ),
        in_specs=[SM, SM] + [VM] * 9,
        out_specs=(VM,) * 5,
        scratch_shapes=[
            pltpu.VMEM((2, nblk + 2, rows, LANES), F32),
            pltpu.VMEM((2, nblk + 3, rows, LANES), F32),
            pltpu.VMEM(probe.shape, F32),
            pltpu.VMEM((modes, 2 * side, side), BF16),
            pltpu.VMEM((modes * side, 2 * side), BF16),
        ],
        compiler_params=pltpu.CompilerParams(vmem_limit_bytes=56 * 1024 * 1024),
        name="frames",
    )(meta, pos, mid, row_a, row_b, col_a, col_b, probe, amp, lt, rt)


def row_margin_kernel(meta_ref, top_ref, bot_ref, got_a_ref, got_b_ref, out_a_ref, out_b_ref):
    nblk = top_ref.shape[1]
    row_odd, core = meta_ref[1], meta_ref[2]
    rows = got_a_ref.shape[1]

    def emit(out_ref, own_ref, start):
        for c in range(2):
            for b in range(nblk):
                out_ref[c, b] = own_ref[c, b].astype(BF16)
            for got_ref, blk in ((got_a_ref, (1 - core) * (nblk - 1)), (got_b_ref, core * (nblk - 1))):
                out_ref[c, blk] = (own_ref[c, blk] + got_ref[c, start : start + HALO, :].astype(F32)).astype(BF16)

    @pl.when(row_odd == 0)
    def _():
        emit(out_a_ref, bot_ref, rows - HALO)
        emit(out_b_ref, top_ref, 0)

    @pl.when(row_odd == 1)
    def _():
        emit(out_a_ref, top_ref, 0)
        emit(out_b_ref, bot_ref, rows - HALO)


def row_margins(meta, main, got_a, got_b):
    nblk, rows = main.shape[1], main.shape[2]
    whole = pl.BlockSpec((2, rows, LANES), lambda i: (0, 0, 0))
    shape = jax.ShapeDtypeStruct((2, nblk, HALO, LANES), BF16)
    edge = lambda at: pl.BlockSpec((2, nblk, HALO, LANES), lambda i: (0, 0, at, 0))
    out = pl.BlockSpec((2, nblk, HALO, LANES), lambda i: (0, 0, 0, 0))
    return pl.pallas_call(
        row_margin_kernel,
        grid=(1,),
        out_shape=(shape, shape),
        in_specs=[SM, edge(0), edge(rows // HALO - 1), whole, whole],
        out_specs=(out, out),
        name="row_margins",
    )(meta, main, main, got_a, got_b)


def pair_sum_kernel(keep_ref, got_ref, out_ref):
    out_ref[...] = (keep_ref[...] + got_ref[...].astype(F32)).astype(BF16)


def pair_sum(keep, got):
    return pl.pallas_call(
        pair_sum_kernel,
        out_shape=jax.ShapeDtypeStruct(keep.shape, BF16),
        in_specs=[VM, VM],
        out_specs=VM,
        name="pair_sum",
    )(keep, got)


def peer_sum_kernel(scale, got_ref, out_ref):
    total = jnp.sum(got_ref[...].astype(F32), axis=0) * scale
    out_ref[...] = jnp.broadcast_to(total.astype(BF16)[None], out_ref.shape)


def peer_sum(got, scale):
    return pl.pallas_call(
        lambda *refs: peer_sum_kernel(scale, *refs),
        out_shape=jax.ShapeDtypeStruct(got.shape, BF16),
        in_specs=[VM],
        out_specs=VM,
        name="peer_sum",
    )(got)


def object_kernel(meta_ref, main_ref, col_a_ref, col_b_ref, row_a_ref, row_b_ref, obj_ref, acc):
    nblk = main_ref.shape[1]
    tile = obj_ref.shape[1]
    row_odd, core = meta_ref[1], meta_ref[2]
    acc[...] = main_ref[:, :, HALO : HALO + tile, :]
    row_a = pl.multiple_of((1 - row_odd) * (tile - HALO), HALO)
    row_b = pl.multiple_of(row_odd * (tile - HALO), HALO)
    for c in range(2):
        acc[c, (1 - core) * (nblk - 1)] += col_a_ref[c, HALO : HALO + tile, :].astype(F32)
        acc[c, core * (nblk - 1)] += col_b_ref[c, HALO : HALO + tile, :].astype(F32)
        for b in range(nblk):
            acc[c, b, pl.ds(row_a, HALO), :] += row_a_ref[c, b].astype(F32)
            acc[c, b, pl.ds(row_b, HALO), :] += row_b_ref[c, b].astype(F32)
        for b in range(nblk):
            obj_ref[c, :, b * LANES : (b + 1) * LANES] = acc[c, b]


def finish_object(meta, main, col_a, col_b, row_a, row_b):
    nblk, rows = main.shape[1], main.shape[2]
    tile = rows - 2 * HALO
    return pl.pallas_call(
        object_kernel,
        out_shape=jax.ShapeDtypeStruct((2, tile, nblk * LANES), F32),
        in_specs=[SM] + [VM] * 5,
        out_specs=VM,
        scratch_shapes=[pltpu.VMEM((2, nblk, tile, LANES), F32)],
        compiler_params=pltpu.CompilerParams(vmem_limit_bytes=40 * 1024 * 1024),
        name="finish_object",
    )(meta, main, col_a, col_b, row_a, row_b)


def probe_kernel(meta_ref, mine_ref, theirs_ref, out_ref):
    core = meta_ref[2]
    modes, side = out_ref.shape[1], out_ref.shape[2]
    for part_ref, at in ((mine_ref, core), (theirs_ref, 1 - core)):
        for m in range(modes):
            for i in range(side // CHUNK):
                for j in range(side // LANES):
                    k = (m * (side // CHUNK) + i) * (side // LANES) + j
                    out_ref[at, m, i * CHUNK : (i + 1) * CHUNK, j * LANES : (j + 1) * LANES] = part_ref[k].astype(F32)


def finish_probe(meta, mine, theirs, shape):
    return pl.pallas_call(
        probe_kernel,
        out_shape=jax.ShapeDtypeStruct(shape, F32),
        in_specs=[SM, VM, VM],
        out_specs=VM,
        name="finish_probe",
    )(meta, mine, theirs)


def trade(value, axis, phase):
    n = lax.axis_size(axis)
    pairs = [(i, ((i + phase) ^ 1) - phase) for i in range(n)]
    return lax.ppermute(value, axis, [(i, j) for i, j in pairs if 0 <= j < n])


def shards(object_field, probe_modes, measured_amp, scan_positions, frame_counts):
    tile = object_field.shape[1]
    slots = measured_amp.shape[2]
    row_odd = lax.axis_index("row") % 2
    core = lax.axis_index("core")
    meta = jnp.stack([frame_counts[0, 0], row_odd, core]).astype(jnp.int32)
    bottom = object_field[:, tile - HALO :, :]
    top = object_field[:, :HALO, :]
    row_a = trade(jnp.where(row_odd == 0, bottom, top), "row", 0)
    row_b = trade(jnp.where(row_odd == 0, top, bottom), "row", 1)
    above = jnp.where(row_odd == 0, row_b, row_a)
    below = jnp.where(row_odd == 0, row_a, row_b)

    def column(lo):
        return jnp.concatenate([v[:, :, lo : lo + HALO] for v in (above, object_field, below)], axis=1)

    right, left = column(tile - HALO), column(0)
    col_a = trade(jnp.where(core == 0, right, left), COL, 0)
    col_b = trade(jnp.where(core == 0, left, right), COL, 1)
    lt, rt = fourier_tables(probe_modes.shape[-1])
    main, out_a, out_b, keep, send = run_frames(
        meta, scan_positions[0, 0], object_field, row_a, row_b, col_a, col_b, probe_modes, measured_amp[0, 0], lt, rt
    )
    scale = 1.0 / math.sqrt(lax.axis_size("row") * lax.axis_size(COL) * slots)
    pair = pair_sum(keep, trade(send, COL, 0))
    got_a = trade(out_a, COL, 0)
    got_b = trade(out_b, COL, 1)
    peers = lax.all_to_all(pair, PEERS, 0, 0, tiled=True)
    rows_a, rows_b = row_margins(meta, main, got_a, got_b)
    back_a = trade(rows_a, "row", 0)
    back_b = trade(rows_b, "row", 1)
    mine = lax.all_to_all(peer_sum(peers, scale), PEERS, 0, 0, tiled=True)
    theirs = trade(mine, COL, 0)
    obj = finish_object(meta, main, got_a, got_b, back_a, back_b)
    return obj, finish_probe(meta, mine, theirs, probe_modes.shape)


def solution(mesh):
    n_col = mesh.shape["col"]
    fine = Mesh(mesh.devices.reshape(mesh.shape["row"], n_col // 2, 2), ("row",) + COL)
    in_specs = (
        P(None, "row", COL),
        P(),
        P("row", COL, None, None, None),
        P("row", COL, None, None),
        P("row", COL),
    )
    out_specs = (P(None, "row", COL), P())
    return jax.shard_map(shards, mesh=fine, in_specs=in_specs, out_specs=out_specs, check_vma=False)
```

time: 504 us -> 109 us (0.22)
  the two profiles are of different devices: /device:TPU:1 before, /device:TPU:4 now
where the time goes in v1:
time: 109 us
  starting transfers between devices  46.8 us (43%)
  Pallas kernels  26.7 us (24%)
  waiting for transfers between devices  25.7 us (24%)
  local copies, waits for them, and re-layouts  6.25 us (6%)
  other arithmetic  1.86 us (2%)
  between operations  1.48 us (1%)
    ppermute x10, starting transfers between devices, trade(): return lax.ppermute(value, axis, [(i, j) for i, j in pairs if 0 <= j < n])  20.8 us
    all_to_all x1, starting transfers between devices, shards(): peers = lax.all_to_all(pair, PEERS, 0, 0, tiled=True)  19 us
    ppermute x10, waiting for transfers between devices, trade(): return lax.ppermute(value, axis, [(i, j) for i, j in pairs if 0 <= j < n])  17.5 us
    pallas_call x1, Pallas kernels, run_frames(): pl.pallas_call(frames_kernel, out_shape=(jax.ShapeDtypeStruct((2, nblk, r...  15.6 us
    all_to_all x1, waiting for transfers between devices, shards(): peers = lax.all_to_all(pair, PEERS, 0, 0, tiled=True)  8.28 us
    all_to_all x1, starting transfers between devices, shards(): mine = lax.all_to_all(peer_sum(peers, scale), PEERS, 0, 0, tiled=True)  7 us
    unnamed x24, local copies, waits for them, and re-layouts  5.12 us
    pallas_call x1, Pallas kernels, finish_object(): pl.pallas_call(object_kernel, out_shape=jax.ShapeDtypeStruct((2, tile, nb...  2.9 us
  transfers between devices with their start and end apart: 12, of which 6 were waited for; matrix products, arithmetic and copies ran while one was open for 2% of the time, Pallas kernels for 7%

profile of v1, /device:TPU:4, one launch (start us, length us, event | category | flops | bytes accessed | tf_op | source)
XLA Modules:
  0.0 108.8 jit_solution(12262009014544025580)
XLA Ops:
  0.6 1.1 broadcast_select_fusion.4
  1.7 2.0 %collective-permute-start = (bf16[2,128,512]{2,1,0:T(8,128)(2,1)S(1)}, bf16[2,128,512]{2,1,0:T(8,128)(2,1)S(1)}, u32[]{:S(2)}, u32[]{:S(2)}) collective-permute-start(bf16[2,128,512]{2,1,0:T(8,128)(2,1)S(1)} %get-tuple-element.19), channel_id=1, source_target_pairs={{0,16},{16,0},{32,48},{48,32},{64,80},{80,64},{96,112},{112,96},{1... | collective-permute-start | bytes 786440 | tf_op jit(solution)/shard_map/ppermute | solution.py:285
  3.7 4.4 %collective-permute-start.1 = (bf16[2,128,512]{2,1,0:T(8,128)(2,1)S(1)}, bf16[2,128,512]{2,1,0:T(8,128)(2,1)S(1)}, u32[]{:S(2)}, u32[]{:S(2)}) collective-permute-start(bf16[2,128,512]{2,1,0:T(8,128)(2,1)S(1)} %get-tuple-element.18), channel_id=1, source_target_pairs={{16,32},{32,16},{48,64},{64,48},{80,96},{96,80},{17,33},{33,17},{4... | collective-permute-start | bytes 786440 | tf_op jit(solution)/shard_map/ppermute | solution.py:285
  8.1 1.1 fusion
  9.2 0.8 collective-permute-done.row_a_ref
  10.0 7.0 %collective-permute-done.1.row_b_ref = bf16[2,128,512]{2,1,0:T(8,128)(2,1)S(1)} collective-permute-done((bf16[2,128,512]{2,1,0:T(8,128)(2,1)S(1)}, bf16[2,128,512]{2,1,0:T(8,128)(2,1)S(1)}, u32[]{:S(2)}, u32[]{:S(2)}) %collective-permute-start.1) | collective-permute-done | bytes 262176 | tf_op jit(solution)/shard_map/ppermute | solution.py:285
  20.2 15.6 %frames.1 = (f32[2,4,768,128]{3,2,1,0:T(8,128)}, bf16[2,768,128]{2,1,0:T(8,128)(2,1)}, bf16[2,768,128]{2,1,0:T(8,128)(2,1)}, f32[64,16,128]{2,1,0:T(8,128)}, bf16[64,16,128]{2,1,0:T(8,128)(2,1)}) custom-call(s32[3]{0:T(128)} %pad_add_fusion.meta_ref, s32[2,8]{1,0:T(2,128)} %bitcast.7, bf16[2,512,512]{2,1,0:T(8,128)(2,1)} %mid_ref.1, ...), custom_call_target="tpu_custom_call" | custom-call | tf_op jit(solution)/shard_map/frames/pallas_call | solution.py:139
  35.8 7.4 %collective-permute-start.8 = (bf16[64,16,128]{2,1,0:T(8,128)(2,1)}, bf16[64,16,128]{2,1,0:T(8,128)(2,1)S(1)}, u32[]{:S(2)}, u32[]{:S(2)}) collective-permute-start(bf16[64,16,128]{2,1,0:T(8,128)(2,1)} %get-tuple-element.15), channel_id=1, source_target_pairs={{0,1},{1,0},{2,3},{3,2},{4,5},{5,4},{6,7},{7,6},{8,9},{9,8},{10,11... | collective-permute-start | bytes 786440 | tf_op jit(solution)/shard_map/ppermute | solution.py:285
  43.3 1.4 %collective-permute-done.8.got_ref = bf16[64,16,128]{2,1,0:T(8,128)(2,1)S(1)} collective-permute-done((bf16[64,16,128]{2,1,0:T(8,128)(2,1)}, bf16[64,16,128]{2,1,0:T(8,128)(2,1)S(1)}, u32[]{:S(2)}, u32[]{:S(2)}) %collective-permute-start.8) | collective-permute-done | bytes 262176 | tf_op jit(solution)/shard_map/ppermute | solution.py:285
  45.3 1.9 %pair_sum.1 = bf16[64,16,128]{2,1,0:T(8,128)(2,1)} custom-call(f32[64,16,128]{2,1,0:T(8,128)} %get-tuple-element.14.keep_ref, bf16[64,16,128]{2,1,0:T(8,128)(2,1)} %copy-done.11), custom_call_target="tpu_custom_call" | custom-call | tf_op jit(solution)/shard_map/pair_sum/pallas_call | solution.py:206
  47.2 19.0 %all-to-all-start = ((bf16[64,16,128]{2,1,0:T(8,128)(2,1)}), bf16[64,16,128]{2,1,0:T(8,128)(2,1)S(1)}, u32[]{:S(2)}, u32[]{:S(2)}) async-start(bf16[64,16,128]{2,1,0:T(8,128)(2,1)} %pair_sum.1), calls=%async_computation | async-start | bytes 524288 | tf_op jit(solution)/shard_map/all_to_all | solution.py:315
  67.0 8.3 %all-to-all-done.refs_0_ = bf16[64,16,128]{2,1,0:T(8,128)(2,1)S(1)} async-done(((bf16[64,16,128]{2,1,0:T(8,128)(2,1)}), bf16[64,16,128]{2,1,0:T(8,128)(2,1)S(1)}, u32[]{:S(2)}, u32[]{:S(2)}) %all-to-all-start) | async-done | bytes 262176 | tf_op jit(solution)/shard_map/all_to_all | solution.py:315
  76.0 1.7 %peer_sum.1 = bf16[64,16,128]{2,1,0:T(8,128)(2,1)} custom-call(bf16[64,16,128]{2,1,0:T(8,128)(2,1)} %copy-done.8), custom_call_target="tpu_custom_call" | custom-call | tf_op jit(solution)/shard_map/peer_sum/pallas_call | solution.py:221
  77.7 7.0 %all-to-all-start.1 = ((bf16[64,16,128]{2,1,0:T(8,128)(2,1)}), bf16[64,16,128]{2,1,0:T(8,128)(2,1)}, u32[]{:S(2)}, u32[]{:S(2)}) async-start(bf16[64,16,128]{2,1,0:T(8,128)(2,1)} %peer_sum.1), calls=%async_computation.1 | async-start | bytes 524288 | tf_op jit(solution)/shard_map/all_to_all | solution.py:319
  84.8 0.8 copy-done.3
  85.6 2.5 %row_margins.1 = (bf16[2,4,128,128]{3,2,1,0:T(8,128)(2,1)}, bf16[2,4,128,128]{3,2,1,0:T(8,128)(2,1)}) custom-call(s32[3]{0:T(128)} %pad_add_fusion.meta_ref, f32[2,4,768,128]{3,2,1,0:T(8,128)} %get-tuple-element.9.top_ref.bot_ref.main_ref, f32[2,4,768,128]{3,2,1,0:T(8,128)} %get-tuple-element.9.top_ref.bot_ref.main_ref, bf16[2,768,128]{2,1,0:T(8,128)(2,1)} %copy-done.1, ...), custom_call_target="tpu_custom_call" | custom-call | tf_op jit(solution)/shard_map/row_margins/pallas_call | solution.py:191
  88.2 1.5 %collective-permute-start.6 = (bf16[2,4,128,128]{3,2,1,0:T(8,128)(2,1)}, bf16[2,4,128,128]{3,2,1,0:T(8,128)(2,1)S(1)}, u32[]{:S(2)}, u32[]{:S(2)}) collective-permute-start(bf16[2,4,128,128]{3,2,1,0:T(8,128)(2,1)} %get-tuple-element.12), channel_id=1, source_target_pairs={{0,16},{16,0},{32,48},{48,32},{64,80},{80,64},{96,112},{112,96},{1... | collective-permute-start | bytes 786440 | tf_op jit(solution)/shard_map/ppermute | solution.py:285
  89.7 3.8 %collective-permute-start.7 = (bf16[2,4,128,128]{3,2,1,0:T(8,128)(2,1)}, bf16[2,4,128,128]{3,2,1,0:T(8,128)(2,1)}, u32[]{:S(2)}, u32[]{:S(2)}) collective-permute-start(bf16[2,4,128,128]{3,2,1,0:T(8,128)(2,1)} %get-tuple-element.13), channel_id=1, source_target_pairs={{16,32},{32,16},{48,64},{64,48},{80,96},{96,80},{17,33},{33,17},{4... | collective-permute-start | bytes 786440 | tf_op jit(solution)/shard_map/ppermute | solution.py:285
  93.6 2.0 %collective-permute-done.6.row_a_ref = bf16[2,4,128,128]{3,2,1,0:T(8,128)(2,1)S(1)} collective-permute-done((bf16[2,4,128,128]{3,2,1,0:T(8,128)(2,1)}, bf16[2,4,128,128]{3,2,1,0:T(8,128)(2,1)S(1)}, u32[]{:S(2)}, u32[]{:S(2)}) %collective-permute-start.6) | collective-permute-done | bytes 262176 | tf_op jit(solution)/shard_map/ppermute | solution.py:285
  95.6 6.3 %collective-permute-done.7.row_b_ref = bf16[2,4,128,128]{3,2,1,0:T(8,128)(2,1)} collective-permute-done((bf16[2,4,128,128]{3,2,1,0:T(8,128)(2,1)}, bf16[2,4,128,128]{3,2,1,0:T(8,128)(2,1)}, u32[]{:S(2)}, u32[]{:S(2)}) %collective-permute-start.7) | collective-permute-done | bytes 262176 | tf_op jit(solution)/shard_map/ppermute | solution.py:285
  101.9 1.0 copy-done.2
  102.9 1.0 copy-done.4
  103.9 2.9 %finish_object.1 = f32[2,512,512]{2,1,0:T(8,128)} custom-call(s32[3]{0:T(128)S(1)} %copy-done.5, f32[2,4,768,128]{3,2,1,0:T(8,128)S(1)} %copy-done, bf16[2,768,128]{2,1,0:T(8,128)(2,1)S(1)} %copy-done.2, bf16[2,768,128]{2,1,0:T(8,128)(2,1)S(1)} %copy-done.4, bf16[2,4,128,128]{3,2,1,0:T(8,128)(2,1)S(1)} %collective-permute-done.6.row_a_ref, ...), custom_call_target="tpu_custom_call" | custom-call | tf_op jit(solution)/shard_map/finish_object/pallas_call | solution.py:250
  106.8 2.1 %finish_probe.1 = f32[2,2,256,256]{3,2,1,0:T(8,128)} custom-call(s32[3]{0:T(128)} %pad_add_fusion.meta_ref, bf16[64,16,128]{2,1,0:T(8,128)(2,1)} %all-to-all-done.1.mine_ref, bf16[64,16,128]{2,1,0:T(8,128)(2,1)} %collective-permute-done.9.theirs_ref), custom_call_target="tpu_custom_call" | custom-call | tf_op jit(solution)/shard_map/finish_probe/pallas_call | solution.py:273
  (36 shorter events, 4.8 us)
Async XLA Ops:
  1.7 8.3 %collective-permute-start = (bf16[2,128,512]{2,1,0:T(8,128)(2,1)S(1)}, bf16[2,128,512]{2,1,0:T(8,128)(2,1)S(1)}, u32[]{:S(2)}, u32[]{:S(2)}) collective-permute-start(bf16[2,128,512]{2,1,0:T(8,128)(2,1)S(1)} %get-tuple-element.19), channel_id=1, source_target_pairs={{0,16},{16,0},{32,48},{48,32},{64,80},{80,64},{96,112},{112,96},{1... | collective-permute-start | bytes 786440 | tf_op jit(solution)/shard_map/ppermute | solution.py:285
  3.7 13.3 %collective-permute-start.1 = (bf16[2,128,512]{2,1,0:T(8,128)(2,1)S(1)}, bf16[2,128,512]{2,1,0:T(8,128)(2,1)S(1)}, u32[]{:S(2)}, u32[]{:S(2)}) collective-permute-start(bf16[2,128,512]{2,1,0:T(8,128)(2,1)S(1)} %get-tuple-element.18), channel_id=1, source_target_pairs={{16,32},{32,16},{48,64},{64,48},{80,96},{96,80},{17,33},{33,17},{4... | collective-permute-start | bytes 786440 | tf_op jit(solution)/shard_map/ppermute | solution.py:285
  10.0 9.3 %copy-start.6 = (bf16[2,128,512]{2,1,0:T(8,128)(2,1)}, bf16[2,128,512]{2,1,0:T(8,128)(2,1)S(1)}, u32[]{:S(2)}) copy-start(bf16[2,128,512]{2,1,0:T(8,128)(2,1)S(1)} %collective-permute-done.row_a_ref) | copy-start | bytes 786436
  17.0 2.3 %copy-start.7 = (bf16[2,128,512]{2,1,0:T(8,128)(2,1)}, bf16[2,128,512]{2,1,0:T(8,128)(2,1)S(1)}, u32[]{:S(2)}) copy-start(bf16[2,128,512]{2,1,0:T(8,128)(2,1)S(1)} %collective-permute-done.1.row_b_ref) | copy-start | bytes 786436
  17.3 2.0 %collective-permute-start.2 = (bf16[2,768,128]{2,1,0:T(8,128)(2,1)S(1)}, bf16[2,768,128]{2,1,0:T(8,128)(2,1)S(1)}, u32[]{:S(2)}, u32[]{:S(2)}) collective-permute-start(bf16[2,768,128]{2,1,0:T(8,128)(2,1)S(1)} %get-tuple-element.21), channel_id=1, source_target_pairs={{0,1},{1,0},{2,3},{3,2},{4,5},{5,4},{6,7},{7,6},{8,9},{9,8},{10,11... | collective-permute-start | bytes 1179656 | tf_op jit(solution)/shard_map/ppermute | solution.py:285
  17.3 1.9 %collective-permute-start.3 = (bf16[2,768,128]{2,1,0:T(8,128)(2,1)S(1)}, bf16[2,768,128]{2,1,0:T(8,128)(2,1)S(1)}, u32[]{:S(2)}, u32[]{:S(2)}) collective-permute-start(bf16[2,768,128]{2,1,0:T(8,128)(2,1)S(1)} %get-tuple-element.20), channel_id=1, source_target_pairs={{1,2},{2,1},{3,4},{4,3},{5,6},{6,5},{7,8},{8,7},{9,10},{10,9},{11,... | collective-permute-start | bytes 1179656 | tf_op jit(solution)/shard_map/ppermute | solution.py:285
  19.3 0.7 copy-start.9
  19.3 0.9 copy-start.10
  35.8 8.8 %collective-permute-start.8 = (bf16[64,16,128]{2,1,0:T(8,128)(2,1)}, bf16[64,16,128]{2,1,0:T(8,128)(2,1)S(1)}, u32[]{:S(2)}, u32[]{:S(2)}) collective-permute-start(bf16[64,16,128]{2,1,0:T(8,128)(2,1)} %get-tuple-element.15), channel_id=1, source_target_pairs={{0,1},{1,0},{2,3},{3,2},{4,5},{5,4},{6,7},{7,6},{8,9},{9,8},{10,11... | collective-permute-start | bytes 786440 | tf_op jit(solution)/shard_map/ppermute | solution.py:285
  44.6 0.7 copy-start.11
  47.2 28.1 %all-to-all-start = ((bf16[64,16,128]{2,1,0:T(8,128)(2,1)}), bf16[64,16,128]{2,1,0:T(8,128)(2,1)S(1)}, u32[]{:S(2)}, u32[]{:S(2)}) async-start(bf16[64,16,128]{2,1,0:T(8,128)(2,1)} %pair_sum.1), calls=%async_computation | async-start | bytes 524288 | tf_op jit(solution)/shard_map/all_to_all | solution.py:315
  66.2 18.5 %collective-permute-start.4 = (bf16[2,768,128]{2,1,0:T(8,128)(2,1)}, bf16[2,768,128]{2,1,0:T(8,128)(2,1)S(1)}, u32[]{:S(2)}, u32[]{:S(2)}) collective-permute-start(bf16[2,768,128]{2,1,0:T(8,128)(2,1)} %get-tuple-element.10), channel_id=1, source_target_pairs={{0,1},{1,0},{2,3},{3,2},{4,5},{5,4},{6,7},{7,6},{8,9},{9,8},{10,11... | collective-permute-start | bytes 1179656 | tf_op jit(solution)/shard_map/ppermute | solution.py:285
  66.3 18.5 %collective-permute-start.5 = (bf16[2,768,128]{2,1,0:T(8,128)(2,1)}, bf16[2,768,128]{2,1,0:T(8,128)(2,1)S(1)}, u32[]{:S(2)}, u32[]{:S(2)}) collective-permute-start(bf16[2,768,128]{2,1,0:T(8,128)(2,1)} %get-tuple-element.11), channel_id=1, source_target_pairs={{1,2},{2,1},{3,4},{4,3},{5,6},{6,5},{7,8},{8,7},{9,10},{10,9},{11,... | collective-permute-start | bytes 1179656 | tf_op jit(solution)/shard_map/ppermute | solution.py:285
  75.3 0.7 copy-start.8
  77.7 15.7 %all-to-all-start.1 = ((bf16[64,16,128]{2,1,0:T(8,128)(2,1)}), bf16[64,16,128]{2,1,0:T(8,128)(2,1)}, u32[]{:S(2)}, u32[]{:S(2)}) async-start(bf16[64,16,128]{2,1,0:T(8,128)(2,1)} %peer_sum.1), calls=%async_computation.1 | async-start | bytes 524288 | tf_op jit(solution)/shard_map/all_to_all | solution.py:319
  84.8 0.9 copy-start.1
  84.8 0.8 copy-start.3
  85.6 16.2 %copy-start = (f32[2,4,768,128]{3,2,1,0:T(8,128)S(1)}, f32[2,4,768,128]{3,2,1,0:T(8,128)}, u32[]{:S(2)}) copy-start(f32[2,4,768,128]{3,2,1,0:T(8,128)} %get-tuple-element.9.top_ref.bot_ref.main_ref) | copy-start | bytes 9437188
  85.6 16.2 %copy-start.5 = (s32[3]{0:T(128)S(1)}, s32[3]{0:T(128)}, u32[]{:S(2)}) copy-start(s32[3]{0:T(128)} %pad_add_fusion.meta_ref) | copy-start | bytes 40
  88.2 7.4 %collective-permute-start.6 = (bf16[2,4,128,128]{3,2,1,0:T(8,128)(2,1)}, bf16[2,4,128,128]{3,2,1,0:T(8,128)(2,1)S(1)}, u32[]{:S(2)}, u32[]{:S(2)}) collective-permute-start(bf16[2,4,128,128]{3,2,1,0:T(8,128)(2,1)} %get-tuple-element.12), channel_id=1, source_target_pairs={{0,16},{16,0},{32,48},{48,32},{64,80},{80,64},{96,112},{112,96},{1... | collective-permute-start | bytes 786440 | tf_op jit(solution)/shard_map/ppermute | solution.py:285
  89.7 12.2 %collective-permute-start.7 = (bf16[2,4,128,128]{3,2,1,0:T(8,128)(2,1)}, bf16[2,4,128,128]{3,2,1,0:T(8,128)(2,1)}, u32[]{:S(2)}, u32[]{:S(2)}) collective-permute-start(bf16[2,4,128,128]{3,2,1,0:T(8,128)(2,1)} %get-tuple-element.13), channel_id=1, source_target_pairs={{16,32},{32,16},{48,64},{64,48},{80,96},{96,80},{17,33},{33,17},{4... | collective-permute-start | bytes 786440 | tf_op jit(solution)/shard_map/ppermute | solution.py:285
  93.5 13.3 %collective-permute-start.9 = (bf16[64,16,128]{2,1,0:T(8,128)(2,1)}, bf16[64,16,128]{2,1,0:T(8,128)(2,1)}, u32[]{:S(2)}, u32[]{:S(2)}) collective-permute-start(bf16[64,16,128]{2,1,0:T(8,128)(2,1)} %all-to-all-done.1.mine_ref), channel_id=1, source_target_pairs={{0,1},{1,0},{2,3},{3,2},{4,5},{5,4},{6,7},{7,6},{8,9},{9,8},{10,11... | collective-permute-start | bytes 786440 | tf_op jit(solution)/shard_map/ppermute | solution.py:285
  101.9 1.0 copy-start.2
  102.9 1.0 copy-start.4

commit v2 on v1

v2 whole, which is shorter than its diff:
```python
import math

import jax
import jax.numpy as jnp
import numpy as np
from jax import lax
from jax.experimental import pallas as pl
from jax.experimental.pallas import tpu as pltpu
from jax.sharding import Mesh
from jax.sharding import PartitionSpec as P

HALO = 128
LANES = 128
CHUNK = 16
BF16 = jnp.bfloat16
F32 = jnp.float32
COL = ("colc", "core")
PEERS = ("row", "colc")
VM = pl.BlockSpec(memory_space=pltpu.VMEM)
SM = pl.BlockSpec(memory_space=pltpu.SMEM)


def fourier_tables(side):
    indices = np.arange(side)
    angles = 2.0 * math.pi / side * (indices[:, None] * indices[None, :] % side)
    real = jnp.asarray((np.cos(angles) / math.sqrt(side)).astype(np.float32)).astype(BF16)
    imag = jnp.asarray((-np.sin(angles) / math.sqrt(side)).astype(np.float32)).astype(BF16)
    return jnp.block([[real, -imag], [imag, real]]), jnp.block([[real, imag], [-imag, real]])


def matmul(a, b):
    return jnp.dot(a, b, preferred_element_type=F32)


def frames_kernel(
    meta_ref, pos_ref, mid_ref, row_a_ref, row_b_ref, col_a_ref, col_b_ref, cor_a_ref, cor_b_ref, probe_ref, amp_ref,
    lt_ref, rt_ref,
    obj_hbm, strip_a_hbm, strip_b_hbm, out_a_hbm, out_b_hbm, send_hbm,
    ext, grad, pgrad, stage, firsts, out_a, out_b, send, sems,
):
    side = probe_ref.shape[-1]
    modes = probe_ref.shape[1]
    tile = mid_ref.shape[1]
    nblk = tile // LANES
    count, row_odd, core = meta_ref[0], meta_ref[1], meta_ref[2]
    row_a = pl.multiple_of((1 - row_odd) * (HALO + tile), HALO)
    row_b = pl.multiple_of(row_odd * (HALO + tile), HALO)
    col_a = (1 - core) * (nblk + 1)
    col_b = core * (nblk + 1)
    for c in range(2):
        for b in range(nblk):
            cols = slice(b * LANES, (b + 1) * LANES)
            ext[c, b + 1, pl.ds(row_a, HALO), :] = row_a_ref[c, :, cols].astype(F32)
            ext[c, b + 1, HALO : HALO + tile, :] = mid_ref[c, :, cols].astype(F32)
            ext[c, b + 1, pl.ds(row_b, HALO), :] = row_b_ref[c, :, cols].astype(F32)
        for col, own_ref, cor_ref in ((col_a, col_a_ref, cor_a_ref), (col_b, col_b_ref, cor_b_ref)):
            ext[c, col, pl.ds(row_a, HALO), :] = cor_ref[c].astype(F32)
            ext[c, col, HALO : HALO + tile, :] = own_ref[c].astype(F32)
            ext[c, col, pl.ds(row_b, HALO), :] = cor_ref[2 + c].astype(F32)
    grad[...] = jnp.zeros_like(grad)
    pgrad[...] = jnp.zeros_like(pgrad)
    lane = lax.broadcasted_iota(jnp.int32, (side, LANES), 1)

    def step(s, carry):
        row = pos_ref[0, s]
        col = pos_ref[1, s]
        cq = col // LANES
        cr = col % LANES
        back_shift = (LANES - cr) % LANES
        keep = lane < LANES - cr
        patch = []
        for c in range(2):
            rolled = [
                pltpu.roll(ext[c, jnp.minimum(cq + j, nblk + 1), pl.ds(row, side), :], back_shift, 1)
                for j in range(side // LANES + 1)
            ]
            patch.append([jnp.where(keep, rolled[j], rolled[j + 1]) for j in range(side // LANES)])
        patch_r = jnp.concatenate(patch[0], axis=1)
        patch_i = jnp.concatenate(patch[1], axis=1)
        for m in range(modes):
            pr = probe_ref[0, m]
            pi = probe_ref[1, m]
            stage[m, 0:side, :] = (pr * patch_r - pi * patch_i).astype(BF16)
            stage[m, side:, :] = (pr * patch_i + pi * patch_r).astype(BF16)
        for m in range(modes):
            f = matmul(lt_ref[...], stage[m]).astype(BF16)
            firsts[m * side : (m + 1) * side, 0:side] = f[:side]
            firsts[m * side : (m + 1) * side, side:] = f[side:]
        psi = matmul(firsts[...], rt_ref[...])
        psi_r = [psi[m * side : (m + 1) * side, :side] for m in range(modes)]
        psi_i = [psi[m * side : (m + 1) * side, side:] for m in range(modes)]
        power = sum(psi_r[m] * psi_r[m] + psi_i[m] * psi_i[m] for m in range(modes))
        factor = 1.0 - amp_ref[s].astype(F32) * lax.rsqrt(jnp.maximum(power, 0.25))
        for m in range(modes):
            stage[m, 0:side, :] = (psi_r[m] * factor).astype(BF16)
            stage[m, side:, :] = (psi_i[m] * factor).astype(BF16)
        for m in range(modes):
            f = matmul(rt_ref[...], stage[m]).astype(BF16)
            firsts[m * side : (m + 1) * side, 0:side] = f[:side]
            firsts[m * side : (m + 1) * side, side:] = f[side:]
        back = matmul(firsts[...], lt_ref[...])
        sum_r = jnp.zeros((side, side), F32)
        sum_i = jnp.zeros((side, side), F32)
        for m in range(modes):
            pr = probe_ref[0, m]
            pi = probe_ref[1, m]
            g_r = back[m * side : (m + 1) * side, :side]
            g_i = back[m * side : (m + 1) * side, side:]
            sum_r = sum_r + (pr * g_r + pi * g_i)
            sum_i = sum_i + (pr * g_i - pi * g_r)
            pgrad[0, m] += patch_r * g_r + patch_i * g_i
            pgrad[1, m] += patch_r * g_i - patch_i * g_r
        for c, v in enumerate((sum_r, sum_i)):
            parts = [pltpu.roll(v[:, j * LANES : (j + 1) * LANES], cr, 1) for j in range(side // LANES)]
            for j in range(side // LANES + 1):
                low = parts[j - 1] if j > 0 else jnp.zeros((side, LANES), F32)
                high = parts[j] if j < side // LANES else jnp.zeros((side, LANES), F32)
                grad[c, cq + j, pl.ds(row, side), :] += jnp.where(lane >= cr, high, low)
        return carry

    lax.fori_loop(0, count, step, 0)
    copies = []

    def put(src, dst):
        copies.append(pltpu.make_async_copy(src, dst, sems.at[len(copies)]))
        copies[-1].start()

    for c in range(2):
        for b in range(nblk):
            put(grad.at[c, b + 1, HALO : HALO + tile, :], obj_hbm.at[c, :, b * LANES : (b + 1) * LANES])
        put(grad.at[c, 1 : nblk + 1, pl.ds(row_a, HALO), :], strip_a_hbm.at[c])
        put(grad.at[c, 1 : nblk + 1, pl.ds(row_b, HALO), :], strip_b_hbm.at[c])
    for c in range(2):
        for m in range(modes):
            for i in range(side // CHUNK):
                for j in range(side // LANES):
                    send[(c * modes + m) * (side // CHUNK) + i, j * CHUNK : (j + 1) * CHUNK, :] = pgrad[
                        c, m, i * CHUNK : (i + 1) * CHUNK, j * LANES : (j + 1) * LANES
                    ].astype(BF16)
    put(send, send_hbm)
    for c in range(2):
        out_a[c] = grad[c, col_a].astype(BF16)
        out_b[c] = grad[c, col_b].astype(BF16)
    put(out_a, out_a_hbm)
    put(out_b, out_b_hbm)
    for copy in copies:
        copy.wait()


def run_frames(meta, pos, mid, halo, probe, amp, lt, rt):
    side = probe.shape[-1]
    modes = probe.shape[1]
    tile = mid.shape[1]
    nblk = tile // LANES
    rows = tile + 2 * HALO
    per_peer = CHUNK * (side // LANES)
    peers = 2 * modes * side // CHUNK
    return pl.pallas_call(
        frames_kernel,
        out_shape=(
            pltpu.HBM((2, tile, tile), F32),
            pltpu.HBM((2, nblk, HALO, LANES), F32),
            pltpu.HBM((2, nblk, HALO, LANES), F32),
            pltpu.HBM((2, rows, LANES), BF16),
            pltpu.HBM((2, rows, LANES), BF16),
            pltpu.HBM((peers, per_peer, LANES), BF16),
        ),
        in_specs=[SM, SM] + [VM] * 11,
        out_specs=(pl.BlockSpec(memory_space=pltpu.HBM),) * 6,
        scratch_shapes=[
            pltpu.VMEM((2, nblk + 2, rows, LANES), F32),
            pltpu.VMEM((2, nblk + 3, rows, LANES), F32),
            pltpu.VMEM(probe.shape, F32),
            pltpu.VMEM((modes, 2 * side, side), BF16),
            pltpu.VMEM((modes * side, 2 * side), BF16),
            pltpu.VMEM((2, rows, LANES), BF16),
            pltpu.VMEM((2, rows, LANES), BF16),
            pltpu.VMEM((peers, per_peer, LANES), BF16),
            pltpu.SemaphoreType.DMA((2 * nblk + 7,)),
        ],
        compiler_params=pltpu.CompilerParams(vmem_limit_bytes=32 * 1024 * 1024),
        name="frames",
    )(meta, pos, mid, *halo, probe, amp, lt, rt)


def row_margin_kernel(meta_ref, strip_a_ref, strip_b_ref, got_a_ref, got_b_ref, out_a_ref, out_b_ref):
    nblk, rows = strip_a_ref.shape[1], got_a_ref.shape[1]
    row_odd, core = meta_ref[1], meta_ref[2]

    def emit(own_ref, out_ref, start):
        for c in range(2):
            for b in range(nblk):
                out_ref[c, b] = own_ref[c, b].astype(BF16)
            for got_ref, blk in ((got_a_ref, (1 - core) * (nblk - 1)), (got_b_ref, core * (nblk - 1))):
                out_ref[c, blk] = (own_ref[c, blk] + got_ref[c, start : start + HALO, :].astype(F32)).astype(BF16)

    @pl.when(row_odd == 0)
    def _():
        emit(strip_a_ref, out_a_ref, rows - HALO)
        emit(strip_b_ref, out_b_ref, 0)

    @pl.when(row_odd == 1)
    def _():
        emit(strip_a_ref, out_a_ref, 0)
        emit(strip_b_ref, out_b_ref, rows - HALO)


def row_margins(meta, strip_a, strip_b, got_a, got_b):
    shape = jax.ShapeDtypeStruct(strip_a.shape, BF16)
    return pl.pallas_call(
        row_margin_kernel,
        out_shape=(shape, shape),
        in_specs=[SM] + [VM] * 4,
        out_specs=(VM, VM),
        compiler_params=pltpu.CompilerParams(vmem_limit_bytes=16 * 1024 * 1024),
        cost_estimate=pl.CostEstimate(flops=5000000000, transcendentals=0, bytes_accessed=0),
        name="row_margins",
    )(meta, strip_a, strip_b, got_a, got_b)


def add_cols_kernel(meta_ref, part_ref, col_a_ref, col_b_ref, obj_ref):
    tile = part_ref.shape[1]
    inner = slice(HALO, HALO + tile)
    at_b = pl.program_id(0) == meta_ref[2]

    @pl.when(at_b)
    def _():
        obj_ref[...] = part_ref[...] + col_b_ref[:, inner, :].astype(F32)

    @pl.when(jnp.logical_not(at_b))
    def _():
        obj_ref[...] = part_ref[...] + col_a_ref[:, inner, :].astype(F32)


def add_cols(meta, part, col_a, col_b):
    tile, cols = part.shape[1:]
    edge = pl.BlockSpec((2, tile, LANES), lambda i: (0, 0, i * (cols // LANES - 1)))
    return pl.pallas_call(
        add_cols_kernel,
        grid=(2,),
        out_shape=jax.ShapeDtypeStruct(part.shape, F32),
        in_specs=[SM, edge, VM, VM],
        out_specs=edge,
        input_output_aliases={1: 0},
        cost_estimate=pl.CostEstimate(flops=5000000000, transcendentals=0, bytes_accessed=0),
        compiler_params=pltpu.CompilerParams(vmem_limit_bytes=16 * 1024 * 1024),
        name="add_cols",
    )(meta, part, col_a, col_b)


def add_rows_kernel(meta_ref, part_ref, row_a_ref, row_b_ref, obj_ref):
    nblk = row_a_ref.shape[1]
    at_b = pl.program_id(0) == meta_ref[1]

    def add(row_ref):
        for c in range(2):
            for b in range(nblk):
                cols = slice(b * LANES, (b + 1) * LANES)
                obj_ref[c, :, cols] = part_ref[c, :, cols] + row_ref[c, b].astype(F32)

    @pl.when(at_b)
    def _():
        add(row_b_ref)

    @pl.when(jnp.logical_not(at_b))
    def _():
        add(row_a_ref)


def add_rows(meta, part, row_a, row_b):
    tile, cols = part.shape[1:]
    edge = pl.BlockSpec((2, HALO, cols), lambda i: (0, i * (tile // HALO - 1), 0))
    return pl.pallas_call(
        add_rows_kernel,
        grid=(2,),
        out_shape=jax.ShapeDtypeStruct(part.shape, F32),
        in_specs=[SM, edge, VM, VM],
        out_specs=edge,
        input_output_aliases={1: 0},
        cost_estimate=pl.CostEstimate(flops=5000000000, transcendentals=0, bytes_accessed=0),
        compiler_params=pltpu.CompilerParams(vmem_limit_bytes=16 * 1024 * 1024),
        name="add_rows",
    )(meta, part, row_a, row_b)


def probe_kernel(got_ref, out_ref):
    modes, side = out_ref.shape[1], out_ref.shape[2]
    for c in range(2):
        for m in range(modes):
            for i in range(side // CHUNK):
                for j in range(side // LANES):
                    out_ref[c, m, i * CHUNK : (i + 1) * CHUNK, j * LANES : (j + 1) * LANES] = got_ref[
                        (c * modes + m) * (side // CHUNK) + i, j * CHUNK : (j + 1) * CHUNK, :
                    ].astype(F32)


def finish_probe(got, shape):
    return pl.pallas_call(
        probe_kernel,
        out_shape=jax.ShapeDtypeStruct(shape, F32),
        in_specs=[VM],
        out_specs=VM,
        compiler_params=pltpu.CompilerParams(vmem_limit_bytes=16 * 1024 * 1024),
        name="finish_probe",
    )(got)


def trade(value, axis, phase):
    n = lax.axis_size(axis)
    pairs = [(i, ((i + phase) ^ 1) - phase) for i in range(n)]
    return lax.ppermute(value, axis, [(i, j) for i, j in pairs if 0 <= j < n])


def shards(object_field, probe_modes, measured_amp, scan_positions, frame_counts):
    tile = object_field.shape[1]
    slots = measured_amp.shape[2]
    row_odd = lax.axis_index("row") % 2
    core = lax.axis_index("core")
    meta = jnp.stack([frame_counts[0, 0], row_odd, core]).astype(jnp.int32)
    even = row_odd == 0
    first = core == 0
    bottom = object_field[:, tile - HALO :, :]
    top = object_field[:, :HALO, :]
    row_a = trade(jnp.where(even, bottom, top), "row", 0)
    row_b = trade(jnp.where(even, top, bottom), "row", 1)
    right = object_field[:, :, tile - HALO :]
    left = object_field[:, :, :HALO]
    col_a = trade(jnp.where(first, right, left), COL, 0)
    col_b = trade(jnp.where(first, left, right), COL, 1)
    rights = jnp.concatenate([row_a[:, :, tile - HALO :], row_b[:, :, tile - HALO :]], axis=0)
    lefts = jnp.concatenate([row_a[:, :, :HALO], row_b[:, :, :HALO]], axis=0)
    cor_a = trade(jnp.where(first, rights, lefts), COL, 0)
    cor_b = trade(jnp.where(first, lefts, rights), COL, 1)
    lt, rt = fourier_tables(probe_modes.shape[-1])
    part, strip_a, strip_b, out_a, out_b, send = run_frames(
        meta, scan_positions[0, 0], object_field, (row_a, row_b, col_a, col_b, cor_a, cor_b),
        probe_modes, measured_amp[0, 0], lt, rt,
    )
    scale = 1.0 / math.sqrt(lax.axis_size("row") * lax.axis_size(COL) * slots)
    got_a = trade(out_a, COL, 0)
    got_b = trade(out_b, COL, 1)
    peers = lax.all_to_all(send, PEERS, 0, 0, tiled=True)
    rows_a, rows_b = row_margins(meta, strip_a, strip_b, got_a, got_b)
    peers, rows_a, rows_b = lax.optimization_barrier((peers, rows_a, rows_b))
    back_a = trade(rows_a, "row", 0)
    back_b = trade(rows_b, "row", 1)
    half = jnp.sum(peers.astype(F32), axis=0)
    total = ((half + trade(half, COL, 0)) * scale).astype(BF16)
    whole = lax.all_to_all(jnp.broadcast_to(total[None], send.shape), PEERS, 0, 0, tiled=True)
    part = add_cols(meta, part, got_a, got_b)
    obj = add_rows(meta, part, back_a, back_b)
    whole, obj = lax.optimization_barrier((whole, obj))
    return obj, finish_probe(whole, probe_modes.shape)


def solution(mesh):
    n_col = mesh.shape["col"]
    fine = Mesh(mesh.devices.reshape(mesh.shape["row"], n_col // 2, 2), ("row",) + COL)
    in_specs = (
        P(None, "row", COL),
        P(),
        P("row", COL, None, None, None),
        P("row", COL, None, None),
        P("row", COL),
    )
    out_specs = (P(None, "row", COL), P())
    return jax.shard_map(shards, mesh=fine, in_specs=in_specs, out_specs=out_specs, check_vma=False)
```

time: 109 us -> 99.3 us (0.911)
  the two profiles are of different devices: /device:TPU:4 before, /device:TPU:0 now
where the time goes in v2:
time: 99.3 us; the launch traced here: 97.4 us
  starting transfers between devices  49.9 us (50%)
  waiting for transfers between devices  20.8 us (21%)
  Pallas kernels  16 us (16%)
  local copies, waits for them, and re-layouts  5.95 us (6%)
  other arithmetic  3.3 us (3%)
  between operations  1.48 us (1%)
    all_to_all x1, starting transfers between devices, shards(): peers = lax.all_to_all(send, PEERS, 0, 0, tiled=True)  23.7 us
    ppermute x11, starting transfers between devices, trade(): return lax.ppermute(value, axis, [(i, j) for i, j in pairs if 0 <= j < n])  17 us
    all_to_all x1, waiting for transfers between devices, shards(): peers = lax.all_to_all(send, PEERS, 0, 0, tiled=True)  10.1 us
    pallas_call x1, Pallas kernels, run_frames(): pl.pallas_call(frames_kernel, out_shape=(pltpu.HBM((2, tile, tile), F32),...  10.1 us
    all_to_all x1, starting transfers between devices, shards(): lax.all_to_all(jnp.broadcast_to(total[None], send.shape), PEERS, 0, 0, ti...  9.24 us
    all_to_all x1, waiting for transfers between devices, shards(): lax.all_to_all(jnp.broadcast_to(total[None], send.shape), PEERS, 0, 0, ti...  8.7 us
    unnamed x16, local copies, waits for them, and re-layouts  4.18 us
    pallas_call x1, Pallas kernels, add_rows(): pl.pallas_call(add_rows_kernel, grid=(2,), out_shape=jax.ShapeDtypeStruct...  2.1 us
  transfers between devices with their start and end apart: 13, of which 5 were waited for; matrix products, arithmetic and copies ran while one was open for 3% of the time, Pallas kernels for 5%

profile of v2, /device:TPU:0, one launch (start us, length us, event | category | flops | bytes accessed | tf_op | source)
XLA Modules:
  0.0 97.4 jit_solution(17556529029223296095)
XLA Ops:
  0.7 2.0 %broadcast_select_fusion.2 = (bf16[2,128,512]{2,1,0:T(8,128)(2,1)}, bf16[2,128,512]{2,1,0:T(8,128)(2,1)}) fusion(pred[]{:T(512)S(6)} %eq.8, bf16[2,512,512]{2,1,0:T(8,128)(2,1)} %mid_ref.1), kind=kLoop, calls=%fused_computation.3 | loop fusion | flops 262144 | bytes 1048577 | tf_op jit(solution)/shard_map/jit(_where)/select_n | solution.py:325
  3.4 5.2 %collective-permute-start = (bf16[2,128,512]{2,1,0:T(8,128)(2,1)}, bf16[2,128,512]{2,1,0:T(8,128)(2,1)}, u32[]{:S(2)}, u32[]{:S(2)}) collective-permute-start(bf16[2,128,512]{2,1,0:T(8,128)(2,1)} %get-tuple-element.31), channel_id=1, source_target_pairs={{0,16},{16,0},{32,48},{48,32},{64,80},{80,64},{96,112},{112,96},{1... | collective-permute-start | bytes 786440 | tf_op jit(solution)/shard_map/ppermute | solution.py:311
  8.6 1.1 %broadcast_select_fusion = (bf16[2,512,128]{2,1,0:T(8,128)(2,1)S(1)}, bf16[2,512,128]{2,1,0:T(8,128)(2,1)S(1)}) fusion(pred[]{:T(512)S(6)} %eq.9, bf16[2,512,512]{2,1,0:T(8,128)(2,1)} %mid_ref.1), kind=kLoop, calls=%fused_computation.1 | loop fusion | flops 262144 | bytes 1048577 | tf_op jit(solution)/shard_map/jit(_where)/select_n | solution.py:329
  9.7 0.7 collective-permute-start.3
  10.4 2.9 %collective-permute-start.2 = (bf16[2,512,128]{2,1,0:T(8,128)(2,1)S(1)}, bf16[2,512,128]{2,1,0:T(8,128)(2,1)S(1)}, u32[]{:S(2)}, u32[]{:S(2)}) collective-permute-start(bf16[2,512,128]{2,1,0:T(8,128)(2,1)S(1)} %get-tuple-element.29), channel_id=1, source_target_pairs={{0,1},{1,0},{2,3},{3,2},{4,5},{5,4},{6,7},{7,6},{8,9},{9,8},{10,11... | collective-permute-start | bytes 786440 | tf_op jit(solution)/shard_map/ppermute | solution.py:311
  13.3 1.6 %collective-permute-done.row_a_ref = bf16[2,128,512]{2,1,0:T(8,128)(2,1)} collective-permute-done((bf16[2,128,512]{2,1,0:T(8,128)(2,1)}, bf16[2,128,512]{2,1,0:T(8,128)(2,1)}, u32[]{:S(2)}, u32[]{:S(2)}) %collective-permute-start) | collective-permute-done | bytes 262176 | tf_op jit(solution)/shard_map/ppermute | solution.py:311
  14.9 0.9 fusion
  15.9 0.7 collective-permute-start.5
  16.5 2.9 %collective-permute-start.4 = (bf16[4,128,128]{2,1,0:T(8,128)(2,1)S(1)}, bf16[4,128,128]{2,1,0:T(8,128)(2,1)S(1)}, u32[]{:S(2)}, u32[]{:S(2)}) collective-permute-start(bf16[4,128,128]{2,1,0:T(8,128)(2,1)S(1)} %get-tuple-element.33), channel_id=1, source_target_pairs={{0,1},{1,0},{2,3},{3,2},{4,5},{5,4},{6,7},{7,6},{8,9},{9,8},{10,11... | collective-permute-start | bytes 393224 | tf_op jit(solution)/shard_map/ppermute | solution.py:311
  20.5 1.0 %copy-done.3 = bf16[512,512]{1,0:T(8,128)(2,1)S(1)} copy-done((bf16[512,512]{1,0:T(8,128)(2,1)S(1)}, bf16[512,512]{1,0:T(8,128)(2,1)}, u32[]{:S(2)}) %copy-start.3) | copy-done | bytes 524312
  21.5 1.0 %copy-done.4 = bf16[512,512]{1,0:T(8,128)(2,1)S(1)} copy-done((bf16[512,512]{1,0:T(8,128)(2,1)S(1)}, bf16[512,512]{1,0:T(8,128)(2,1)}, u32[]{:S(2)}) %copy-start.4) | copy-done | bytes 524312
  22.6 10.1 %frames.1 = (f32[2,512,512]{2,1,0:T(8,128)}, f32[2,4,128,128]{3,2,1,0:T(8,128)}, f32[2,4,128,128]{3,2,1,0:T(8,128)}, bf16[2,768,128]{2,1,0:T(8,128)(2,1)}, bf16[...) custom-call(s32[3]{0:T(128)S(1)} %pad_add_fusion.meta_ref, s32[2,8]{1,0:T(2,128)S(1)} %bitcast.7, ...), custom_call_target="tpu_custom_call" | custom-call | tf_op jit(solution)/shard_map/frames/pallas_call | solution.py:158
  32.7 2.1 %collective-permute-start.6 = (bf16[2,768,128]{2,1,0:T(8,128)(2,1)}, bf16[2,768,128]{2,1,0:T(8,128)(2,1)S(1)}, u32[]{:S(2)}, u32[]{:S(2)}) collective-permute-start(bf16[2,768,128]{2,1,0:T(8,128)(2,1)} %get-tuple-element.18), channel_id=1, source_target_pairs={{0,1},{1,0},{2,3},{3,2},{4,5},{5,4},{6,7},{7,6},{8,9},{9,8},{10,11... | collective-permute-start | bytes 1179656 | tf_op jit(solution)/shard_map/ppermute | solution.py:311
  34.8 0.7 collective-permute-start.7
  35.5 23.7 %all-to-all-start = ((bf16[64,32,128]{2,1,0:T(8,128)(2,1)}), bf16[64,32,128]{2,1,0:T(8,128)(2,1)S(1)}, u32[]{:S(2)}, u32[]{:S(2)}) async-start(bf16[64,32,128]{2,1,0:T(8,128)(2,1)} %get-tuple-element.15), calls=%async_computation | async-start | bytes 1048576 | tf_op jit(solution)/shard_map/all_to_all | solution.py:342
  59.2 1.0 %copy-done.6 = f32[2,4,128,128]{3,2,1,0:T(8,128)S(1)} copy-done((f32[2,4,128,128]{3,2,1,0:T(8,128)S(1)}, f32[2,4,128,128]{3,2,1,0:T(8,128)}, u32[]{:S(2)}) %copy-start.6) | copy-done | bytes 524312
  60.2 1.0 %copy-done.7 = f32[2,4,128,128]{3,2,1,0:T(8,128)S(1)} copy-done((f32[2,4,128,128]{3,2,1,0:T(8,128)S(1)}, f32[2,4,128,128]{3,2,1,0:T(8,128)}, u32[]{:S(2)}) %copy-start.7) | copy-done | bytes 524312
  61.9 10.1 %all-to-all-done = bf16[64,32,128]{2,1,0:T(8,128)(2,1)S(1)} async-done(((bf16[64,32,128]{2,1,0:T(8,128)(2,1)}), bf16[64,32,128]{2,1,0:T(8,128)(2,1)S(1)}, u32[]{:S(2)}, u32[]{:S(2)}) %all-to-all-start) | async-done | bytes 524320 | tf_op jit(solution)/shard_map/all_to_all | solution.py:342
  73.4 0.9 broadcast_in_dim.2
  74.2 9.2 %all-to-all-start.1 = ((bf16[64,32,128]{2,1,0:T(8,128)(2,1)}), bf16[64,32,128]{2,1,0:T(8,128)(2,1)S(1)}, u32[]{:S(2)}, u32[]{:S(2)}) async-start(bf16[64,32,128]{2,1,0:T(8,128)(2,1)} %broadcast_in_dim.2), calls=%async_computation.1 | async-start | bytes 1048576 | tf_op jit(solution)/shard_map/all_to_all | solution.py:349
  83.5 2.1 %add_cols.1.part_ref = f32[2,512,512]{2,1,0:T(8,128)} custom-call(s32[3]{0:T(128)S(1)} %pad_add_fusion.meta_ref, f32[2,512,512]{2,1,0:T(8,128)} %get-tuple-element.23.part_ref, bf16[2,768,128]{2,1,0:T(8,128)(2,1)S(1)} %collective-permute-done.6.got_a_ref.col_a_ref, ...), custom_call_target="tpu_custom_call", output_to_operand_aliasing={{}: (1, {})} | custom-call | flops 5000000000 | tf_op jit(solution)/shard_map/add_cols/pallas_call | solution.py:238
  85.6 2.1 %add_rows.1 = f32[2,512,512]{2,1,0:T(8,128)} custom-call(s32[3]{0:T(128)S(1)} %pad_add_fusion.meta_ref, f32[2,512,512]{2,1,0:T(8,128)} %add_cols.1.part_ref, bf16[2,4,128,128]{3,2,1,0:T(8,128)(2,1)S(1)} %collective-permute-done.9.row_a_ref, bf16[2,4,128,128]{3,2,1,0:T(8,128)(2,1)S(1)} %collective-permute-done.10.row_b_ref), custom_call_target="tpu_custom_call", output_to_operand_aliasing={{}: (1, {})} | custom-call | flops 5000000000 | tf_op jit(solution)/shard_map/add_rows/pallas_call | solution.py:273
  87.7 8.7 %all-to-all-done.1.got_ref = bf16[64,32,128]{2,1,0:T(8,128)(2,1)S(1)} async-done(((bf16[64,32,128]{2,1,0:T(8,128)(2,1)}), bf16[64,32,128]{2,1,0:T(8,128)(2,1)S(1)}, u32[]{:S(2)}, u32[]{:S(2)}) %all-to-all-start.1) | async-done | bytes 524320 | tf_op jit(solution)/shard_map/all_to_all | solution.py:349
  96.4 1.0 %finish_probe.1 = f32[2,2,256,256]{3,2,1,0:T(8,128)} custom-call(bf16[64,32,128]{2,1,0:T(8,128)(2,1)S(1)} %all-to-all-done.1.got_ref), custom_call_target="tpu_custom_call" | custom-call | tf_op jit(solution)/shard_map/finish_probe/pallas_call | solution.py:298
  (32 shorter events, 3.1 us)
Async XLA Ops:
  0.6 19.8 %copy-start = (bf16[2,512,512]{2,1,0:T(8,128)(2,1)S(1)}, bf16[2,512,512]{2,1,0:T(8,128)(2,1)}, u32[]{:S(2)}) copy-start(bf16[2,512,512]{2,1,0:T(8,128)(2,1)} %mid_ref.1) | copy-start | bytes 3145732
  0.6 19.8 %copy-start.5 = (s32[1,1,2,8]{3,2,1,0:T(2,128)S(1)}, s32[1,1,2,8]{3,2,1,0:T(2,128)}, u32[]{:S(2)}) copy-start(s32[1,1,2,8]{3,2,1,0:T(2,128)} %param.10) | copy-start | bytes 196
  0.7 19.8 %copy-start.2 = (bf16[1,1,8,256,256]{4,3,2,1,0:T(8,128)(2,1)S(1)}, bf16[1,1,8,256,256]{4,3,2,1,0:T(8,128)(2,1)}, u32[]{:S(2)}) copy-start(bf16[1,1,8,256,256]{4,3,2,1,0:T(8,128)(2,1)} %param.9) | copy-start | bytes 3145732
  0.7 19.8 %copy-start.1 = (f32[2,2,256,256]{3,2,1,0:T(8,128)S(1)}, f32[2,2,256,256]{3,2,1,0:T(8,128)}, u32[]{:S(2)}) copy-start(f32[2,2,256,256]{3,2,1,0:T(8,128)} %probe_ref.1) | copy-start | bytes 3145732
  2.7 10.6 %collective-permute-start.1 = (bf16[2,128,512]{2,1,0:T(8,128)(2,1)}, bf16[2,128,512]{2,1,0:T(8,128)(2,1)S(1)}, u32[]{:S(2)}, u32[]{:S(2)}) collective-permute-start(bf16[2,128,512]{2,1,0:T(8,128)(2,1)} %get-tuple-element.30), channel_id=1, source_target_pairs={{16,32},{32,16},{48,64},{64,48},{80,96},{96,80},{17,33},{33,17},{4... | collective-permute-start | bytes 786440 | tf_op jit(solution)/shard_map/ppermute | solution.py:311
  3.4 11.6 %collective-permute-start = (bf16[2,128,512]{2,1,0:T(8,128)(2,1)}, bf16[2,128,512]{2,1,0:T(8,128)(2,1)}, u32[]{:S(2)}, u32[]{:S(2)}) collective-permute-start(bf16[2,128,512]{2,1,0:T(8,128)(2,1)} %get-tuple-element.31), channel_id=1, source_target_pairs={{0,16},{16,0},{32,48},{48,32},{64,80},{80,64},{96,112},{112,96},{1... | collective-permute-start | bytes 786440 | tf_op jit(solution)/shard_map/ppermute | solution.py:311
  9.7 10.5 %collective-permute-start.3 = (bf16[2,512,128]{2,1,0:T(8,128)(2,1)S(1)}, bf16[2,512,128]{2,1,0:T(8,128)(2,1)S(1)}, u32[]{:S(2)}, u32[]{:S(2)}) collective-permute-start(bf16[2,512,128]{2,1,0:T(8,128)(2,1)S(1)} %get-tuple-element.28), channel_id=1, source_target_pairs={{1,2},{2,1},{3,4},{4,3},{5,6},{6,5},{7,8},{8,7},{9,10},{10,9},{11,... | collective-permute-start | bytes 786440 | tf_op jit(solution)/shard_map/ppermute | solution.py:311
  10.4 9.8 %collective-permute-start.2 = (bf16[2,512,128]{2,1,0:T(8,128)(2,1)S(1)}, bf16[2,512,128]{2,1,0:T(8,128)(2,1)S(1)}, u32[]{:S(2)}, u32[]{:S(2)}) collective-permute-start(bf16[2,512,128]{2,1,0:T(8,128)(2,1)S(1)} %get-tuple-element.29), channel_id=1, source_target_pairs={{0,1},{1,0},{2,3},{3,2},{4,5},{5,4},{6,7},{7,6},{8,9},{9,8},{10,11... | collective-permute-start | bytes 786440 | tf_op jit(solution)/shard_map/ppermute | solution.py:311
  15.9 4.3 %collective-permute-start.5 = (bf16[4,128,128]{2,1,0:T(8,128)(2,1)S(1)}, bf16[4,128,128]{2,1,0:T(8,128)(2,1)S(1)}, u32[]{:S(2)}, u32[]{:S(2)}) collective-permute-start(bf16[4,128,128]{2,1,0:T(8,128)(2,1)S(1)} %get-tuple-element.32), channel_id=1, source_target_pairs={{1,2},{2,1},{3,4},{4,3},{5,6},{6,5},{7,8},{8,7},{9,10},{10,9},{11,... | collective-permute-start | bytes 393224 | tf_op jit(solution)/shard_map/ppermute | solution.py:311
  16.5 3.9 %collective-permute-start.4 = (bf16[4,128,128]{2,1,0:T(8,128)(2,1)S(1)}, bf16[4,128,128]{2,1,0:T(8,128)(2,1)S(1)}, u32[]{:S(2)}, u32[]{:S(2)}) collective-permute-start(bf16[4,128,128]{2,1,0:T(8,128)(2,1)S(1)} %get-tuple-element.33), channel_id=1, source_target_pairs={{0,1},{1,0},{2,3},{3,2},{4,5},{5,4},{6,7},{7,6},{8,9},{9,8},{10,11... | collective-permute-start | bytes 393224 | tf_op jit(solution)/shard_map/ppermute | solution.py:311
  20.5 1.0 %copy-start.3 = (bf16[512,512]{1,0:T(8,128)(2,1)S(1)}, bf16[512,512]{1,0:T(8,128)(2,1)}, u32[]{:S(2)}) copy-start(bf16[512,512]{1,0:T(8,128)(2,1)} %constant.45.rt_ref) | copy-start | bytes 1572868
  21.5 1.0 %copy-start.4 = (bf16[512,512]{1,0:T(8,128)(2,1)S(1)}, bf16[512,512]{1,0:T(8,128)(2,1)}, u32[]{:S(2)}) copy-start(bf16[512,512]{1,0:T(8,128)(2,1)} %constant.42.lt_ref) | copy-start | bytes 1572868
  32.7 26.5 %collective-permute-start.6 = (bf16[2,768,128]{2,1,0:T(8,128)(2,1)}, bf16[2,768,128]{2,1,0:T(8,128)(2,1)S(1)}, u32[]{:S(2)}, u32[]{:S(2)}) collective-permute-start(bf16[2,768,128]{2,1,0:T(8,128)(2,1)} %get-tuple-element.18), channel_id=1, source_target_pairs={{0,1},{1,0},{2,3},{3,2},{4,5},{5,4},{6,7},{7,6},{8,9},{9,8},{10,11... | collective-permute-start | bytes 1179656 | tf_op jit(solution)/shard_map/ppermute | solution.py:311
  34.8 24.4 %collective-permute-start.7 = (bf16[2,768,128]{2,1,0:T(8,128)(2,1)}, bf16[2,768,128]{2,1,0:T(8,128)(2,1)S(1)}, u32[]{:S(2)}, u32[]{:S(2)}) collective-permute-start(bf16[2,768,128]{2,1,0:T(8,128)(2,1)} %get-tuple-element.19), channel_id=1, source_target_pairs={{1,2},{2,1},{3,4},{4,3},{5,6},{6,5},{7,8},{8,7},{9,10},{10,9},{11,... | collective-permute-start | bytes 1179656 | tf_op jit(solution)/shard_map/ppermute | solution.py:311
  35.5 36.6 %all-to-all-start = ((bf16[64,32,128]{2,1,0:T(8,128)(2,1)}), bf16[64,32,128]{2,1,0:T(8,128)(2,1)S(1)}, u32[]{:S(2)}, u32[]{:S(2)}) async-start(bf16[64,32,128]{2,1,0:T(8,128)(2,1)} %get-tuple-element.15), calls=%async_computation | async-start | bytes 1048576 | tf_op jit(solution)/shard_map/all_to_all | solution.py:342
  59.2 1.0 %copy-start.6 = (f32[2,4,128,128]{3,2,1,0:T(8,128)S(1)}, f32[2,4,128,128]{3,2,1,0:T(8,128)}, u32[]{:S(2)}) copy-start(f32[2,4,128,128]{3,2,1,0:T(8,128)} %get-tuple-element.16.strip_a_ref) | copy-start | bytes 1572868
  60.2 1.0 %copy-start.7 = (f32[2,4,128,128]{3,2,1,0:T(8,128)S(1)}, f32[2,4,128,128]{3,2,1,0:T(8,128)}, u32[]{:S(2)}) copy-start(f32[2,4,128,128]{3,2,1,0:T(8,128)} %get-tuple-element.17.strip_b_ref) | copy-start | bytes 1572868
  72.1 1.3 %collective-permute-start.8 = (f32[32,128]{1,0:T(8,128)S(1)}, f32[32,128]{1,0:T(8,128)S(1)}, u32[]{:S(2)}, u32[]{:S(2)}) collective-permute-start(f32[32,128]{1,0:T(8,128)S(1)} %convert_reduce_fusion), channel_id=1, source_target_pairs={{0,1},{1,0},{2,3},{3,2},{4,5},{5,4},{6,7},{7,6},{8,9},{9,8},{10,11... | collective-permute-start | bytes 49160 | tf_op jit(solution)/shard_map/ppermute | solution.py:311
  72.2 13.4 %collective-permute-start.9 = (bf16[2,4,128,128]{3,2,1,0:T(8,128)(2,1)S(1)}, bf16[2,4,128,128]{3,2,1,0:T(8,128)(2,1)S(1)}, u32[]{:S(2)}, u32[]{:S(2)}) collective-permute-start(bf16[2,4,128,128]{3,2,1,0:T(8,128)(2,1)S(1)} %get-tuple-element.24), channel_id=1, source_target_pairs={{0,16},{16,0},{32,48},{48,32},{64,80},{80,64},{96,112},{112,96},{1... | collective-permute-start | bytes 786440 | tf_op jit(solution)/shard_map/ppermute | solution.py:311
  72.6 13.0 %collective-permute-start.10 = (bf16[2,4,128,128]{3,2,1,0:T(8,128)(2,1)S(1)}, bf16[2,4,128,128]{3,2,1,0:T(8,128)(2,1)S(1)}, u32[]{:S(2)}, u32[]{:S(2)}) collective-permute-start(bf16[2,4,128,128]{3,2,1,0:T(8,128)(2,1)S(1)} %get-tuple-element.25), channel_id=1, source_target_pairs={{16,32},{32,16},{48,64},{64,48},{80,96},{96,80},{17,33},{33,17},{4... | collective-permute-start | bytes 786440 | tf_op jit(solution)/shard_map/ppermute | solution.py:311
  74.2 22.1 %all-to-all-start.1 = ((bf16[64,32,128]{2,1,0:T(8,128)(2,1)}), bf16[64,32,128]{2,1,0:T(8,128)(2,1)S(1)}, u32[]{:S(2)}, u32[]{:S(2)}) async-start(bf16[64,32,128]{2,1,0:T(8,128)(2,1)} %broadcast_in_dim.2), calls=%async_computation.1 | async-start | bytes 1048576 | tf_op jit(solution)/shard_map/all_to_all | solution.py:349

commit v3 on v2

v3 whole, which is shorter than its diff:
```python
import math

import jax
import jax.numpy as jnp
import numpy as np
from jax import lax
from jax.experimental import pallas as pl
from jax.experimental.pallas import tpu as pltpu
from jax.sharding import Mesh
from jax.sharding import PartitionSpec as P

HALO = 128
LANES = 128
CHUNK = 16
BF16 = jnp.bfloat16
F32 = jnp.float32
COL = ("colc", "core")
PEERS = ("row", "colc")
VM = pl.BlockSpec(memory_space=pltpu.VMEM)
SM = pl.BlockSpec(memory_space=pltpu.SMEM)


def fourier_tables(side):
    indices = np.arange(side)
    angles = 2.0 * math.pi / side * (indices[:, None] * indices[None, :] % side)
    real = jnp.asarray((np.cos(angles) / math.sqrt(side)).astype(np.float32)).astype(BF16)
    imag = jnp.asarray((-np.sin(angles) / math.sqrt(side)).astype(np.float32)).astype(BF16)
    return jnp.stack([jnp.block([[real, -imag], [imag, real]]), jnp.block([[real, imag], [-imag, real]])])


def place():
    return lax.axis_index("row") % 2, lax.axis_index("core")


def matmul(a, b):
    return jnp.dot(a, b, preferred_element_type=F32)


def margins_kernel(obj, edge_a, edge_b, row_a, row_b, col_a, col_b, sems):
    tile = obj.shape[1]
    row_odd, core = place()
    copies = []

    def put(src, dst):
        copies.append(pltpu.make_async_copy(src, dst, sems.at[len(copies)]))
        copies[-1].start()

    for edge, row, at in ((edge_b, row_b, row_odd), (edge_a, row_a, 1 - row_odd)):
        rows = pl.ds(pl.multiple_of(at * (tile - HALO), HALO), HALO)
        put(obj.at[:, rows, 0:HALO], edge.at[0:2])
        put(obj.at[:, rows, tile - HALO :], edge.at[2:4])
        put(obj.at[:, rows, HALO : tile - HALO], row)
    for col, at in ((col_b, core), (col_a, 1 - core)):
        put(obj.at[:, :, pl.ds(pl.multiple_of(at * (tile - HALO), HALO), HALO)], col)
    for copy in copies:
        copy.wait()


def margins(obj):
    tile = obj.shape[1]
    edge = jax.ShapeDtypeStruct((4, HALO, HALO), BF16)
    row = jax.ShapeDtypeStruct((2, HALO, tile - 2 * HALO), BF16)
    col = jax.ShapeDtypeStruct((2, tile, HALO), BF16)
    return pl.pallas_call(
        margins_kernel,
        out_shape=(edge, edge, row, row, col, col),
        in_specs=[pl.BlockSpec(memory_space=pltpu.HBM)],
        out_specs=(VM,) * 6,
        scratch_shapes=[pltpu.SemaphoreType.DMA((8,))],
        compiler_params=pltpu.CompilerParams(vmem_limit_bytes=8 * 1024 * 1024),
        name="margins",
    )(pltpu.with_memory_space_constraint(obj, pltpu.HBM))


def corners_kernel(edge_a, edge_b, cor_a, cor_b):
    core = lax.axis_index("core")
    for cor, at in ((cor_b, core), (cor_a, 1 - core)):
        cor[0:2] = edge_a[pl.ds(2 * at, 2)]
        cor[2:4] = edge_b[pl.ds(2 * at, 2)]


def corners(edge_a, edge_b):
    shape = jax.ShapeDtypeStruct(edge_a.shape, BF16)
    return pl.pallas_call(
        corners_kernel,
        out_shape=(shape, shape),
        in_specs=[VM, VM],
        out_specs=(VM, VM),
        compiler_params=pltpu.CompilerParams(vmem_limit_bytes=8 * 1024 * 1024),
        name="corners",
    )(edge_a, edge_b)


def frames_kernel(
    count_ref, pos_ref, edge_a_ref, edge_b_ref, row_a_ref, row_b_ref, col_a_ref, col_b_ref, cor_a_ref, cor_b_ref,
    ext_ref, grad_ref, pgrad_ref, probe_ref, amp_ref, tables_ref,
    ext, grad, pgrad, obj_hbm, strip_a_hbm, strip_b_hbm, out_a_hbm, out_b_hbm, keep_hbm, send_hbm,
    patch, waves, chi, firsts, backs, out_a, out_b, keep_out, send, sems,
):
    side = probe_ref.shape[-1]
    modes = probe_ref.shape[1]
    tile = col_a_ref.shape[1]
    nblk = tile // LANES
    count = count_ref[0, 0]
    row_odd, core = place()
    row_a = pl.multiple_of((1 - row_odd) * (HALO + tile), HALO)
    row_b = pl.multiple_of(row_odd * (HALO + tile), HALO)
    col_a = (1 - core) * (nblk + 1)
    col_b = core * (nblk + 1)
    lt_ref, rt_ref = tables_ref.at[0], tables_ref.at[1]
    for c in range(2):
        for b in range(nblk):
            outer = b in (0, nblk - 1)
            for at, edge_ref, row_ref in ((row_a, edge_a_ref, row_a_ref), (row_b, edge_b_ref, row_b_ref)):
                if outer:
                    ext[c, b + 1, pl.ds(at, HALO), :] = edge_ref[c + 2 * min(b, 1)].astype(F32)
                else:
                    ext[c, b + 1, pl.ds(at, HALO), :] = row_ref[c, :, (b - 1) * LANES : b * LANES].astype(F32)
        for col, own_ref, cor_ref in ((col_a, col_a_ref, cor_a_ref), (col_b, col_b_ref, cor_b_ref)):
            ext[c, col, pl.ds(row_a, HALO), :] = cor_ref[c].astype(F32)
            ext[c, col, HALO : HALO + tile, :] = own_ref[c].astype(F32)
            ext[c, col, pl.ds(row_b, HALO), :] = cor_ref[2 + c].astype(F32)
    lane = lax.broadcasted_iota(jnp.int32, (side, LANES), 1)

    def gather(s, slot):
        row = pos_ref[0, 0, 0, s]
        col = pos_ref[0, 0, 1, s]
        cq = col // LANES
        cr = col % LANES
        back_shift = (LANES - cr) % LANES
        keep = lane < LANES - cr
        for c in range(2):
            rolled = [
                pltpu.roll(ext[c, jnp.minimum(cq + j, nblk + 1), pl.ds(row, side), :], back_shift, 1)
                for j in range(side // LANES + 1)
            ]
            for j in range(side // LANES):
                patch[slot, c, :, j * LANES : (j + 1) * LANES] = jnp.where(keep, rolled[j], rolled[j + 1])

    def exits(slot):
        patch_r = patch[slot, 0]
        patch_i = patch[slot, 1]
        for m in range(modes):
            pr = probe_ref[0, m]
            pi = probe_ref[1, m]
            waves[m, 0:side, :] = (pr * patch_r - pi * patch_i).astype(BF16)
            waves[m, side:, :] = (pr * patch_i + pi * patch_r).astype(BF16)

    def left(table, src, dst):
        for m in range(modes):
            f = matmul(table, src[m]).astype(BF16)
            dst[m * side : (m + 1) * side, 0:side] = f[:side]
            dst[m * side : (m + 1) * side, side:] = f[side:]

    def make_chi(s):
        psi = matmul(firsts[...], rt_ref[...])
        psi_r = [psi[m * side : (m + 1) * side, :side] for m in range(modes)]
        psi_i = [psi[m * side : (m + 1) * side, side:] for m in range(modes)]
        power = sum(psi_r[m] * psi_r[m] + psi_i[m] * psi_i[m] for m in range(modes))
        factor = 1.0 - amp_ref[s].astype(F32) * lax.rsqrt(jnp.maximum(power, 0.25))
        for m in range(modes):
            chi[m, 0:side, :] = (psi_r[m] * factor).astype(BF16)
            chi[m, side:, :] = (psi_i[m] * factor).astype(BF16)

    def finish(s, slot, back):
        row = pos_ref[0, 0, 0, s]
        col = pos_ref[0, 0, 1, s]
        cq = col // LANES
        cr = col % LANES
        patch_r = patch[slot, 0]
        patch_i = patch[slot, 1]
        sum_r = jnp.zeros((side, side), F32)
        sum_i = jnp.zeros((side, side), F32)
        for m in range(modes):
            pr = probe_ref[0, m]
            pi = probe_ref[1, m]
            g_r = back[m * side : (m + 1) * side, :side]
            g_i = back[m * side : (m + 1) * side, side:]
            sum_r = sum_r + (pr * g_r + pi * g_i)
            sum_i = sum_i + (pr * g_i - pi * g_r)
            pgrad[0, m] += patch_r * g_r + patch_i * g_i
            pgrad[1, m] += patch_r * g_i - patch_i * g_r
        for c, v in enumerate((sum_r, sum_i)):
            parts = [pltpu.roll(v[:, j * LANES : (j + 1) * LANES], cr, 1) for j in range(side // LANES)]
            for j in range(side // LANES + 1):
                low = parts[j - 1] if j > 0 else jnp.zeros((side, LANES), F32)
                high = parts[j] if j < side // LANES else jnp.zeros((side, LANES), F32)
                grad[c, jnp.minimum(cq + j, nblk + 1), pl.ds(row, side), :] += jnp.where(lane >= cr, high, low)

    gather(0, 0)
    exits(0)
    left(lt_ref[...], waves, firsts)
    make_chi(0)

    def step(s, carry):
        slot = s % 2
        gather(s + 1, 1 - slot)
        left(rt_ref[...], chi, backs)
        exits(1 - slot)
        back = matmul(backs[...], lt_ref[...])
        left(lt_ref[...], waves, firsts)
        finish(s, slot, back)
        make_chi(s + 1)
        return carry

    lax.fori_loop(0, count - 1, step, 0)
    last = count - 1
    left(rt_ref[...], chi, backs)
    finish(last, last % 2, matmul(backs[...], lt_ref[...]))
    copies = []

    def put(src, dst):
        copies.append(pltpu.make_async_copy(src, dst, sems.at[len(copies)]))
        copies[-1].start()

    for c in range(2):
        for b in range(nblk):
            put(grad.at[c, b + 1, HALO : HALO + tile, :], obj_hbm.at[c, :, b * LANES : (b + 1) * LANES])
        put(grad.at[c, 1 : nblk + 1, pl.ds(row_a, HALO), :], strip_a_hbm.at[c])
        put(grad.at[c, 1 : nblk + 1, pl.ds(row_b, HALO), :], strip_b_hbm.at[c])
    for m in range(modes):
        for i in range(side // CHUNK):
            for j in range(side // LANES):
                k = (m * (side // CHUNK) + i) * (side // LANES) + j
                at = (m, slice(i * CHUNK, (i + 1) * CHUNK), slice(j * LANES, (j + 1) * LANES))
                send[k] = pgrad[(1 - core,) + at].astype(BF16)
                keep_out[k] = pgrad[(core,) + at]
    put(send, send_hbm)
    put(keep_out, keep_hbm)
    for c in range(2):
        out_a[c] = grad[c, col_a].astype(BF16)
        out_b[c] = grad[c, col_b].astype(BF16)
    put(out_a, out_a_hbm)
    put(out_b, out_b_hbm)
    for copy in copies:
        copy.wait()


def prepare_kernel(mid_hbm, probe_hbm, amp_hbm, tables_hbm, ext, grad, pgrad, probe, amp, tables, mid, sems):
    tile = mid.shape[1]
    copies = [
        pltpu.make_async_copy(src, dst, sems.at[i])
        for i, (src, dst) in enumerate(((mid_hbm, mid), (probe_hbm, probe), (amp_hbm, amp), (tables_hbm, tables)))
    ]
    for copy in copies:
        copy.start()
    grad[...] = jnp.zeros_like(grad)
    pgrad[...] = jnp.zeros_like(pgrad)
    copies[0].wait()
    for c in range(2):
        for b in range(tile // LANES):
            ext[c, b + 1, HALO : HALO + tile, :] = mid[c, :, b * LANES : (b + 1) * LANES].astype(F32)
    for copy in copies[1:]:
        copy.wait()


def prepare(mid, probe, amp, tables):
    tile = mid.shape[1]
    big = pltpu.VMEM((2, tile // LANES + 2, tile + 2 * HALO, LANES), F32)
    hbm = pl.BlockSpec(memory_space=pltpu.HBM)
    return pl.pallas_call(
        prepare_kernel,
        out_shape=(big, big, pltpu.VMEM(probe.shape, F32), pltpu.VMEM(probe.shape, F32), pltpu.VMEM(amp.shape, BF16),
                   pltpu.VMEM(tables.shape, BF16)),
        in_specs=[hbm] * 4,
        out_specs=(VM,) * 6,
        scratch_shapes=[pltpu.VMEM(mid.shape, BF16), pltpu.SemaphoreType.DMA((4,))],
        compiler_params=pltpu.CompilerParams(vmem_limit_bytes=16 * 1024 * 1024),
        cost_estimate=pl.CostEstimate(flops=5000000000, transcendentals=0, bytes_accessed=0),
        name="prepare",
    )(*[pltpu.with_memory_space_constraint(x, pltpu.HBM) for x in (mid, probe, amp, tables)])


def run_frames(count, pos, halo, prepared):
    ext, grad, pgrad, probe, amp, tables = prepared
    side = probe.shape[-1]
    modes = probe.shape[1]
    nblk = ext.shape[1] - 2
    rows = ext.shape[2]
    tile = rows - 2 * HALO
    chunks = modes * side * side // (CHUNK * LANES)
    first = 2 + len(halo)
    return pl.pallas_call(
        frames_kernel,
        out_shape=(
            pltpu.VMEM(ext.shape, F32),
            pltpu.VMEM(grad.shape, F32),
            pltpu.VMEM(pgrad.shape, F32),
            pltpu.HBM((2, tile, tile), F32),
            pltpu.HBM((2, nblk, HALO, LANES), F32),
            pltpu.HBM((2, nblk, HALO, LANES), F32),
            pltpu.HBM((2, rows, LANES), BF16),
            pltpu.HBM((2, rows, LANES), BF16),
            pltpu.HBM((chunks, CHUNK, LANES), F32),
            pltpu.HBM((chunks, CHUNK, LANES), BF16),
        ),
        in_specs=[SM, SM] + [VM] * (len(halo) + 6),
        out_specs=(VM,) * 3 + (pl.BlockSpec(memory_space=pltpu.HBM),) * 7,
        input_output_aliases={first: 0, first + 1: 1, first + 2: 2},
        scratch_shapes=[
            pltpu.VMEM((2, 2, side, side), F32),
            pltpu.VMEM((modes, 2 * side, side), BF16),
            pltpu.VMEM((modes, 2 * side, side), BF16),
            pltpu.VMEM((modes * side, 2 * side), BF16),
            pltpu.VMEM((modes * side, 2 * side), BF16),
            pltpu.VMEM((2, rows, LANES), BF16),
            pltpu.VMEM((2, rows, LANES), BF16),
            pltpu.VMEM((chunks, CHUNK, LANES), F32),
            pltpu.VMEM((chunks, CHUNK, LANES), BF16),
            pltpu.SemaphoreType.DMA((2 * nblk + 8,)),
        ],
        compiler_params=pltpu.CompilerParams(vmem_limit_bytes=20 * 1024 * 1024),
        name="frames",
    )(count, pos, *halo, *prepared)[3:]


def row_margin_kernel(
    strip_a_hbm, strip_b_hbm, got_a_ref, got_b_ref, out_a_ref, out_b_ref, strip_a_ref, strip_b_ref, sem_a, sem_b
):
    nblk, rows = strip_a_ref.shape[1], got_a_ref.shape[1]
    row_odd, core = place()
    copy_a = pltpu.make_async_copy(strip_a_hbm, strip_a_ref, sem_a)
    copy_b = pltpu.make_async_copy(strip_b_hbm, strip_b_ref, sem_b)
    copy_a.start()
    copy_b.start()
    copy_a.wait()
    copy_b.wait()

    def emit(own_ref, out_ref, start):
        for c in range(2):
            for b in range(nblk):
                out_ref[c, b] = own_ref[c, b].astype(BF16)
            for got_ref, blk in ((got_a_ref, (1 - core) * (nblk - 1)), (got_b_ref, core * (nblk - 1))):
                out_ref[c, blk] = (own_ref[c, blk] + got_ref[c, start : start + HALO, :].astype(F32)).astype(BF16)

    @pl.when(row_odd == 0)
    def _():
        emit(strip_a_ref, out_a_ref, rows - HALO)
        emit(strip_b_ref, out_b_ref, 0)

    @pl.when(row_odd == 1)
    def _():
        emit(strip_a_ref, out_a_ref, 0)
        emit(strip_b_ref, out_b_ref, rows - HALO)


def row_margins(strip_a, strip_b, got_a, got_b):
    shape = jax.ShapeDtypeStruct(strip_a.shape, BF16)
    return pl.pallas_call(
        row_margin_kernel,
        out_shape=(shape, shape),
        in_specs=[pl.BlockSpec(memory_space=pltpu.HBM)] * 2 + [VM] * 2,
        out_specs=(VM, VM),
        scratch_shapes=[
            pltpu.VMEM(strip_a.shape, F32),
            pltpu.VMEM(strip_b.shape, F32),
            pltpu.SemaphoreType.DMA(()),
            pltpu.SemaphoreType.DMA(()),
        ],
        compiler_params=pltpu.CompilerParams(vmem_limit_bytes=16 * 1024 * 1024),
        cost_estimate=pl.CostEstimate(flops=5000000000, transcendentals=0, bytes_accessed=0),
        name="row_margins",
    )(*[pltpu.with_memory_space_constraint(x, pltpu.HBM) for x in (strip_a, strip_b)], got_a, got_b)


def add_cols_kernel(part_ref, col_a_ref, col_b_ref, obj_ref):
    tile = part_ref.shape[1]
    inner = slice(HALO, HALO + tile)
    at_b = pl.program_id(0) == lax.axis_index("core")

    @pl.when(at_b)
    def _():
        obj_ref[...] = part_ref[...] + col_b_ref[:, inner, :].astype(F32)

    @pl.when(jnp.logical_not(at_b))
    def _():
        obj_ref[...] = part_ref[...] + col_a_ref[:, inner, :].astype(F32)


def add_cols(part, col_a, col_b):
    tile, cols = part.shape[1:]
    edge = pl.BlockSpec((2, tile, LANES), lambda i: (0, 0, i * (cols // LANES - 1)))
    return pl.pallas_call(
        add_cols_kernel,
        grid=(2,),
        out_shape=jax.ShapeDtypeStruct(part.shape, F32),
        in_specs=[edge, VM, VM],
        out_specs=edge,
        input_output_aliases={0: 0},
        cost_estimate=pl.CostEstimate(flops=5000000000, transcendentals=0, bytes_accessed=0),
        compiler_params=pltpu.CompilerParams(vmem_limit_bytes=16 * 1024 * 1024),
        name="add_cols",
    )(part, col_a, col_b)


def add_rows_kernel(part_ref, row_a_ref, row_b_ref, obj_ref):
    nblk = row_a_ref.shape[1]
    at_b = pl.program_id(0) == lax.axis_index("row") % 2

    def add(row_ref):
        for c in range(2):
            for b in range(nblk):
                cols = slice(b * LANES, (b + 1) * LANES)
                obj_ref[c, :, cols] = part_ref[c, :, cols] + row_ref[c, b].astype(F32)

    @pl.when(at_b)
    def _():
        add(row_b_ref)

    @pl.when(jnp.logical_not(at_b))
    def _():
        add(row_a_ref)


def add_rows(part, row_a, row_b):
    tile, cols = part.shape[1:]
    edge = pl.BlockSpec((2, HALO, cols), lambda i: (0, i * (tile // HALO - 1), 0))
    return pl.pallas_call(
        add_rows_kernel,
        grid=(2,),
        out_shape=jax.ShapeDtypeStruct(part.shape, F32),
        in_specs=[edge, VM, VM],
        out_specs=edge,
        input_output_aliases={0: 0},
        cost_estimate=pl.CostEstimate(flops=5000000000, transcendentals=0, bytes_accessed=0),
        compiler_params=pltpu.CompilerParams(vmem_limit_bytes=16 * 1024 * 1024),
        name="add_rows",
    )(part, row_a, row_b)


def probe_kernel(mine_ref, theirs_ref, out_ref):
    core = lax.axis_index("core")
    modes, side = out_ref.shape[1], out_ref.shape[2]
    for part_ref, at in ((mine_ref, core), (theirs_ref, 1 - core)):
        for m in range(modes):
            for i in range(side // CHUNK):
                for j in range(side // LANES):
                    k = (m * (side // CHUNK) + i) * (side // LANES) + j
                    out_ref[at, m, i * CHUNK : (i + 1) * CHUNK, j * LANES : (j + 1) * LANES] = part_ref[k].astype(F32)


def finish_probe(mine, theirs, shape):
    return pl.pallas_call(
        probe_kernel,
        out_shape=jax.ShapeDtypeStruct(shape, F32),
        in_specs=[VM, VM],
        out_specs=VM,
        compiler_params=pltpu.CompilerParams(vmem_limit_bytes=16 * 1024 * 1024),
        name="finish_probe",
    )(mine, theirs)


def trade(value, axis, phase):
    n = lax.axis_size(axis)
    pairs = [(i, ((i + phase) ^ 1) - phase) for i in range(n)]
    return lax.ppermute(value, axis, [(i, j) for i, j in pairs if 0 <= j < n])


def shards(object_field, probe_modes, measured_amp, scan_positions, frame_counts):
    slots = measured_amp.shape[2]
    to_edge_a, to_edge_b, to_row_a, to_row_b, to_col_a, to_col_b = margins(object_field)
    edge_b = trade(to_edge_b, "row", 1)
    edge_a = trade(to_edge_a, "row", 0)
    col_b = trade(to_col_b, COL, 1)
    col_a = trade(to_col_a, COL, 0)
    row_b = trade(to_row_b, "row", 1)
    row_a = trade(to_row_a, "row", 0)
    to_cor_a, to_cor_b = corners(edge_a, edge_b)
    cor_b = trade(to_cor_b, COL, 1)
    cor_a = trade(to_cor_a, COL, 0)
    prepared = prepare(object_field, probe_modes, measured_amp[0, 0], fourier_tables(probe_modes.shape[-1]))
    part, strip_a, strip_b, out_a, out_b, keep, send = run_frames(
        frame_counts, scan_positions, (edge_a, edge_b, row_a, row_b, col_a, col_b, cor_a, cor_b), prepared
    )
    scale = 1.0 / math.sqrt(lax.axis_size("row") * lax.axis_size(COL) * slots)
    pair = (keep + trade(send, COL, 0).astype(F32)).astype(BF16)
    got_a = trade(out_a, COL, 0)
    got_b = trade(out_b, COL, 1)
    peers = lax.all_to_all(pair, PEERS, 0, 0, tiled=True)
    rows_a, rows_b = row_margins(strip_a, strip_b, got_a, got_b)
    part = add_cols(part, got_a, got_b)
    peers, part = lax.optimization_barrier((peers, part))
    back_a = trade(rows_a, "row", 0)
    back_b = trade(rows_b, "row", 1)
    total = (jnp.sum(peers.astype(F32), axis=0) * scale).astype(BF16)
    mine = lax.all_to_all(jnp.broadcast_to(total[None], send.shape), PEERS, 0, 0, tiled=True)
    obj = add_rows(part, back_a, back_b)
    mine, obj = lax.optimization_barrier((mine, obj))
    return obj, finish_probe(mine, trade(mine, COL, 0), probe_modes.shape)


def solution(mesh):
    n_col = mesh.shape["col"]
    fine = Mesh(mesh.devices.reshape(mesh.shape["row"], n_col // 2, 2), ("row",) + COL)
    in_specs = (
        P(None, "row", COL),
        P(),
        P("row", COL, None, None, None),
        P("row", COL, None, None),
        P("row", COL),
    )
    out_specs = (P(None, "row", COL), P())
    return jax.shard_map(shards, mesh=fine, in_specs=in_specs, out_specs=out_specs, check_vma=False)
```

time: 99.3 us -> 90.4 us (0.910)
  the two profiles are of different devices: /device:TPU:0 before, /device:TPU:1 now
where the time goes in v3:
time: 90.4 us; the launch traced here: 90.2 us
  starting transfers between devices  51.6 us (57%)
  Pallas kernels  18.6 us (21%)
  waiting for transfers between devices  15.8 us (17%)
  other arithmetic  1.89 us (2%)
  between operations  1.5 us (2%)
    ppermute x14, starting transfers between devices, trade(): return lax.ppermute(value, axis, [(i, j) for i, j in pairs if 0 <= j < n])  33.3 us
    all_to_all x1, starting transfers between devices, shards(): peers = lax.all_to_all(pair, PEERS, 0, 0, tiled=True)  11.2 us
    pallas_call x1, Pallas kernels, run_frames(): pl.pallas_call(frames_kernel, out_shape=(pltpu.VMEM(ext.shape, F32), pltp...  8.49 us
    all_to_all x1, starting transfers between devices, shards(): lax.all_to_all(jnp.broadcast_to(total[None], send.shape), PEERS, 0, 0, ti...  7.13 us
    all_to_all x1, waiting for transfers between devices, shards(): lax.all_to_all(jnp.broadcast_to(total[None], send.shape), PEERS, 0, 0, ti...  7.11 us
    ppermute x14, waiting for transfers between devices, trade(): return lax.ppermute(value, axis, [(i, j) for i, j in pairs if 0 <= j < n])  4.6 us
    all_to_all x1, waiting for transfers between devices, shards(): peers = lax.all_to_all(pair, PEERS, 0, 0, tiled=True)  4.06 us
    pallas_call x1, Pallas kernels, prepare(): pl.pallas_call(prepare_kernel, out_shape=(big, big, pltpu.VMEM(probe.shap...  2.21 us
  transfers between devices with their start and end apart: 16, of which 4 were waited for; matrix products, arithmetic and copies ran while one was open for 3% of the time, Pallas kernels for 9%

profile of v3, /device:TPU:1, one launch (start us, length us, event | category | flops | bytes accessed | tf_op | source)
XLA Modules:
  0.0 90.2 jit_solution(5221169779399286219)
XLA Ops:
  0.6 1.4 %margins.1 = (bf16[4,128,128]{2,1,0:T(8,128)(2,1)S(1)}, bf16[4,128,128]{2,1,0:T(8,128)(2,1)S(1)}, bf16[2,128,256]{2,1,0:T(8,128)(2,1)S(1)}, bf16[2,128,256]{2,1,...) custom-call(bf16[2,512,512]{2,1,0:T(8,128)(2,1)} %mid_hbm.1), custom_call_target="tpu_custom_call" | custom-call | tf_op jit(solution)/shard_map/margins/pallas_call | solution.py:64
  2.0 2.5 %collective-permute-start = (bf16[4,128,128]{2,1,0:T(8,128)(2,1)S(1)}, bf16[4,128,128]{2,1,0:T(8,128)(2,1)S(1)}, u32[]{:S(2)}, u32[]{:S(2)}) collective-permute-start(bf16[4,128,128]{2,1,0:T(8,128)(2,1)S(1)} %get-tuple-element.29), channel_id=1, source_target_pairs={{0,16},{16,0},{32,48},{48,32},{64,80},{80,64},{96,112},{112,96},{1... | collective-permute-start | bytes 393224 | tf_op jit(solution)/shard_map/ppermute | solution.py:456
  5.3 4.3 %collective-permute-start.2 = (bf16[2,128,256]{2,1,0:T(8,128)(2,1)S(1)}, bf16[2,128,256]{2,1,0:T(8,128)(2,1)S(1)}, u32[]{:S(2)}, u32[]{:S(2)}) collective-permute-start(bf16[2,128,256]{2,1,0:T(8,128)(2,1)S(1)} %get-tuple-element.31), channel_id=1, source_target_pairs={{0,16},{16,0},{32,48},{48,32},{64,80},{80,64},{96,112},{112,96},{1... | collective-permute-start | bytes 393224 | tf_op jit(solution)/shard_map/ppermute | solution.py:456
  10.2 1.6 %collective-permute-start.4 = (bf16[2,512,128]{2,1,0:T(8,128)(2,1)S(1)}, bf16[2,512,128]{2,1,0:T(8,128)(2,1)S(1)}, u32[]{:S(2)}, u32[]{:S(2)}) collective-permute-start(bf16[2,512,128]{2,1,0:T(8,128)(2,1)S(1)} %get-tuple-element.33), channel_id=1, source_target_pairs={{0,1},{1,0},{2,3},{3,2},{4,5},{5,4},{6,7},{7,6},{8,9},{9,8},{10,11... | collective-permute-start | bytes 786440 | tf_op jit(solution)/shard_map/ppermute | solution.py:456
  11.8 3.0 %collective-permute-start.5 = (bf16[2,512,128]{2,1,0:T(8,128)(2,1)S(1)}, bf16[2,512,128]{2,1,0:T(8,128)(2,1)S(1)}, u32[]{:S(2)}, u32[]{:S(2)}) collective-permute-start(bf16[2,512,128]{2,1,0:T(8,128)(2,1)S(1)} %get-tuple-element.34), channel_id=1, source_target_pairs={{1,2},{2,1},{3,4},{4,3},{5,6},{6,5},{7,8},{8,7},{9,10},{10,9},{11,... | collective-permute-start | bytes 786440 | tf_op jit(solution)/shard_map/ppermute | solution.py:456
  15.0 3.5 %collective-permute-start.7 = (bf16[4,128,128]{2,1,0:T(8,128)(2,1)S(1)}, bf16[4,128,128]{2,1,0:T(8,128)(2,1)S(1)}, u32[]{:S(2)}, u32[]{:S(2)}) collective-permute-start(bf16[4,128,128]{2,1,0:T(8,128)(2,1)S(1)} %get-tuple-element.36), channel_id=1, source_target_pairs={{1,2},{2,1},{3,4},{4,3},{5,6},{6,5},{7,8},{8,7},{9,10},{10,9},{11,... | collective-permute-start | bytes 393224 | tf_op jit(solution)/shard_map/ppermute | solution.py:456
  18.6 2.2 %prepare.1 = (f32[2,6,768,128]{3,2,1,0:T(8,128)S(1)}, f32[2,6,768,128]{3,2,1,0:T(8,128)S(1)}, f32[2,2,256,256]{3,2,1,0:T(8,128)S(1)}, f32[2,2,256,256]{3,2,1,0:T...) custom-call(bf16[2,512,512]{2,1,0:T(8,128)(2,1)} %mid_hbm.1, ...), custom_call_target="tpu_custom_call" | custom-call | flops 5000000000 | tf_op jit(solution)/shard_map/prepare/pallas_call | solution.py:261
  21.4 3.4 %collective-permute-done.7.cor_b_ref = bf16[4,128,128]{2,1,0:T(8,128)(2,1)S(1)} collective-permute-done((bf16[4,128,128]{2,1,0:T(8,128)(2,1)S(1)}, bf16[4,128,128]{2,1,0:T(8,128)(2,1)S(1)}, u32[]{:S(2)}, u32[]{:S(2)}) %collective-permute-start.7) | collective-permute-done | bytes 131104 | tf_op jit(solution)/shard_map/ppermute | solution.py:456
  24.9 8.5 %frames.1 = (f32[2,6,768,128]{3,2,1,0:T(8,128)S(1)}, f32[2,6,768,128]{3,2,1,0:T(8,128)S(1)}, f32[2,2,256,256]{3,2,1,0:T(8,128)S(1)}, f32[2,512,512]{2,1,0:T(8,12...) custom-call(s32[1,1]{1,0:T(1,128)S(6)} %copy.19.count_ref, ...), custom_call_target="tpu_custom_call", output_to_operand_aliasing={{0}: (10, {}), {1}: (11, {}), {2}: (12, {})} | custom-call | tf_op jit(solution)/shard_map/frames/pallas_call | solution.py:283
  34.0 11.4 %collective-permute-start.10 = (bf16[2,768,128]{2,1,0:T(8,128)(2,1)}, bf16[2,768,128]{2,1,0:T(8,128)(2,1)S(1)}, u32[]{:S(2)}, u32[]{:S(2)}) collective-permute-start(bf16[2,768,128]{2,1,0:T(8,128)(2,1)} %get-tuple-element.47), channel_id=1, source_target_pairs={{1,2},{2,1},{3,4},{4,3},{5,6},{6,5},{7,8},{8,7},{9,10},{10,9},{11,... | collective-permute-start | bytes 1179656 | tf_op jit(solution)/shard_map/ppermute | solution.py:456
  45.4 1.8 %add_convert_fusion = bf16[64,16,128]{2,1,0:T(8,128)(2,1)} fusion(f32[64,16,128]{2,1,0:T(8,128)} %get-tuple-element.43, bf16[64,16,128]{2,1,0:T(8,128)(2,1)S(1)} %collective-permute-done.8), kind=kLoop, calls=%fused_computation.1 | loop fusion | flops 393216 | bytes 1048576 | tf_op jit(solution)/shard_map/convert_element_type | solution.py:476
  47.2 11.2 %all-to-all-start = ((bf16[64,16,128]{2,1,0:T(8,128)(2,1)}), bf16[64,16,128]{2,1,0:T(8,128)(2,1)S(1)}, u32[]{:S(2)}, u32[]{:S(2)}) async-start(bf16[64,16,128]{2,1,0:T(8,128)(2,1)} %add_convert_fusion), calls=%async_computation | async-start | bytes 524288 | tf_op jit(solution)/shard_map/all_to_all | solution.py:479
  58.5 1.3 %row_margins.1 = (bf16[2,4,128,128]{3,2,1,0:T(8,128)(2,1)S(1)}, bf16[2,4,128,128]{3,2,1,0:T(8,128)(2,1)S(1)}) custom-call(f32[2,4,128,128]{3,2,1,0:T(8,128)} %get-tuple-element.50.strip_a_hbm, f32[2,4,128,128]{3,2,1,0:T(8,128)} %get-tuple-element.51.strip_b_hbm, bf16[2,768,128]{2,1,0:T(8,128)(2,1)S(1)} %collective-permute-done.9.col_a_ref.got_a_ref, ...), custom_call_target="tpu_custom_call" | custom-call | flops 5000000000 | tf_op jit(solution)/shard_map/row_margins/pallas_call | solution.py:349
  59.8 1.1 %collective-permute-start.11 = (bf16[2,4,128,128]{3,2,1,0:T(8,128)(2,1)S(1)}, bf16[2,4,128,128]{3,2,1,0:T(8,128)(2,1)S(1)}, u32[]{:S(2)}, u32[]{:S(2)}) collective-permute-start(bf16[2,4,128,128]{3,2,1,0:T(8,128)(2,1)S(1)} %get-tuple-element.52), channel_id=1, source_target_pairs={{0,16},{16,0},{32,48},{48,32},{64,80},{80,64},{96,112},{112,96},{1... | collective-permute-start | bytes 786440 | tf_op jit(solution)/shard_map/ppermute | solution.py:456
  60.9 0.7 collective-permute-start.12
  61.5 2.1 %add_cols.1.part_ref = f32[2,512,512]{2,1,0:T(8,128)} custom-call(f32[2,512,512]{2,1,0:T(8,128)} %get-tuple-element.45.part_ref, bf16[2,768,128]{2,1,0:T(8,128)(2,1)S(1)} %collective-permute-done.9.col_a_ref.got_a_ref, bf16[2,768,128]{2,1,0:T(8,128)(2,1)S(1)} %collective-permute-done.10.col_b_ref.got_b_ref), custom_call_target="tpu_custom_call", output_to_operand_aliasing={{}: (0, {})} | custom-call | flops 5000000000 | tf_op jit(solution)/shard_map/add_cols/pallas_call | solution.py:383
  63.6 4.1 %all-to-all-done = bf16[64,16,128]{2,1,0:T(8,128)(2,1)S(1)} async-done(((bf16[64,16,128]{2,1,0:T(8,128)(2,1)}), bf16[64,16,128]{2,1,0:T(8,128)(2,1)S(1)}, u32[]{:S(2)}, u32[]{:S(2)}) %all-to-all-start) | async-done | bytes 262176 | tf_op jit(solution)/shard_map/all_to_all | solution.py:479
  67.8 0.7 broadcast_in_dim.2
  68.5 7.1 %all-to-all-start.1 = ((bf16[64,16,128]{2,1,0:T(8,128)(2,1)}), bf16[64,16,128]{2,1,0:T(8,128)(2,1)S(1)}, u32[]{:S(2)}, u32[]{:S(2)}) async-start(bf16[64,16,128]{2,1,0:T(8,128)(2,1)} %broadcast_in_dim.2), calls=%async_computation.1 | async-start | bytes 524288 | tf_op jit(solution)/shard_map/all_to_all | solution.py:486
  75.6 2.1 %add_rows.1 = f32[2,512,512]{2,1,0:T(8,128)} custom-call(f32[2,512,512]{2,1,0:T(8,128)} %add_cols.1.part_ref, bf16[2,4,128,128]{3,2,1,0:T(8,128)(2,1)S(1)} %collective-permute-done.11.row_a_ref, bf16[2,4,128,128]{3,2,1,0:T(8,128)(2,1)S(1)} %collective-permute-done.12.row_b_ref), custom_call_target="tpu_custom_call", output_to_operand_aliasing={{}: (0, {})} | custom-call | flops 5000000000 | tf_op jit(solution)/shard_map/add_rows/pallas_call | solution.py:418
  77.7 7.1 %all-to-all-done.1.mine_ref = bf16[64,16,128]{2,1,0:T(8,128)(2,1)S(1)} async-done(((bf16[64,16,128]{2,1,0:T(8,128)(2,1)}), bf16[64,16,128]{2,1,0:T(8,128)(2,1)S(1)}, u32[]{:S(2)}, u32[]{:S(2)}) %all-to-all-start.1) | async-done | bytes 262176 | tf_op jit(solution)/shard_map/all_to_all | solution.py:486
  84.8 3.1 %collective-permute-start.13 = (bf16[64,16,128]{2,1,0:T(8,128)(2,1)S(1)}, bf16[64,16,128]{2,1,0:T(8,128)(2,1)S(1)}, u32[]{:S(2)}, u32[]{:S(2)}) collective-permute-start(bf16[64,16,128]{2,1,0:T(8,128)(2,1)S(1)} %all-to-all-done.1.mine_ref), channel_id=1, source_target_pairs={{0,1},{1,0},{2,3},{3,2},{4,5},{5,4},{6,7},{7,6},{8,9},{9,8},{10,11... | collective-permute-start | bytes 786440 | tf_op jit(solution)/shard_map/ppermute | solution.py:456
  88.0 1.2 %collective-permute-done.13.theirs_ref = bf16[64,16,128]{2,1,0:T(8,128)(2,1)S(1)} collective-permute-done((bf16[64,16,128]{2,1,0:T(8,128)(2,1)S(1)}, bf16[64,16,128]{2,1,0:T(8,128)(2,1)S(1)}, u32[]{:S(2)}, u32[]{:S(2)}) %collective-permute-start.13) | collective-permute-done | bytes 262176 | tf_op jit(solution)/shard_map/ppermute | solution.py:456
  89.1 1.0 %finish_probe.1 = f32[2,2,256,256]{3,2,1,0:T(8,128)} custom-call(bf16[64,16,128]{2,1,0:T(8,128)(2,1)S(1)} %all-to-all-done.1.mine_ref, bf16[64,16,128]{2,1,0:T(8,128)(2,1)S(1)} %collective-permute-done.13.theirs_ref), custom_call_target="tpu_custom_call" | custom-call | tf_op jit(solution)/shard_map/finish_probe/pallas_call | solution.py:443
  (22 shorter events, 2.1 us)
Async XLA Ops:
  2.0 9.8 %collective-permute-start = (bf16[4,128,128]{2,1,0:T(8,128)(2,1)S(1)}, bf16[4,128,128]{2,1,0:T(8,128)(2,1)S(1)}, u32[]{:S(2)}, u32[]{:S(2)}) collective-permute-start(bf16[4,128,128]{2,1,0:T(8,128)(2,1)S(1)} %get-tuple-element.29), channel_id=1, source_target_pairs={{0,16},{16,0},{32,48},{48,32},{64,80},{80,64},{96,112},{112,96},{1... | collective-permute-start | bytes 393224 | tf_op jit(solution)/shard_map/ppermute | solution.py:456
  4.6 10.3 %collective-permute-start.1 = (bf16[4,128,128]{2,1,0:T(8,128)(2,1)S(1)}, bf16[4,128,128]{2,1,0:T(8,128)(2,1)S(1)}, u32[]{:S(2)}, u32[]{:S(2)}) collective-permute-start(bf16[4,128,128]{2,1,0:T(8,128)(2,1)S(1)} %get-tuple-element.30), channel_id=1, source_target_pairs={{16,32},{32,16},{48,64},{64,48},{80,96},{96,80},{17,33},{33,17},{4... | collective-permute-start | bytes 393224 | tf_op jit(solution)/shard_map/ppermute | solution.py:456
  5.3 9.7 %collective-permute-start.2 = (bf16[2,128,256]{2,1,0:T(8,128)(2,1)S(1)}, bf16[2,128,256]{2,1,0:T(8,128)(2,1)S(1)}, u32[]{:S(2)}, u32[]{:S(2)}) collective-permute-start(bf16[2,128,256]{2,1,0:T(8,128)(2,1)S(1)} %get-tuple-element.31), channel_id=1, source_target_pairs={{0,16},{16,0},{32,48},{48,32},{64,80},{80,64},{96,112},{112,96},{1... | collective-permute-start | bytes 393224 | tf_op jit(solution)/shard_map/ppermute | solution.py:456
  9.6 11.9 %collective-permute-start.3 = (bf16[2,128,256]{2,1,0:T(8,128)(2,1)S(1)}, bf16[2,128,256]{2,1,0:T(8,128)(2,1)S(1)}, u32[]{:S(2)}, u32[]{:S(2)}) collective-permute-start(bf16[2,128,256]{2,1,0:T(8,128)(2,1)S(1)} %get-tuple-element.32), channel_id=1, source_target_pairs={{16,32},{32,16},{48,64},{64,48},{80,96},{96,80},{17,33},{33,17},{4... | collective-permute-start | bytes 393224 | tf_op jit(solution)/shard_map/ppermute | solution.py:456
  10.2 14.6 %collective-permute-start.4 = (bf16[2,512,128]{2,1,0:T(8,128)(2,1)S(1)}, bf16[2,512,128]{2,1,0:T(8,128)(2,1)S(1)}, u32[]{:S(2)}, u32[]{:S(2)}) collective-permute-start(bf16[2,512,128]{2,1,0:T(8,128)(2,1)S(1)} %get-tuple-element.33), channel_id=1, source_target_pairs={{0,1},{1,0},{2,3},{3,2},{4,5},{5,4},{6,7},{7,6},{8,9},{9,8},{10,11... | collective-permute-start | bytes 786440 | tf_op jit(solution)/shard_map/ppermute | solution.py:456
  11.8 13.0 %collective-permute-start.5 = (bf16[2,512,128]{2,1,0:T(8,128)(2,1)S(1)}, bf16[2,512,128]{2,1,0:T(8,128)(2,1)S(1)}, u32[]{:S(2)}, u32[]{:S(2)}) collective-permute-start(bf16[2,512,128]{2,1,0:T(8,128)(2,1)S(1)} %get-tuple-element.34), channel_id=1, source_target_pairs={{1,2},{2,1},{3,4},{4,3},{5,6},{6,5},{7,8},{8,7},{9,10},{10,9},{11,... | collective-permute-start | bytes 786440 | tf_op jit(solution)/shard_map/ppermute | solution.py:456
  14.9 6.5 %collective-permute-start.6 = (bf16[4,128,128]{2,1,0:T(8,128)(2,1)S(1)}, bf16[4,128,128]{2,1,0:T(8,128)(2,1)S(1)}, u32[]{:S(2)}, u32[]{:S(2)}) collective-permute-start(bf16[4,128,128]{2,1,0:T(8,128)(2,1)S(1)} %get-tuple-element.35), channel_id=1, source_target_pairs={{0,1},{1,0},{2,3},{3,2},{4,5},{5,4},{6,7},{7,6},{8,9},{9,8},{10,11... | collective-permute-start | bytes 393224 | tf_op jit(solution)/shard_map/ppermute | solution.py:456
  15.0 9.9 %collective-permute-start.7 = (bf16[4,128,128]{2,1,0:T(8,128)(2,1)S(1)}, bf16[4,128,128]{2,1,0:T(8,128)(2,1)S(1)}, u32[]{:S(2)}, u32[]{:S(2)}) collective-permute-start(bf16[4,128,128]{2,1,0:T(8,128)(2,1)S(1)} %get-tuple-element.36), channel_id=1, source_target_pairs={{1,2},{2,1},{3,4},{4,3},{5,6},{6,5},{7,8},{8,7},{9,10},{10,9},{11,... | collective-permute-start | bytes 393224 | tf_op jit(solution)/shard_map/ppermute | solution.py:456
  18.5 6.3 %copy-start = (s32[1,1,2,8]{3,2,1,0:T(2,128)S(1)}, s32[1,1,2,8]{3,2,1,0:T(2,128)}, u32[]{:S(2)}) copy-start(s32[1,1,2,8]{3,2,1,0:T(2,128)} %pos_ref.1) | copy-start | bytes 196
  33.4 12.0 %collective-permute-start.8 = (bf16[64,16,128]{2,1,0:T(8,128)(2,1)}, bf16[64,16,128]{2,1,0:T(8,128)(2,1)S(1)}, u32[]{:S(2)}, u32[]{:S(2)}) collective-permute-start(bf16[64,16,128]{2,1,0:T(8,128)(2,1)} %get-tuple-element.44), channel_id=1, source_target_pairs={{0,1},{1,0},{2,3},{3,2},{4,5},{5,4},{6,7},{7,6},{8,9},{9,8},{10,11... | collective-permute-start | bytes 786440 | tf_op jit(solution)/shard_map/ppermute | solution.py:456
  33.5 25.0 %collective-permute-start.9 = (bf16[2,768,128]{2,1,0:T(8,128)(2,1)}, bf16[2,768,128]{2,1,0:T(8,128)(2,1)S(1)}, u32[]{:S(2)}, u32[]{:S(2)}) collective-permute-start(bf16[2,768,128]{2,1,0:T(8,128)(2,1)} %get-tuple-element.46), channel_id=1, source_target_pairs={{0,1},{1,0},{2,3},{3,2},{4,5},{5,4},{6,7},{7,6},{8,9},{9,8},{10,11... | collective-permute-start | bytes 1179656 | tf_op jit(solution)/shard_map/ppermute | solution.py:456
  34.0 24.5 %collective-permute-start.10 = (bf16[2,768,128]{2,1,0:T(8,128)(2,1)}, bf16[2,768,128]{2,1,0:T(8,128)(2,1)S(1)}, u32[]{:S(2)}, u32[]{:S(2)}) collective-permute-start(bf16[2,768,128]{2,1,0:T(8,128)(2,1)} %get-tuple-element.47), channel_id=1, source_target_pairs={{1,2},{2,1},{3,4},{4,3},{5,6},{6,5},{7,8},{8,7},{9,10},{10,9},{11,... | collective-permute-start | bytes 1179656 | tf_op jit(solution)/shard_map/ppermute | solution.py:456
  47.2 20.5 %all-to-all-start = ((bf16[64,16,128]{2,1,0:T(8,128)(2,1)}), bf16[64,16,128]{2,1,0:T(8,128)(2,1)S(1)}, u32[]{:S(2)}, u32[]{:S(2)}) async-start(bf16[64,16,128]{2,1,0:T(8,128)(2,1)} %add_convert_fusion), calls=%async_computation | async-start | bytes 524288 | tf_op jit(solution)/shard_map/all_to_all | solution.py:479
  59.8 15.9 %collective-permute-start.11 = (bf16[2,4,128,128]{3,2,1,0:T(8,128)(2,1)S(1)}, bf16[2,4,128,128]{3,2,1,0:T(8,128)(2,1)S(1)}, u32[]{:S(2)}, u32[]{:S(2)}) collective-permute-start(bf16[2,4,128,128]{3,2,1,0:T(8,128)(2,1)S(1)} %get-tuple-element.52), channel_id=1, source_target_pairs={{0,16},{16,0},{32,48},{48,32},{64,80},{80,64},{96,112},{112,96},{1... | collective-permute-start | bytes 786440 | tf_op jit(solution)/shard_map/ppermute | solution.py:456
  60.9 14.8 %collective-permute-start.12 = (bf16[2,4,128,128]{3,2,1,0:T(8,128)(2,1)S(1)}, bf16[2,4,128,128]{3,2,1,0:T(8,128)(2,1)S(1)}, u32[]{:S(2)}, u32[]{:S(2)}) collective-permute-start(bf16[2,4,128,128]{3,2,1,0:T(8,128)(2,1)S(1)} %get-tuple-element.53), channel_id=1, source_target_pairs={{16,32},{32,16},{48,64},{64,48},{80,96},{96,80},{17,33},{33,17},{4... | collective-permute-start | bytes 786440 | tf_op jit(solution)/shard_map/ppermute | solution.py:456
  68.5 16.3 %all-to-all-start.1 = ((bf16[64,16,128]{2,1,0:T(8,128)(2,1)}), bf16[64,16,128]{2,1,0:T(8,128)(2,1)S(1)}, u32[]{:S(2)}, u32[]{:S(2)}) async-start(bf16[64,16,128]{2,1,0:T(8,128)(2,1)} %broadcast_in_dim.2), calls=%async_computation.1 | async-start | bytes 524288 | tf_op jit(solution)/shard_map/all_to_all | solution.py:486
  84.8 4.3 %collective-permute-start.13 = (bf16[64,16,128]{2,1,0:T(8,128)(2,1)S(1)}, bf16[64,16,128]{2,1,0:T(8,128)(2,1)S(1)}, u32[]{:S(2)}, u32[]{:S(2)}) collective-permute-start(bf16[64,16,128]{2,1,0:T(8,128)(2,1)S(1)} %all-to-all-done.1.mine_ref), channel_id=1, source_target_pairs={{0,1},{1,0},{2,3},{3,2},{4,5},{5,4},{6,7},{7,6},{8,9},{9,8},{10,11... | collective-permute-start | bytes 786440 | tf_op jit(solution)/shard_map/ppermute | solution.py:456

commit v4 on v3

--- a/solution.py
+++ b/solution.py
@@ -1,3 +1,4 @@
+import functools
 import math
 
 import jax
@@ -36,7 +37,7 @@
     return jnp.dot(a, b, preferred_element_type=F32)
 
 
-def margins_kernel(obj, edge_a, edge_b, row_a, row_b, col_a, col_b, sems):
+def margins_kernel(obj, row_a, row_b, col_a, col_b, sems):
     tile = obj.shape[1]
     row_odd, core = place()
     copies = []
@@ -45,11 +46,8 @@
         copies.append(pltpu.make_async_copy(src, dst, sems.at[len(copies)]))
         copies[-1].start()
 
-    for edge, row, at in ((edge_b, row_b, row_odd), (edge_a, row_a, 1 - row_odd)):
-        rows = pl.ds(pl.multiple_of(at * (tile - HALO), HALO), HALO)
-        put(obj.at[:, rows, 0:HALO], edge.at[0:2])
-        put(obj.at[:, rows, tile - HALO :], edge.at[2:4])
-        put(obj.at[:, rows, HALO : tile - HALO], row)
+    for row, at in ((row_b, row_odd), (row_a, 1 - row_odd)):
+        put(obj.at[:, pl.ds(pl.multiple_of(at * (tile - HALO), HALO), HALO), :], row)
     for col, at in ((col_b, core), (col_a, 1 - core)):
         put(obj.at[:, :, pl.ds(pl.multiple_of(at * (tile - HALO), HALO), HALO)], col)
     for copy in copies:
@@ -58,29 +56,42 @@
 
 def margins(obj):
     tile = obj.shape[1]
-    edge = jax.ShapeDtypeStruct((4, HALO, HALO), BF16)
-    row = jax.ShapeDtypeStruct((2, HALO, tile - 2 * HALO), BF16)
+    row = jax.ShapeDtypeStruct((2, HALO, tile), BF16)
     col = jax.ShapeDtypeStruct((2, tile, HALO), BF16)
     return pl.pallas_call(
         margins_kernel,
-        out_shape=(edge, edge, row, row, col, col),
+        out_shape=(row, row, col, col),
         in_specs=[pl.BlockSpec(memory_space=pltpu.HBM)],
-        out_specs=(VM,) * 6,
-        scratch_shapes=[pltpu.SemaphoreType.DMA((8,))],
+        out_specs=(VM,) * 4,
+        scratch_shapes=[pltpu.SemaphoreType.DMA((4,))],
         compiler_params=pltpu.CompilerParams(vmem_limit_bytes=8 * 1024 * 1024),
         name="margins",
     )(pltpu.with_memory_space_constraint(obj, pltpu.HBM))
 
 
-def corners_kernel(edge_a, edge_b, cor_a, cor_b):
+def corners_kernel(row_a, row_b, cor_a, cor_b):
+    tile = row_a.shape[2]
     core = lax.axis_index("core")
-    for cor, at in ((cor_b, core), (cor_a, 1 - core)):
-        cor[0:2] = edge_a[pl.ds(2 * at, 2)]
-        cor[2:4] = edge_b[pl.ds(2 * at, 2)]
-
-
-def corners(edge_a, edge_b):
-    shape = jax.ShapeDtypeStruct(edge_a.shape, BF16)
+
+    def emit(cor, cols):
+        cor[0:2] = row_a[:, :, cols]
+        cor[2:4] = row_b[:, :, cols]
+
+    low, high = slice(0, HALO), slice(tile - HALO, tile)
+
+    @pl.when(core == 0)
+    def _():
+        emit(cor_a, high)
+        emit(cor_b, low)
+
+    @pl.when(core == 1)
+    def _():
+        emit(cor_a, low)
+        emit(cor_b, high)
+
+
+def corners(row_a, row_b):
+    shape = jax.ShapeDtypeStruct((4, HALO, HALO), BF16)
     return pl.pallas_call(
         corners_kernel,
         out_shape=(shape, shape),
@@ -88,14 +99,14 @@
         out_specs=(VM, VM),
         compiler_params=pltpu.CompilerParams(vmem_limit_bytes=8 * 1024 * 1024),
         name="corners",
-    )(edge_a, edge_b)
+    )(row_a, row_b)
 
 
 def frames_kernel(
-    count_ref, pos_ref, edge_a_ref, edge_b_ref, row_a_ref, row_b_ref, col_a_ref, col_b_ref, cor_a_ref, cor_b_ref,
+    count_ref, pos_ref, row_a_ref, row_b_ref, col_a_ref, col_b_ref, cor_a_ref, cor_b_ref,
     ext_ref, grad_ref, pgrad_ref, probe_ref, amp_ref, tables_ref,
-    ext, grad, pgrad, obj_hbm, strip_a_hbm, strip_b_hbm, out_a_hbm, out_b_hbm, keep_hbm, send_hbm,
-    patch, waves, chi, firsts, backs, out_a, out_b, keep_out, send, sems,
+    ext, grad, pgrad, obj_hbm, strip_a_hbm, strip_b_hbm, out_a_hbm, out_b_hbm, keep_out, send,
+    patch, waves, chi, firsts, backs, out_a, out_b, sems,
 ):
     side = probe_ref.shape[-1]
     modes = probe_ref.shape[1]
@@ -110,12 +121,8 @@
     lt_ref, rt_ref = tables_ref.at[0], tables_ref.at[1]
     for c in range(2):
         for b in range(nblk):
-            outer = b in (0, nblk - 1)
-            for at, edge_ref, row_ref in ((row_a, edge_a_ref, row_a_ref), (row_b, edge_b_ref, row_b_ref)):
-                if outer:
-                    ext[c, b + 1, pl.ds(at, HALO), :] = edge_ref[c + 2 * min(b, 1)].astype(F32)
-                else:
-                    ext[c, b + 1, pl.ds(at, HALO), :] = row_ref[c, :, (b - 1) * LANES : b * LANES].astype(F32)
+            for at, ref in ((row_a, row_a_ref), (row_b, row_b_ref)):
+                ext[c, b + 1, pl.ds(at, HALO), :] = ref[c, :, b * LANES : (b + 1) * LANES].astype(F32)
         for col, own_ref, cor_ref in ((col_a, col_a_ref, cor_a_ref), (col_b, col_b_ref, cor_b_ref)):
             ext[c, col, pl.ds(row_a, HALO), :] = cor_ref[c].astype(F32)
             ext[c, col, HALO : HALO + tile, :] = own_ref[c].astype(F32)
@@ -218,6 +225,11 @@
             put(grad.at[c, b + 1, HALO : HALO + tile, :], obj_hbm.at[c, :, b * LANES : (b + 1) * LANES])
         put(grad.at[c, 1 : nblk + 1, pl.ds(row_a, HALO), :], strip_a_hbm.at[c])
         put(grad.at[c, 1 : nblk + 1, pl.ds(row_b, HALO), :], strip_b_hbm.at[c])
+    for c in range(2):
+        out_a[c] = grad[c, col_a].astype(BF16)
+        out_b[c] = grad[c, col_b].astype(BF16)
+    put(out_a, out_a_hbm)
+    put(out_b, out_b_hbm)
     for m in range(modes):
         for i in range(side // CHUNK):
             for j in range(side // LANES):
@@ -225,13 +237,6 @@
                 at = (m, slice(i * CHUNK, (i + 1) * CHUNK), slice(j * LANES, (j + 1) * LANES))
                 send[k] = pgrad[(1 - core,) + at].astype(BF16)
                 keep_out[k] = pgrad[(core,) + at]
-    put(send, send_hbm)
-    put(keep_out, keep_hbm)
-    for c in range(2):
-        out_a[c] = grad[c, col_a].astype(BF16)
-        out_b[c] = grad[c, col_b].astype(BF16)
-    put(out_a, out_a_hbm)
-    put(out_b, out_b_hbm)
     for copy in copies:
         copy.wait()
 
@@ -291,11 +296,11 @@
             pltpu.HBM((2, nblk, HALO, LANES), F32),
             pltpu.HBM((2, rows, LANES), BF16),
             pltpu.HBM((2, rows, LANES), BF16),
-            pltpu.HBM((chunks, CHUNK, LANES), F32),
-            pltpu.HBM((chunks, CHUNK, LANES), BF16),
+            pltpu.VMEM((chunks, CHUNK, LANES), F32),
+            pltpu.VMEM((chunks, CHUNK, LANES), BF16),
         ),
         in_specs=[SM, SM] + [VM] * (len(halo) + 6),
-        out_specs=(VM,) * 3 + (pl.BlockSpec(memory_space=pltpu.HBM),) * 7,
+        out_specs=(VM,) * 3 + (pl.BlockSpec(memory_space=pltpu.HBM),) * 5 + (VM,) * 2,
         input_output_aliases={first: 0, first + 1: 1, first + 2: 2},
         scratch_shapes=[
             pltpu.VMEM((2, 2, side, side), F32),
@@ -305,13 +310,11 @@
             pltpu.VMEM((modes * side, 2 * side), BF16),
             pltpu.VMEM((2, rows, LANES), BF16),
             pltpu.VMEM((2, rows, LANES), BF16),
-            pltpu.VMEM((chunks, CHUNK, LANES), F32),
-            pltpu.VMEM((chunks, CHUNK, LANES), BF16),
-            pltpu.SemaphoreType.DMA((2 * nblk + 8,)),
+            pltpu.SemaphoreType.DMA((2 * nblk + 6,)),
         ],
-        compiler_params=pltpu.CompilerParams(vmem_limit_bytes=20 * 1024 * 1024),
+        compiler_params=pltpu.CompilerParams(vmem_limit_bytes=8 * 1024 * 1024),
         name="frames",
-    )(count, pos, *halo, *prepared)[3:]
+    )(count, pos, *halo, *prepared)
 
 
 def row_margin_kernel(
@@ -363,69 +366,66 @@
     )(*[pltpu.with_memory_space_constraint(x, pltpu.HBM) for x in (strip_a, strip_b)], got_a, got_b)
 
 
-def add_cols_kernel(part_ref, col_a_ref, col_b_ref, obj_ref):
-    tile = part_ref.shape[1]
+def peer_sum_kernel(scale, got_ref, out_ref):
+    total = jnp.sum(got_ref[...].astype(F32), axis=0) * scale
+    out_ref[...] = jnp.broadcast_to(total.astype(BF16)[None], out_ref.shape)
+
+
+def peer_sum(got, scale):
+    return pl.pallas_call(
+        functools.partial(peer_sum_kernel, scale),
+        out_shape=jax.ShapeDtypeStruct(got.shape, BF16),
+        in_specs=[VM],
+        out_specs=VM,
+        compiler_params=pltpu.CompilerParams(vmem_limit_bytes=8 * 1024 * 1024),
+        cost_estimate=pl.CostEstimate(flops=5000000000, transcendentals=0, bytes_accessed=0),
+        name="peer_sum",
+    )(got)
+
+
+def object_kernel(part_hbm, col_a_ref, col_b_ref, row_a_ref, row_b_ref, obj_hbm, acc, in_sems, out_sems):
+    nblk, tile = acc.shape[1], acc.shape[2]
+    row_odd, core = place()
     inner = slice(HALO, HALO + tile)
-    at_b = pl.program_id(0) == lax.axis_index("core")
-
-    @pl.when(at_b)
-    def _():
-        obj_ref[...] = part_ref[...] + col_b_ref[:, inner, :].astype(F32)
-
-    @pl.when(jnp.logical_not(at_b))
-    def _():
-        obj_ref[...] = part_ref[...] + col_a_ref[:, inner, :].astype(F32)
-
-
-def add_cols(part, col_a, col_b):
-    tile, cols = part.shape[1:]
-    edge = pl.BlockSpec((2, tile, LANES), lambda i: (0, 0, i * (cols // LANES - 1)))
-    return pl.pallas_call(
-        add_cols_kernel,
-        grid=(2,),
-        out_shape=jax.ShapeDtypeStruct(part.shape, F32),
-        in_specs=[edge, VM, VM],
-        out_specs=edge,
-        input_output_aliases={0: 0},
+    row_a = pl.multiple_of((1 - row_odd) * (tile - HALO), HALO)
+    row_b = pl.multiple_of(row_odd * (tile - HALO), HALO)
+    blocks = [(c, b) for c in range(2) for b in range(nblk)]
+    fetches, copies = [], []
+    for i, (c, b) in enumerate(blocks):
+        cols = slice(b * LANES, (b + 1) * LANES)
+        fetches.append(pltpu.make_async_copy(part_hbm.at[c, :, cols], acc.at[c, b], in_sems.at[i]))
+        copies.append(pltpu.make_async_copy(acc.at[c, b], obj_hbm.at[c, :, cols], out_sems.at[i]))
+        fetches[i].start()
+    for i, (c, b) in enumerate(blocks):
+        fetches[i].wait()
+        if b == 0:
+            acc[c, b] += jnp.where(core == 0, col_b_ref[c, inner, :], col_a_ref[c, inner, :]).astype(F32)
+        if b == nblk - 1:
+            acc[c, b] += jnp.where(core == 0, col_a_ref[c, inner, :], col_b_ref[c, inner, :]).astype(F32)
+        acc[c, b, pl.ds(row_a, HALO), :] += row_a_ref[c, b].astype(F32)
+        acc[c, b, pl.ds(row_b, HALO), :] += row_b_ref[c, b].astype(F32)
+        copies[i].start()
+    for copy in copies:
+        copy.wait()
+
+
+def finish_object(part, col_a, col_b, row_a, row_b):
+    tile = part.shape[1]
+    nblk = part.shape[2] // LANES
+    return pl.pallas_call(
+        object_kernel,
+        out_shape=pltpu.HBM(part.shape, F32),
+        in_specs=[pl.BlockSpec(memory_space=pltpu.HBM)] + [VM] * 4,
+        out_specs=pl.BlockSpec(memory_space=pltpu.HBM),
+        scratch_shapes=[
+            pltpu.VMEM((2, nblk, tile, LANES), F32),
+            pltpu.SemaphoreType.DMA((2 * nblk,)),
+            pltpu.SemaphoreType.DMA((2 * nblk,)),
+        ],
+        compiler_params=pltpu.CompilerParams(vmem_limit_bytes=8 * 1024 * 1024),
         cost_estimate=pl.CostEstimate(flops=5000000000, transcendentals=0, bytes_accessed=0),
-        compiler_params=pltpu.CompilerParams(vmem_limit_bytes=16 * 1024 * 1024),
-        name="add_cols",
-    )(part, col_a, col_b)
-
-
-def add_rows_kernel(part_ref, row_a_ref, row_b_ref, obj_ref):
-    nblk = row_a_ref.shape[1]
-    at_b = pl.program_id(0) == lax.axis_index("row") % 2
-
-    def add(row_ref):
-        for c in range(2):
-            for b in range(nblk):
-                cols = slice(b * LANES, (b + 1) * LANES)
-                obj_ref[c, :, cols] = part_ref[c, :, cols] + row_ref[c, b].astype(F32)
-
-    @pl.when(at_b)
-    def _():
-        add(row_b_ref)
-
-    @pl.when(jnp.logical_not(at_b))
-    def _():
-        add(row_a_ref)
-
-
-def add_rows(part, row_a, row_b):
-    tile, cols = part.shape[1:]
-    edge = pl.BlockSpec((2, HALO, cols), lambda i: (0, i * (tile // HALO - 1), 0))
-    return pl.pallas_call(
-        add_rows_kernel,
-        grid=(2,),
-        out_shape=jax.ShapeDtypeStruct(part.shape, F32),
-        in_specs=[edge, VM, VM],
-        out_specs=edge,
-        input_output_aliases={0: 0},
-        cost_estimate=pl.CostEstimate(flops=5000000000, transcendentals=0, bytes_accessed=0),
-        compiler_params=pltpu.CompilerParams(vmem_limit_bytes=16 * 1024 * 1024),
-        name="add_rows",
-    )(part, row_a, row_b)
+        name="finish_object",
+    )(pltpu.with_memory_space_constraint(part, pltpu.HBM), col_a, col_b, row_a, row_b)
 
 
 def probe_kernel(mine_ref, theirs_ref, out_ref):
@@ -458,19 +458,17 @@
 
 def shards(object_field, probe_modes, measured_amp, scan_positions, frame_counts):
     slots = measured_amp.shape[2]
-    to_edge_a, to_edge_b, to_row_a, to_row_b, to_col_a, to_col_b = margins(object_field)
-    edge_b = trade(to_edge_b, "row", 1)
-    edge_a = trade(to_edge_a, "row", 0)
+    to_row_a, to_row_b, to_col_a, to_col_b = margins(object_field)
+    row_b = trade(to_row_b, "row", 1)
+    row_a = trade(to_row_a, "row", 0)
     col_b = trade(to_col_b, COL, 1)
     col_a = trade(to_col_a, COL, 0)
-    row_b = trade(to_row_b, "row", 1)
-    row_a = trade(to_row_a, "row", 0)
-    to_cor_a, to_cor_b = corners(edge_a, edge_b)
+    to_cor_a, to_cor_b = corners(row_a, row_b)
     cor_b = trade(to_cor_b, COL, 1)
     cor_a = trade(to_cor_a, COL, 0)
     prepared = prepare(object_field, probe_modes, measured_amp[0, 0], fourier_tables(probe_modes.shape[-1]))
-    part, strip_a, strip_b, out_a, out_b, keep, send = run_frames(
-        frame_counts, scan_positions, (edge_a, edge_b, row_a, row_b, col_a, col_b, cor_a, cor_b), prepared
+    _, _, _, part, strip_a, strip_b, out_a, out_b, keep, send = run_frames(
+        frame_counts, scan_positions, (row_a, row_b, col_a, col_b, cor_a, cor_b), prepared
     )
     scale = 1.0 / math.sqrt(lax.axis_size("row") * lax.axis_size(COL) * slots)
     pair = (keep + trade(send, COL, 0).astype(F32)).astype(BF16)
@@ -478,13 +476,11 @@
     got_b = trade(out_b, COL, 1)
     peers = lax.all_to_all(pair, PEERS, 0, 0, tiled=True)
     rows_a, rows_b = row_margins(strip_a, strip_b, got_a, got_b)
-    part = add_cols(part, got_a, got_b)
-    peers, part = lax.optimization_barrier((peers, part))
     back_a = trade(rows_a, "row", 0)
     back_b = trade(rows_b, "row", 1)
-    total = (jnp.sum(peers.astype(F32), axis=0) * scale).astype(BF16)
-    mine = lax.all_to_all(jnp.broadcast_to(total[None], send.shape), PEERS, 0, 0, tiled=True)
-    obj = add_rows(part, back_a, back_b)
+    peers, rows_a, rows_b = lax.optimization_barrier((peers, rows_a, rows_b))
+    mine = lax.all_to_all(peer_sum(peers, scale), PEERS, 0, 0, tiled=True)
+    obj = finish_object(part, got_a, got_b, back_a, back_b)
     mine, obj = lax.optimization_barrier((mine, obj))
     return obj, finish_probe(mine, trade(mine, COL, 0), probe_modes.shape)
 

time: 90.4 us -> 86 us (0.951)
  starting transfers between devices: 51.6 us -> 47 us
  other arithmetic: 1.89 us -> 0.76 us
  waiting for transfers between devices: 15.8 us -> 16.8 us
    ppermute x14 -> x12, starting transfers between devices: 33.3 us -> 24.3 us  [trade(): return lax.ppermute(value, axis, [(i, j) for i, j in pairs if 0 <= j < n])]
    all_to_all x1, starting transfers between devices: 11.2 us -> 16.5 us  [shards(): peers = lax.all_to_all(pair, PEERS, 0, 0, tiled=True)]
    all_to_all x1, waiting for transfers between devices: 4.06 us -> 6.15 us  [shards(): peers = lax.all_to_all(pair, PEERS, 0, 0, tiled=True)]
    pallas_call x1, Pallas kernels: 8.49 us -> 9.73 us  [run_frames(): pl.pallas_call(frames_kernel, out_shape=(pltpu.VMEM(ext.shape, F32), pltp...]
    convert_element_type x1, other arithmetic: 1.81 us -> 0.76 us  [shards(): pair = (keep + trade(send, COL, 0).astype(F32)).astype(BF16)]
    pallas_call x3, Pallas kernels: 5.56 us -> 4.51 us  [the longest x1 2.47 us: finish_object(): pl.pallas_call(object_kernel, out_shape=pltpu.HBM(part.shape, F32), in_sp...]
    all_to_all x1, starting transfers between devices: 7.13 us -> 6.14 us  [shards(): mine = lax.all_to_all(peer_sum(peers, scale), PEERS, 0, 0, tiled=True)]
    ppermute x14 -> x12, waiting for transfers between devices: 4.6 us -> 3.95 us  [trade(): return lax.ppermute(value, axis, [(i, j) for i, j in pairs if 0 <= j < n])]
  transfers between devices with their start and end apart: 16 -> 14, of which waited for: 4 -> 5; matrix products, arithmetic and copies ran while one was open for 3% -> 1% of each run, Pallas kernels for 9% -> 8%
where the time goes in v4:
time: 86 us; the launch traced here: 84.9 us
  starting transfers between devices  47 us (55%)
  Pallas kernels  18.9 us (22%)
  waiting for transfers between devices  16.8 us (20%)
  between operations  1.46 us (2%)
    ppermute x12, starting transfers between devices, trade(): return lax.ppermute(value, axis, [(i, j) for i, j in pairs if 0 <= j < n])  24.3 us
    all_to_all x1, starting transfers between devices, shards(): peers = lax.all_to_all(pair, PEERS, 0, 0, tiled=True)  16.5 us
    pallas_call x1, Pallas kernels, run_frames(): pl.pallas_call(frames_kernel, out_shape=(pltpu.VMEM(ext.shape, F32), pltp...  9.73 us
    all_to_all x1, waiting for transfers between devices, shards(): mine = lax.all_to_all(peer_sum(peers, scale), PEERS, 0, 0, tiled=True)  6.73 us
    all_to_all x1, waiting for transfers between devices, shards(): peers = lax.all_to_all(pair, PEERS, 0, 0, tiled=True)  6.15 us
    all_to_all x1, starting transfers between devices, shards(): mine = lax.all_to_all(peer_sum(peers, scale), PEERS, 0, 0, tiled=True)  6.14 us
    ppermute x12, waiting for transfers between devices, trade(): return lax.ppermute(value, axis, [(i, j) for i, j in pairs if 0 <= j < n])  3.95 us
    pallas_call x1, Pallas kernels, finish_object(): pl.pallas_call(object_kernel, out_shape=pltpu.HBM(part.shape, F32), in_sp...  2.47 us
  transfers between devices with their start and end apart: 14, of which 5 were waited for; matrix products, arithmetic and copies ran while one was open for 1% of the time, Pallas kernels for 8%

profile of v4, /device:TPU:1, one launch (start us, length us, event | category | flops | bytes accessed | tf_op | source)
XLA Modules:
  0.0 84.9 jit_solution(1553519270124516552)
XLA Ops:
  0.6 1.2 %margins.1 = (bf16[2,128,512]{2,1,0:T(8,128)(2,1)S(1)}, bf16[2,128,512]{2,1,0:T(8,128)(2,1)S(1)}, bf16[2,512,128]{2,1,0:T(8,128)(2,1)S(1)}, bf16[2,512,128]{2,1,0:T(8,128)(2,1)S(1)}) custom-call(bf16[2,512,512]{2,1,0:T(8,128)(2,1)} %mid_hbm.1), custom_call_target="tpu_custom_call" | custom-call | tf_op jit(solution)/shard_map/margins/pallas_call | solution.py:61
  1.9 2.5 %collective-permute-start = (bf16[2,128,512]{2,1,0:T(8,128)(2,1)S(1)}, bf16[2,128,512]{2,1,0:T(8,128)(2,1)S(1)}, u32[]{:S(2)}, u32[]{:S(2)}) collective-permute-start(bf16[2,128,512]{2,1,0:T(8,128)(2,1)S(1)} %get-tuple-element.26), channel_id=1, source_target_pairs={{0,16},{16,0},{32,48},{48,32},{64,80},{80,64},{96,112},{112,96},{1... | collective-permute-start | bytes 786440 | tf_op jit(solution)/shard_map/ppermute | solution.py:456
  4.4 0.7 collective-permute-start.1
  5.1 1.0 %collective-permute-start.2 = (bf16[2,512,128]{2,1,0:T(8,128)(2,1)S(1)}, bf16[2,512,128]{2,1,0:T(8,128)(2,1)S(1)}, u32[]{:S(2)}, u32[]{:S(2)}) collective-permute-start(bf16[2,512,128]{2,1,0:T(8,128)(2,1)S(1)} %get-tuple-element.28), channel_id=1, source_target_pairs={{0,1},{1,0},{2,3},{3,2},{4,5},{5,4},{6,7},{7,6},{8,9},{9,8},{10,11... | collective-permute-start | bytes 786440 | tf_op jit(solution)/shard_map/ppermute | solution.py:456
  6.1 3.0 %collective-permute-start.3 = (bf16[2,512,128]{2,1,0:T(8,128)(2,1)S(1)}, bf16[2,512,128]{2,1,0:T(8,128)(2,1)S(1)}, u32[]{:S(2)}, u32[]{:S(2)}) collective-permute-start(bf16[2,512,128]{2,1,0:T(8,128)(2,1)S(1)} %get-tuple-element.29), channel_id=1, source_target_pairs={{1,2},{2,1},{3,4},{4,3},{5,6},{6,5},{7,8},{8,7},{9,10},{10,9},{11,... | collective-permute-start | bytes 786440 | tf_op jit(solution)/shard_map/ppermute | solution.py:456
  9.2 1.3 %collective-permute-done.row_a.row_a_ref = bf16[2,128,512]{2,1,0:T(8,128)(2,1)S(1)} collective-permute-done((bf16[2,128,512]{2,1,0:T(8,128)(2,1)S(1)}, bf16[2,128,512]{2,1,0:T(8,128)(2,1)S(1)}, u32[]{:S(2)}, u32[]{:S(2)}) %collective-permute-start) | collective-permute-done | bytes 262176 | tf_op jit(solution)/shard_map/ppermute | solution.py:456
  10.5 1.3 %collective-permute-start.4 = (bf16[4,128,128]{2,1,0:T(8,128)(2,1)S(1)}, bf16[4,128,128]{2,1,0:T(8,128)(2,1)S(1)}, u32[]{:S(2)}, u32[]{:S(2)}) collective-permute-start(bf16[4,128,128]{2,1,0:T(8,128)(2,1)S(1)} %get-tuple-element.30), channel_id=1, source_target_pairs={{0,1},{1,0},{2,3},{3,2},{4,5},{5,4},{6,7},{7,6},{8,9},{9,8},{10,11... | collective-permute-start | bytes 393224 | tf_op jit(solution)/shard_map/ppermute | solution.py:456
  11.8 3.0 %collective-permute-start.5 = (bf16[4,128,128]{2,1,0:T(8,128)(2,1)S(1)}, bf16[4,128,128]{2,1,0:T(8,128)(2,1)S(1)}, u32[]{:S(2)}, u32[]{:S(2)}) collective-permute-start(bf16[4,128,128]{2,1,0:T(8,128)(2,1)S(1)} %get-tuple-element.31), channel_id=1, source_target_pairs={{1,2},{2,1},{3,4},{4,3},{5,6},{6,5},{7,8},{8,7},{9,10},{10,9},{11,... | collective-permute-start | bytes 393224 | tf_op jit(solution)/shard_map/ppermute | solution.py:456
  14.9 2.2 %prepare.1 = (f32[2,6,768,128]{3,2,1,0:T(8,128)S(1)}, f32[2,6,768,128]{3,2,1,0:T(8,128)S(1)}, f32[2,2,256,256]{3,2,1,0:T(8,128)S(1)}, f32[2,2,256,256]{3,2,1,0:T...) custom-call(bf16[2,512,512]{2,1,0:T(8,128)(2,1)} %mid_hbm.1, ...), custom_call_target="tpu_custom_call" | custom-call | flops 5000000000 | tf_op jit(solution)/shard_map/prepare/pallas_call | solution.py:266
  17.8 1.5 %collective-permute-done.5.cor_b_ref = bf16[4,128,128]{2,1,0:T(8,128)(2,1)S(1)} collective-permute-done((bf16[4,128,128]{2,1,0:T(8,128)(2,1)S(1)}, bf16[4,128,128]{2,1,0:T(8,128)(2,1)S(1)}, u32[]{:S(2)}, u32[]{:S(2)}) %collective-permute-start.5) | collective-permute-done | bytes 131104 | tf_op jit(solution)/shard_map/ppermute | solution.py:456
  19.3 9.7 %frames.1 = (f32[2,6,768,128]{3,2,1,0:T(8,128)S(1)}, f32[2,6,768,128]{3,2,1,0:T(8,128)S(1)}, f32[2,2,256,256]{3,2,1,0:T(8,128)S(1)}, f32[2,512,512]{2,1,0:T(8,12...) custom-call(s32[1,1]{1,0:T(1,128)S(6)} %copy.15.count_ref, ...), custom_call_target="tpu_custom_call", output_to_operand_aliasing={{0}: (8, {}), {1}: (9, {}), {2}: (10, {})} | custom-call | tf_op jit(solution)/shard_map/frames/pallas_call | solution.py:288
  29.6 8.0 %collective-permute-start.8 = (bf16[2,768,128]{2,1,0:T(8,128)(2,1)}, bf16[2,768,128]{2,1,0:T(8,128)(2,1)S(1)}, u32[]{:S(2)}, u32[]{:S(2)}) collective-permute-start(bf16[2,768,128]{2,1,0:T(8,128)(2,1)} %get-tuple-element.43), channel_id=1, source_target_pairs={{1,2},{2,1},{3,4},{4,3},{5,6},{6,5},{7,8},{8,7},{9,10},{10,9},{11,... | collective-permute-start | bytes 1179656 | tf_op jit(solution)/shard_map/ppermute | solution.py:456
  37.6 0.8 add_convert_fusion
  38.4 16.5 %all-to-all-start = ((bf16[64,16,128]{2,1,0:T(8,128)(2,1)}), bf16[64,16,128]{2,1,0:T(8,128)(2,1)S(1)}, u32[]{:S(2)}, u32[]{:S(2)}) async-start(bf16[64,16,128]{2,1,0:T(8,128)(2,1)} %add_convert_fusion), calls=%async_computation | async-start | bytes 524288 | tf_op jit(solution)/shard_map/all_to_all | solution.py:477
  54.9 1.3 %row_margins.1 = (bf16[2,4,128,128]{3,2,1,0:T(8,128)(2,1)S(1)}, bf16[2,4,128,128]{3,2,1,0:T(8,128)(2,1)S(1)}) custom-call(f32[2,4,128,128]{3,2,1,0:T(8,128)} %get-tuple-element.40.strip_a_hbm, f32[2,4,128,128]{3,2,1,0:T(8,128)} %get-tuple-element.41.strip_b_hbm, bf16[2,768,128]{2,1,0:T(8,128)(2,1)S(1)} %collective-permute-done.7.got_a_ref.col_a_ref, ...), custom_call_target="tpu_custom_call" | custom-call | flops 5000000000 | tf_op jit(solution)/shard_map/row_margins/pallas_call | solution.py:352
  56.2 1.1 %collective-permute-start.9 = (bf16[2,4,128,128]{3,2,1,0:T(8,128)(2,1)S(1)}, bf16[2,4,128,128]{3,2,1,0:T(8,128)(2,1)S(1)}, u32[]{:S(2)}, u32[]{:S(2)}) collective-permute-start(bf16[2,4,128,128]{3,2,1,0:T(8,128)(2,1)S(1)} %get-tuple-element.44), channel_id=1, source_target_pairs={{0,16},{16,0},{32,48},{48,32},{64,80},{80,64},{96,112},{112,96},{1... | collective-permute-start | bytes 786440 | tf_op jit(solution)/shard_map/ppermute | solution.py:456
  58.0 6.1 %all-to-all-done.got_ref = bf16[64,16,128]{2,1,0:T(8,128)(2,1)S(1)} async-done(((bf16[64,16,128]{2,1,0:T(8,128)(2,1)}), bf16[64,16,128]{2,1,0:T(8,128)(2,1)S(1)}, u32[]{:S(2)}, u32[]{:S(2)}) %all-to-all-start) | async-done | bytes 262176 | tf_op jit(solution)/shard_map/all_to_all | solution.py:477
  64.2 0.8 peer_sum.1
  64.9 6.1 %all-to-all-start.1 = ((bf16[64,16,128]{2,1,0:T(8,128)(2,1)}), bf16[64,16,128]{2,1,0:T(8,128)(2,1)S(1)}, u32[]{:S(2)}, u32[]{:S(2)}) async-start(bf16[64,16,128]{2,1,0:T(8,128)(2,1)} %peer_sum.1), calls=%async_computation.1 | async-start | bytes 524288 | tf_op jit(solution)/shard_map/all_to_all | solution.py:482
  71.1 2.5 %finish_object.1 = f32[2,512,512]{2,1,0:T(8,128)} custom-call(f32[2,512,512]{2,1,0:T(8,128)} %get-tuple-element.47.part_hbm, bf16[2,768,128]{2,1,0:T(8,128)(2,1)S(1)} %collective-permute-done.7.got_a_ref.col_a_ref, bf16[2,768,128]{2,1,0:T(8,128)(2,1)S(1)} %collective-permute-done.8.got_b_ref.col_b_ref, ...), custom_call_target="tpu_custom_call" | custom-call | flops 5000000000 | tf_op jit(solution)/shard_map/finish_object/pallas_call | solution.py:415
  73.6 6.7 %all-to-all-done.1.mine_ref = bf16[64,16,128]{2,1,0:T(8,128)(2,1)S(1)} async-done(((bf16[64,16,128]{2,1,0:T(8,128)(2,1)}), bf16[64,16,128]{2,1,0:T(8,128)(2,1)S(1)}, u32[]{:S(2)}, u32[]{:S(2)}) %all-to-all-start.1) | async-done | bytes 262176 | tf_op jit(solution)/shard_map/all_to_all | solution.py:482
  80.3 2.4 %collective-permute-start.11 = (bf16[64,16,128]{2,1,0:T(8,128)(2,1)S(1)}, bf16[64,16,128]{2,1,0:T(8,128)(2,1)S(1)}, u32[]{:S(2)}, u32[]{:S(2)}) collective-permute-start(bf16[64,16,128]{2,1,0:T(8,128)(2,1)S(1)} %all-to-all-done.1.mine_ref), channel_id=1, source_target_pairs={{0,1},{1,0},{2,3},{3,2},{4,5},{5,4},{6,7},{7,6},{8,9},{9,8},{10,11... | collective-permute-start | bytes 786440 | tf_op jit(solution)/shard_map/ppermute | solution.py:456
  82.7 1.2 %collective-permute-done.11.theirs_ref = bf16[64,16,128]{2,1,0:T(8,128)(2,1)S(1)} collective-permute-done((bf16[64,16,128]{2,1,0:T(8,128)(2,1)S(1)}, bf16[64,16,128]{2,1,0:T(8,128)(2,1)S(1)}, u32[]{:S(2)}, u32[]{:S(2)}) %collective-permute-start.11) | collective-permute-done | bytes 262176 | tf_op jit(solution)/shard_map/ppermute | solution.py:456
  83.9 1.0 %finish_probe.1 = f32[2,2,256,256]{3,2,1,0:T(8,128)} custom-call(bf16[64,16,128]{2,1,0:T(8,128)(2,1)S(1)} %all-to-all-done.1.mine_ref, bf16[64,16,128]{2,1,0:T(8,128)(2,1)S(1)} %collective-permute-done.11.theirs_ref), custom_call_target="tpu_custom_call" | custom-call | tf_op jit(solution)/shard_map/finish_probe/pallas_call | solution.py:443
  (15 shorter events, 1.3 us)
Async XLA Ops:
  1.9 8.6 %collective-permute-start = (bf16[2,128,512]{2,1,0:T(8,128)(2,1)S(1)}, bf16[2,128,512]{2,1,0:T(8,128)(2,1)S(1)}, u32[]{:S(2)}, u32[]{:S(2)}) collective-permute-start(bf16[2,128,512]{2,1,0:T(8,128)(2,1)S(1)} %get-tuple-element.26), channel_id=1, source_target_pairs={{0,16},{16,0},{32,48},{48,32},{64,80},{80,64},{96,112},{112,96},{1... | collective-permute-start | bytes 786440 | tf_op jit(solution)/shard_map/ppermute | solution.py:456
  4.4 6.0 %collective-permute-start.1 = (bf16[2,128,512]{2,1,0:T(8,128)(2,1)S(1)}, bf16[2,128,512]{2,1,0:T(8,128)(2,1)S(1)}, u32[]{:S(2)}, u32[]{:S(2)}) collective-permute-start(bf16[2,128,512]{2,1,0:T(8,128)(2,1)S(1)} %get-tuple-element.27), channel_id=1, source_target_pairs={{16,32},{32,16},{48,64},{64,48},{80,96},{96,80},{17,33},{33,17},{4... | collective-permute-start | bytes 786440 | tf_op jit(solution)/shard_map/ppermute | solution.py:456
  5.1 12.6 %collective-permute-start.2 = (bf16[2,512,128]{2,1,0:T(8,128)(2,1)S(1)}, bf16[2,512,128]{2,1,0:T(8,128)(2,1)S(1)}, u32[]{:S(2)}, u32[]{:S(2)}) collective-permute-start(bf16[2,512,128]{2,1,0:T(8,128)(2,1)S(1)} %get-tuple-element.28), channel_id=1, source_target_pairs={{0,1},{1,0},{2,3},{3,2},{4,5},{5,4},{6,7},{7,6},{8,9},{9,8},{10,11... | collective-permute-start | bytes 786440 | tf_op jit(solution)/shard_map/ppermute | solution.py:456
  6.1 11.6 %collective-permute-start.3 = (bf16[2,512,128]{2,1,0:T(8,128)(2,1)S(1)}, bf16[2,512,128]{2,1,0:T(8,128)(2,1)S(1)}, u32[]{:S(2)}, u32[]{:S(2)}) collective-permute-start(bf16[2,512,128]{2,1,0:T(8,128)(2,1)S(1)} %get-tuple-element.29), channel_id=1, source_target_pairs={{1,2},{2,1},{3,4},{4,3},{5,6},{6,5},{7,8},{8,7},{9,10},{10,9},{11,... | collective-permute-start | bytes 786440 | tf_op jit(solution)/shard_map/ppermute | solution.py:456
  10.5 7.3 %collective-permute-start.4 = (bf16[4,128,128]{2,1,0:T(8,128)(2,1)S(1)}, bf16[4,128,128]{2,1,0:T(8,128)(2,1)S(1)}, u32[]{:S(2)}, u32[]{:S(2)}) collective-permute-start(bf16[4,128,128]{2,1,0:T(8,128)(2,1)S(1)} %get-tuple-element.30), channel_id=1, source_target_pairs={{0,1},{1,0},{2,3},{3,2},{4,5},{5,4},{6,7},{7,6},{8,9},{9,8},{10,11... | collective-permute-start | bytes 393224 | tf_op jit(solution)/shard_map/ppermute | solution.py:456
  11.8 7.4 %collective-permute-start.5 = (bf16[4,128,128]{2,1,0:T(8,128)(2,1)S(1)}, bf16[4,128,128]{2,1,0:T(8,128)(2,1)S(1)}, u32[]{:S(2)}, u32[]{:S(2)}) collective-permute-start(bf16[4,128,128]{2,1,0:T(8,128)(2,1)S(1)} %get-tuple-element.31), channel_id=1, source_target_pairs={{1,2},{2,1},{3,4},{4,3},{5,6},{6,5},{7,8},{8,7},{9,10},{10,9},{11,... | collective-permute-start | bytes 393224 | tf_op jit(solution)/shard_map/ppermute | solution.py:456
  14.9 4.4 %copy-start = (s32[1,1,2,8]{3,2,1,0:T(2,128)S(1)}, s32[1,1,2,8]{3,2,1,0:T(2,128)}, u32[]{:S(2)}) copy-start(s32[1,1,2,8]{3,2,1,0:T(2,128)} %pos_ref.1) | copy-start | bytes 196
  29.0 8.6 %collective-permute-start.6 = (bf16[64,16,128]{2,1,0:T(8,128)(2,1)S(1)}, bf16[64,16,128]{2,1,0:T(8,128)(2,1)S(1)}, u32[]{:S(2)}, u32[]{:S(2)}) collective-permute-start(bf16[64,16,128]{2,1,0:T(8,128)(2,1)S(1)} %get-tuple-element.39), channel_id=1, source_target_pairs={{0,1},{1,0},{2,3},{3,2},{4,5},{5,4},{6,7},{7,6},{8,9},{9,8},{10,11... | collective-permute-start | bytes 786440 | tf_op jit(solution)/shard_map/ppermute | solution.py:456
  29.1 25.8 %collective-permute-start.7 = (bf16[2,768,128]{2,1,0:T(8,128)(2,1)}, bf16[2,768,128]{2,1,0:T(8,128)(2,1)S(1)}, u32[]{:S(2)}, u32[]{:S(2)}) collective-permute-start(bf16[2,768,128]{2,1,0:T(8,128)(2,1)} %get-tuple-element.42), channel_id=1, source_target_pairs={{0,1},{1,0},{2,3},{3,2},{4,5},{5,4},{6,7},{7,6},{8,9},{9,8},{10,11... | collective-permute-start | bytes 1179656 | tf_op jit(solution)/shard_map/ppermute | solution.py:456
  29.6 25.3 %collective-permute-start.8 = (bf16[2,768,128]{2,1,0:T(8,128)(2,1)}, bf16[2,768,128]{2,1,0:T(8,128)(2,1)S(1)}, u32[]{:S(2)}, u32[]{:S(2)}) collective-permute-start(bf16[2,768,128]{2,1,0:T(8,128)(2,1)} %get-tuple-element.43), channel_id=1, source_target_pairs={{1,2},{2,1},{3,4},{4,3},{5,6},{6,5},{7,8},{8,7},{9,10},{10,9},{11,... | collective-permute-start | bytes 1179656 | tf_op jit(solution)/shard_map/ppermute | solution.py:456
  38.4 25.8 %all-to-all-start = ((bf16[64,16,128]{2,1,0:T(8,128)(2,1)}), bf16[64,16,128]{2,1,0:T(8,128)(2,1)S(1)}, u32[]{:S(2)}, u32[]{:S(2)}) async-start(bf16[64,16,128]{2,1,0:T(8,128)(2,1)} %add_convert_fusion), calls=%async_computation | async-start | bytes 524288 | tf_op jit(solution)/shard_map/all_to_all | solution.py:477
  56.2 14.9 %collective-permute-start.9 = (bf16[2,4,128,128]{3,2,1,0:T(8,128)(2,1)S(1)}, bf16[2,4,128,128]{3,2,1,0:T(8,128)(2,1)S(1)}, u32[]{:S(2)}, u32[]{:S(2)}) collective-permute-start(bf16[2,4,128,128]{3,2,1,0:T(8,128)(2,1)S(1)} %get-tuple-element.44), channel_id=1, source_target_pairs={{0,16},{16,0},{32,48},{48,32},{64,80},{80,64},{96,112},{112,96},{1... | collective-permute-start | bytes 786440 | tf_op jit(solution)/shard_map/ppermute | solution.py:456
  57.3 13.8 %collective-permute-start.10 = (bf16[2,4,128,128]{3,2,1,0:T(8,128)(2,1)S(1)}, bf16[2,4,128,128]{3,2,1,0:T(8,128)(2,1)S(1)}, u32[]{:S(2)}, u32[]{:S(2)}) collective-permute-start(bf16[2,4,128,128]{3,2,1,0:T(8,128)(2,1)S(1)} %get-tuple-element.45), channel_id=1, source_target_pairs={{16,32},{32,16},{48,64},{64,48},{80,96},{96,80},{17,33},{33,17},{4... | collective-permute-start | bytes 786440 | tf_op jit(solution)/shard_map/ppermute | solution.py:456
  64.9 15.4 %all-to-all-start.1 = ((bf16[64,16,128]{2,1,0:T(8,128)(2,1)}), bf16[64,16,128]{2,1,0:T(8,128)(2,1)S(1)}, u32[]{:S(2)}, u32[]{:S(2)}) async-start(bf16[64,16,128]{2,1,0:T(8,128)(2,1)} %peer_sum.1), calls=%async_computation.1 | async-start | bytes 524288 | tf_op jit(solution)/shard_map/all_to_all | solution.py:482
  80.3 3.5 %collective-permute-start.11 = (bf16[64,16,128]{2,1,0:T(8,128)(2,1)S(1)}, bf16[64,16,128]{2,1,0:T(8,128)(2,1)S(1)}, u32[]{:S(2)}, u32[]{:S(2)}) collective-permute-start(bf16[64,16,128]{2,1,0:T(8,128)(2,1)S(1)} %all-to-all-done.1.mine_ref), channel_id=1, source_target_pairs={{0,1},{1,0},{2,3},{3,2},{4,5},{5,4},{6,7},{7,6},{8,9},{9,8},{10,11... | collective-permute-start | bytes 786440 | tf_op jit(solution)/shard_map/ppermute | solution.py:456

commit v5 on v4

--- a/solution.py
+++ b/solution.py
@@ -31,6 +31,16 @@
 
 def place():
     return lax.axis_index("row") % 2, lax.axis_index("core")
+
+
+def joined():
+    row, n_row = lax.axis_index("row"), lax.axis_size("row")
+    col, n_col = lax.axis_index(COL), lax.axis_size(COL)
+    return (row > 0) & (row < n_row - 1), (col > 0) & (col < n_col - 1)
+
+
+def live(cond, value):
+    return jnp.where(cond, value, jnp.zeros_like(value))
 
 
 def matmul(a, b):
@@ -114,6 +124,7 @@
     nblk = tile // LANES
     count = count_ref[0, 0]
     row_odd, core = place()
+    row_in, col_in = joined()
     row_a = pl.multiple_of((1 - row_odd) * (HALO + tile), HALO)
     row_b = pl.multiple_of(row_odd * (HALO + tile), HALO)
     col_a = (1 - core) * (nblk + 1)
@@ -121,12 +132,15 @@
     lt_ref, rt_ref = tables_ref.at[0], tables_ref.at[1]
     for c in range(2):
         for b in range(nblk):
-            for at, ref in ((row_a, row_a_ref), (row_b, row_b_ref)):
-                ext[c, b + 1, pl.ds(at, HALO), :] = ref[c, :, b * LANES : (b + 1) * LANES].astype(F32)
-        for col, own_ref, cor_ref in ((col_a, col_a_ref, cor_a_ref), (col_b, col_b_ref, cor_b_ref)):
-            ext[c, col, pl.ds(row_a, HALO), :] = cor_ref[c].astype(F32)
-            ext[c, col, HALO : HALO + tile, :] = own_ref[c].astype(F32)
-            ext[c, col, pl.ds(row_b, HALO), :] = cor_ref[2 + c].astype(F32)
+            cols = slice(b * LANES, (b + 1) * LANES)
+            ext[c, b + 1, pl.ds(row_a, HALO), :] = row_a_ref[c, :, cols].astype(F32)
+            ext[c, b + 1, pl.ds(row_b, HALO), :] = live(row_in, row_b_ref[c, :, cols].astype(F32))
+        ext[c, col_a, pl.ds(row_a, HALO), :] = cor_a_ref[c].astype(F32)
+        ext[c, col_a, HALO : HALO + tile, :] = col_a_ref[c].astype(F32)
+        ext[c, col_a, pl.ds(row_b, HALO), :] = live(row_in, cor_a_ref[2 + c].astype(F32))
+        ext[c, col_b, pl.ds(row_a, HALO), :] = live(col_in, cor_b_ref[c].astype(F32))
+        ext[c, col_b, HALO : HALO + tile, :] = live(col_in, col_b_ref[c].astype(F32))
+        ext[c, col_b, pl.ds(row_b, HALO), :] = live(row_in & col_in, cor_b_ref[2 + c].astype(F32))
     lane = lax.broadcasted_iota(jnp.int32, (side, LANES), 1)
 
     def gather(s, slot):
@@ -322,6 +336,7 @@
 ):
     nblk, rows = strip_a_ref.shape[1], got_a_ref.shape[1]
     row_odd, core = place()
+    _, col_in = joined()
     copy_a = pltpu.make_async_copy(strip_a_hbm, strip_a_ref, sem_a)
     copy_b = pltpu.make_async_copy(strip_b_hbm, strip_b_ref, sem_b)
     copy_a.start()
@@ -333,8 +348,10 @@
         for c in range(2):
             for b in range(nblk):
                 out_ref[c, b] = own_ref[c, b].astype(BF16)
-            for got_ref, blk in ((got_a_ref, (1 - core) * (nblk - 1)), (got_b_ref, core * (nblk - 1))):
-                out_ref[c, blk] = (own_ref[c, blk] + got_ref[c, start : start + HALO, :].astype(F32)).astype(BF16)
+            at = slice(start, start + HALO)
+            blk_a, blk_b = (1 - core) * (nblk - 1), core * (nblk - 1)
+            out_ref[c, blk_a] = (own_ref[c, blk_a] + got_a_ref[c, at, :].astype(F32)).astype(BF16)
+            out_ref[c, blk_b] = (own_ref[c, blk_b] + live(col_in, got_b_ref[c, at, :].astype(F32))).astype(BF16)
 
     @pl.when(row_odd == 0)
     def _():
@@ -386,6 +403,7 @@
 def object_kernel(part_hbm, col_a_ref, col_b_ref, row_a_ref, row_b_ref, obj_hbm, acc, in_sems, out_sems):
     nblk, tile = acc.shape[1], acc.shape[2]
     row_odd, core = place()
+    row_in, col_in = joined()
     inner = slice(HALO, HALO + tile)
     row_a = pl.multiple_of((1 - row_odd) * (tile - HALO), HALO)
     row_b = pl.multiple_of(row_odd * (tile - HALO), HALO)
@@ -399,11 +417,13 @@
     for i, (c, b) in enumerate(blocks):
         fetches[i].wait()
         if b == 0:
-            acc[c, b] += jnp.where(core == 0, col_b_ref[c, inner, :], col_a_ref[c, inner, :]).astype(F32)
+            got_a, got_b = col_a_ref[c, inner, :].astype(F32), live(col_in, col_b_ref[c, inner, :].astype(F32))
+            acc[c, b] += jnp.where(core == 0, got_b, got_a)
         if b == nblk - 1:
-            acc[c, b] += jnp.where(core == 0, col_a_ref[c, inner, :], col_b_ref[c, inner, :]).astype(F32)
+            got_a, got_b = col_a_ref[c, inner, :].astype(F32), live(col_in, col_b_ref[c, inner, :].astype(F32))
+            acc[c, b] += jnp.where(core == 0, got_a, got_b)
         acc[c, b, pl.ds(row_a, HALO), :] += row_a_ref[c, b].astype(F32)
-        acc[c, b, pl.ds(row_b, HALO), :] += row_b_ref[c, b].astype(F32)
+        acc[c, b, pl.ds(row_b, HALO), :] += live(row_in, row_b_ref[c, b].astype(F32))
         copies[i].start()
     for copy in copies:
         copy.wait()
@@ -452,8 +472,7 @@
 
 def trade(value, axis, phase):
     n = lax.axis_size(axis)
-    pairs = [(i, ((i + phase) ^ 1) - phase) for i in range(n)]
-    return lax.ppermute(value, axis, [(i, j) for i, j in pairs if 0 <= j < n])
+    return lax.ppermute(value, axis, [(i, (((i + phase) ^ 1) - phase) % n) for i in range(n)])
 
 
 def shards(object_field, probe_modes, measured_amp, scan_positions, frame_counts):

time: 86 us -> 81.9 us (0.952); the launches traced: 84.9 us -> 82.3 us
  starting transfers between devices: 47 us -> 43.7 us
  waiting for transfers between devices: 16.8 us -> 19.1 us
  Pallas kernels: 18.9 us -> 17.3 us
    all_to_all x1, starting transfers between devices: 16.5 us -> 7.78 us  [shards(): peers = lax.all_to_all(pair, PEERS, 0, 0, tiled=True)]
    ppermute x12, starting transfers between devices: 24.3 us -> 31 us  [trade(): lax.ppermute(value, axis, [(i, ((i + phase ^ 1) - phase) % n) for i in ra...]
    ppermute x12, waiting for transfers between devices: 3.95 us -> 9.69 us  [trade(): lax.ppermute(value, axis, [(i, ((i + phase ^ 1) - phase) % n) for i in ra...]
    all_to_all x1, waiting for transfers between devices: 6.15 us -> 2.72 us  [shards(): peers = lax.all_to_all(pair, PEERS, 0, 0, tiled=True)]
    pallas_call x1, Pallas kernels: 9.73 us -> 8.2 us  [run_frames(): pl.pallas_call(frames_kernel, out_shape=(pltpu.VMEM(ext.shape, F32), pltp...]
    all_to_all x1, starting transfers between devices: 6.14 us -> 4.88 us  [shards(): mine = lax.all_to_all(peer_sum(peers, scale), PEERS, 0, 0, tiled=True)]
  transfers between devices with their start and end apart: 14 -> 14, of which waited for: 5 -> 7; matrix products, arithmetic and copies ran while one was open for 1% -> 1% of each run, Pallas kernels for 8% -> 8%
where the time goes in v5:
time: 81.9 us; the launch traced here: 82.3 us
  starting transfers between devices  43.7 us (53%)
  waiting for transfers between devices  19.1 us (23%)
  Pallas kernels  17.3 us (21%)
  between operations  1.4 us (2%)
    ppermute x12, starting transfers between devices, trade(): lax.ppermute(value, axis, [(i, ((i + phase ^ 1) - phase) % n) for i in ra...  31 us
    ppermute x12, waiting for transfers between devices, trade(): lax.ppermute(value, axis, [(i, ((i + phase ^ 1) - phase) % n) for i in ra...  9.69 us
    pallas_call x1, Pallas kernels, run_frames(): pl.pallas_call(frames_kernel, out_shape=(pltpu.VMEM(ext.shape, F32), pltp...  8.2 us
    all_to_all x1, starting transfers between devices, shards(): peers = lax.all_to_all(pair, PEERS, 0, 0, tiled=True)  7.78 us
    all_to_all x1, waiting for transfers between devices, shards(): mine = lax.all_to_all(peer_sum(peers, scale), PEERS, 0, 0, tiled=True)  6.7 us
    all_to_all x1, starting transfers between devices, shards(): mine = lax.all_to_all(peer_sum(peers, scale), PEERS, 0, 0, tiled=True)  4.88 us
    all_to_all x1, waiting for transfers between devices, shards(): peers = lax.all_to_all(pair, PEERS, 0, 0, tiled=True)  2.72 us
    pallas_call x1, Pallas kernels, finish_object(): pl.pallas_call(object_kernel, out_shape=pltpu.HBM(part.shape, F32), in_sp...  2.48 us
  transfers between devices with their start and end apart: 14, of which 7 were waited for; matrix products, arithmetic and copies ran while one was open for 1% of the time, Pallas kernels for 8%

profile of v5, /device:TPU:1, one launch (start us, length us, event | category | flops | bytes accessed | tf_op | source)
XLA Modules:
  0.0 82.3 jit_solution(9151468645681659487)
XLA Ops:
  0.6 1.2 %margins.1 = (bf16[2,128,512]{2,1,0:T(8,128)(2,1)S(1)}, bf16[2,128,512]{2,1,0:T(8,128)(2,1)S(1)}, bf16[2,512,128]{2,1,0:T(8,128)(2,1)S(1)}, bf16[2,512,128]{2,1,0:T(8,128)(2,1)S(1)}) custom-call(bf16[2,512,512]{2,1,0:T(8,128)(2,1)} %mid_hbm.1), custom_call_target="tpu_custom_call" | custom-call | tf_op jit(solution)/shard_map/margins/pallas_call | solution.py:71
  1.9 2.5 %collective-permute-start = (bf16[2,128,512]{2,1,0:T(8,128)(2,1)S(1)}, bf16[2,128,512]{2,1,0:T(8,128)(2,1)S(1)}, u32[]{:S(2)}, u32[]{:S(2)}) collective-permute-start(bf16[2,128,512]{2,1,0:T(8,128)(2,1)S(1)} %get-tuple-element.26), channel_id=1, source_target_pairs={{0,16},{16,0},{32,48},{48,32},{64,80},{80,64},{96,112},{112,96},{1... | collective-permute-start | bytes 786440 | tf_op jit(solution)/shard_map/ppermute | solution.py:475
  4.4 4.7 %collective-permute-start.1 = (bf16[2,128,512]{2,1,0:T(8,128)(2,1)S(1)}, bf16[2,128,512]{2,1,0:T(8,128)(2,1)S(1)}, u32[]{:S(2)}, u32[]{:S(2)}) collective-permute-start(bf16[2,128,512]{2,1,0:T(8,128)(2,1)S(1)} %get-tuple-element.27), channel_id=1, source_target_pairs={{0,112},{16,32},{32,16},{48,64},{64,48},{80,96},{96,80},{112,0},{1... | collective-permute-start | bytes 786440 | tf_op jit(solution)/shard_map/ppermute | solution.py:475
  9.1 1.2 %collective-permute-start.2 = (bf16[2,512,128]{2,1,0:T(8,128)(2,1)S(1)}, bf16[2,512,128]{2,1,0:T(8,128)(2,1)S(1)}, u32[]{:S(2)}, u32[]{:S(2)}) collective-permute-start(bf16[2,512,128]{2,1,0:T(8,128)(2,1)S(1)} %get-tuple-element.28), channel_id=1, source_target_pairs={{0,1},{1,0},{2,3},{3,2},{4,5},{5,4},{6,7},{7,6},{8,9},{9,8},{10,11... | collective-permute-start | bytes 786440 | tf_op jit(solution)/shard_map/ppermute | solution.py:475
  10.6 4.3 %collective-permute-done.1.row_b.row_b_ref = bf16[2,128,512]{2,1,0:T(8,128)(2,1)S(1)} collective-permute-done((bf16[2,128,512]{2,1,0:T(8,128)(2,1)S(1)}, bf16[2,128,512]{2,1,0:T(8,128)(2,1)S(1)}, u32[]{:S(2)}, u32[]{:S(2)}) %collective-permute-start.1) | collective-permute-done | bytes 262176 | tf_op jit(solution)/shard_map/ppermute | solution.py:475
  14.9 3.4 %collective-permute-start.4 = (bf16[4,128,128]{2,1,0:T(8,128)(2,1)S(1)}, bf16[4,128,128]{2,1,0:T(8,128)(2,1)S(1)}, u32[]{:S(2)}, u32[]{:S(2)}) collective-permute-start(bf16[4,128,128]{2,1,0:T(8,128)(2,1)S(1)} %get-tuple-element.30), channel_id=1, source_target_pairs={{0,1},{1,0},{2,3},{3,2},{4,5},{5,4},{6,7},{7,6},{8,9},{9,8},{10,11... | collective-permute-start | bytes 393224 | tf_op jit(solution)/shard_map/ppermute | solution.py:475
  18.4 1.2 %collective-permute-start.5 = (bf16[4,128,128]{2,1,0:T(8,128)(2,1)S(1)}, bf16[4,128,128]{2,1,0:T(8,128)(2,1)S(1)}, u32[]{:S(2)}, u32[]{:S(2)}) collective-permute-start(bf16[4,128,128]{2,1,0:T(8,128)(2,1)S(1)} %get-tuple-element.31), channel_id=1, source_target_pairs={{0,15},{1,2},{2,1},{3,4},{4,3},{5,6},{6,5},{7,8},{8,7},{9,10},{10,... | collective-permute-start | bytes 393224 | tf_op jit(solution)/shard_map/ppermute | solution.py:475
  19.6 2.2 %prepare.1 = (f32[2,6,768,128]{3,2,1,0:T(8,128)S(1)}, f32[2,6,768,128]{3,2,1,0:T(8,128)S(1)}, f32[2,2,256,256]{3,2,1,0:T(8,128)S(1)}, f32[2,2,256,256]{3,2,1,0:T...) custom-call(bf16[2,512,512]{2,1,0:T(8,128)(2,1)} %mid_hbm.1, ...), custom_call_target="tpu_custom_call" | custom-call | flops 5000000000 | tf_op jit(solution)/shard_map/prepare/pallas_call | solution.py:280
  22.5 2.1 %collective-permute-done.5.cor_b_ref = bf16[4,128,128]{2,1,0:T(8,128)(2,1)S(1)} collective-permute-done((bf16[4,128,128]{2,1,0:T(8,128)(2,1)S(1)}, bf16[4,128,128]{2,1,0:T(8,128)(2,1)S(1)}, u32[]{:S(2)}, u32[]{:S(2)}) %collective-permute-start.5) | collective-permute-done | bytes 131104 | tf_op jit(solution)/shard_map/ppermute | solution.py:475
  24.5 8.2 %frames.1 = (f32[2,6,768,128]{3,2,1,0:T(8,128)S(1)}, f32[2,6,768,128]{3,2,1,0:T(8,128)S(1)}, f32[2,2,256,256]{3,2,1,0:T(8,128)S(1)}, f32[2,512,512]{2,1,0:T(8,12...) custom-call(s32[1,1]{1,0:T(1,128)S(6)} %copy.15.count_ref, ...), custom_call_target="tpu_custom_call", output_to_operand_aliasing={{0}: (8, {}), {1}: (9, {}), {2}: (10, {})} | custom-call | tf_op jit(solution)/shard_map/frames/pallas_call | solution.py:302
  32.7 9.8 %collective-permute-start.6 = (bf16[64,16,128]{2,1,0:T(8,128)(2,1)S(1)}, bf16[64,16,128]{2,1,0:T(8,128)(2,1)S(1)}, u32[]{:S(2)}, u32[]{:S(2)}) collective-permute-start(bf16[64,16,128]{2,1,0:T(8,128)(2,1)S(1)} %get-tuple-element.39), channel_id=1, source_target_pairs={{0,1},{1,0},{2,3},{3,2},{4,5},{5,4},{6,7},{7,6},{8,9},{9,8},{10,11... | collective-permute-start | bytes 786440 | tf_op jit(solution)/shard_map/ppermute | solution.py:475
  42.6 1.1 %collective-permute-done.6 = bf16[64,16,128]{2,1,0:T(8,128)(2,1)S(1)} collective-permute-done((bf16[64,16,128]{2,1,0:T(8,128)(2,1)S(1)}, bf16[64,16,128]{2,1,0:T(8,128)(2,1)S(1)}, u32[]{:S(2)}, u32[]{:S(2)}) %collective-permute-start.6) | collective-permute-done | bytes 262176 | tf_op jit(solution)/shard_map/ppermute | solution.py:475
  44.5 7.8 %all-to-all-start = ((bf16[64,16,128]{2,1,0:T(8,128)(2,1)}), bf16[64,16,128]{2,1,0:T(8,128)(2,1)S(1)}, u32[]{:S(2)}, u32[]{:S(2)}) async-start(bf16[64,16,128]{2,1,0:T(8,128)(2,1)} %add_convert_fusion), calls=%async_computation | async-start | bytes 524288 | tf_op jit(solution)/shard_map/all_to_all | solution.py:496
  52.3 1.1 %collective-permute-done.8.got_b_ref.col_b_ref = bf16[2,768,128]{2,1,0:T(8,128)(2,1)S(1)} collective-permute-done((bf16[2,768,128]{2,1,0:T(8,128)(2,1)}, bf16[2,768,128]{2,1,0:T(8,128)(2,1)S(1)}, u32[]{:S(2)}, u32[]{:S(2)}) %collective-permute-start.8) | collective-permute-done | bytes 393248 | tf_op jit(solution)/shard_map/ppermute | solution.py:475
  53.3 1.3 %row_margins.1 = (bf16[2,4,128,128]{3,2,1,0:T(8,128)(2,1)S(1)}, bf16[2,4,128,128]{3,2,1,0:T(8,128)(2,1)S(1)}) custom-call(f32[2,4,128,128]{3,2,1,0:T(8,128)} %get-tuple-element.40.strip_a_hbm, f32[2,4,128,128]{3,2,1,0:T(8,128)} %get-tuple-element.41.strip_b_hbm, bf16[2,768,128]{2,1,0:T(8,128)(2,1)S(1)} %collective-permute-done.7.got_a_ref.col_a_ref, ...), custom_call_target="tpu_custom_call" | custom-call | flops 5000000000 | tf_op jit(solution)/shard_map/row_margins/pallas_call | solution.py:369
  54.7 4.4 %collective-permute-start.10 = (bf16[2,4,128,128]{3,2,1,0:T(8,128)(2,1)S(1)}, bf16[2,4,128,128]{3,2,1,0:T(8,128)(2,1)S(1)}, u32[]{:S(2)}, u32[]{:S(2)}) collective-permute-start(bf16[2,4,128,128]{3,2,1,0:T(8,128)(2,1)S(1)} %get-tuple-element.45), channel_id=1, source_target_pairs={{0,112},{16,32},{32,16},{48,64},{64,48},{80,96},{96,80},{112,0},{1... | collective-permute-start | bytes 786440 | tf_op jit(solution)/shard_map/ppermute | solution.py:475
  59.1 2.7 %all-to-all-done.got_ref = bf16[64,16,128]{2,1,0:T(8,128)(2,1)S(1)} async-done(((bf16[64,16,128]{2,1,0:T(8,128)(2,1)}), bf16[64,16,128]{2,1,0:T(8,128)(2,1)S(1)}, u32[]{:S(2)}, u32[]{:S(2)}) %all-to-all-start) | async-done | bytes 262176 | tf_op jit(solution)/shard_map/all_to_all | solution.py:496
  61.8 0.8 peer_sum.1
  62.6 4.9 %all-to-all-start.1 = ((bf16[64,16,128]{2,1,0:T(8,128)(2,1)}), bf16[64,16,128]{2,1,0:T(8,128)(2,1)S(1)}, u32[]{:S(2)}, u32[]{:S(2)}) async-start(bf16[64,16,128]{2,1,0:T(8,128)(2,1)} %peer_sum.1), calls=%async_computation.1 | async-start | bytes 524288 | tf_op jit(solution)/shard_map/all_to_all | solution.py:501
  67.5 2.5 %finish_object.1 = f32[2,512,512]{2,1,0:T(8,128)} custom-call(f32[2,512,512]{2,1,0:T(8,128)} %get-tuple-element.47.part_hbm, bf16[2,768,128]{2,1,0:T(8,128)(2,1)S(1)} %collective-permute-done.7.got_a_ref.col_a_ref, bf16[2,768,128]{2,1,0:T(8,128)(2,1)S(1)} %collective-permute-done.8.got_b_ref.col_b_ref, ...), custom_call_target="tpu_custom_call" | custom-call | flops 5000000000 | tf_op jit(solution)/shard_map/finish_object/pallas_call | solution.py:435
  70.0 6.7 %all-to-all-done.1.mine_ref = bf16[64,16,128]{2,1,0:T(8,128)(2,1)S(1)} async-done(((bf16[64,16,128]{2,1,0:T(8,128)(2,1)}), bf16[64,16,128]{2,1,0:T(8,128)(2,1)S(1)}, u32[]{:S(2)}, u32[]{:S(2)}) %all-to-all-start.1) | async-done | bytes 262176 | tf_op jit(solution)/shard_map/all_to_all | solution.py:501
  76.7 3.4 %collective-permute-start.11 = (bf16[64,16,128]{2,1,0:T(8,128)(2,1)S(1)}, bf16[64,16,128]{2,1,0:T(8,128)(2,1)S(1)}, u32[]{:S(2)}, u32[]{:S(2)}) collective-permute-start(bf16[64,16,128]{2,1,0:T(8,128)(2,1)S(1)} %all-to-all-done.1.mine_ref), channel_id=1, source_target_pairs={{0,1},{1,0},{2,3},{3,2},{4,5},{5,4},{6,7},{7,6},{8,9},{9,8},{10,11... | collective-permute-start | bytes 786440 | tf_op jit(solution)/shard_map/ppermute | solution.py:475
  80.1 1.2 %collective-permute-done.11.theirs_ref = bf16[64,16,128]{2,1,0:T(8,128)(2,1)S(1)} collective-permute-done((bf16[64,16,128]{2,1,0:T(8,128)(2,1)S(1)}, bf16[64,16,128]{2,1,0:T(8,128)(2,1)S(1)}, u32[]{:S(2)}, u32[]{:S(2)}) %collective-permute-start.11) | collective-permute-done | bytes 262176 | tf_op jit(solution)/shard_map/ppermute | solution.py:475
  81.2 1.0 %finish_probe.1 = f32[2,2,256,256]{3,2,1,0:T(8,128)} custom-call(bf16[64,16,128]{2,1,0:T(8,128)(2,1)S(1)} %all-to-all-done.1.mine_ref, bf16[64,16,128]{2,1,0:T(8,128)(2,1)S(1)} %collective-permute-done.11.theirs_ref), custom_call_target="tpu_custom_call" | custom-call | tf_op jit(solution)/shard_map/finish_probe/pallas_call | solution.py:463
  (15 shorter events, 1.2 us)
Async XLA Ops:
  1.9 8.7 %collective-permute-start = (bf16[2,128,512]{2,1,0:T(8,128)(2,1)S(1)}, bf16[2,128,512]{2,1,0:T(8,128)(2,1)S(1)}, u32[]{:S(2)}, u32[]{:S(2)}) collective-permute-start(bf16[2,128,512]{2,1,0:T(8,128)(2,1)S(1)} %get-tuple-element.26), channel_id=1, source_target_pairs={{0,16},{16,0},{32,48},{48,32},{64,80},{80,64},{96,112},{112,96},{1... | collective-permute-start | bytes 786440 | tf_op jit(solution)/shard_map/ppermute | solution.py:475
  4.4 10.5 %collective-permute-start.1 = (bf16[2,128,512]{2,1,0:T(8,128)(2,1)S(1)}, bf16[2,128,512]{2,1,0:T(8,128)(2,1)S(1)}, u32[]{:S(2)}, u32[]{:S(2)}) collective-permute-start(bf16[2,128,512]{2,1,0:T(8,128)(2,1)S(1)} %get-tuple-element.27), channel_id=1, source_target_pairs={{0,112},{16,32},{32,16},{48,64},{64,48},{80,96},{96,80},{112,0},{1... | collective-permute-start | bytes 786440 | tf_op jit(solution)/shard_map/ppermute | solution.py:475
  9.1 13.3 %collective-permute-start.2 = (bf16[2,512,128]{2,1,0:T(8,128)(2,1)S(1)}, bf16[2,512,128]{2,1,0:T(8,128)(2,1)S(1)}, u32[]{:S(2)}, u32[]{:S(2)}) collective-permute-start(bf16[2,512,128]{2,1,0:T(8,128)(2,1)S(1)} %get-tuple-element.28), channel_id=1, source_target_pairs={{0,1},{1,0},{2,3},{3,2},{4,5},{5,4},{6,7},{7,6},{8,9},{9,8},{10,11... | collective-permute-start | bytes 786440 | tf_op jit(solution)/shard_map/ppermute | solution.py:475
  10.4 12.1 %collective-permute-start.3 = (bf16[2,512,128]{2,1,0:T(8,128)(2,1)S(1)}, bf16[2,512,128]{2,1,0:T(8,128)(2,1)S(1)}, u32[]{:S(2)}, u32[]{:S(2)}) collective-permute-start(bf16[2,512,128]{2,1,0:T(8,128)(2,1)S(1)} %get-tuple-element.29), channel_id=1, source_target_pairs={{0,15},{1,2},{2,1},{3,4},{4,3},{5,6},{6,5},{7,8},{8,7},{9,10},{10,... | collective-permute-start | bytes 786440 | tf_op jit(solution)/shard_map/ppermute | solution.py:475
  14.9 7.5 %collective-permute-start.4 = (bf16[4,128,128]{2,1,0:T(8,128)(2,1)S(1)}, bf16[4,128,128]{2,1,0:T(8,128)(2,1)S(1)}, u32[]{:S(2)}, u32[]{:S(2)}) collective-permute-start(bf16[4,128,128]{2,1,0:T(8,128)(2,1)S(1)} %get-tuple-element.30), channel_id=1, source_target_pairs={{0,1},{1,0},{2,3},{3,2},{4,5},{5,4},{6,7},{7,6},{8,9},{9,8},{10,11... | collective-permute-start | bytes 393224 | tf_op jit(solution)/shard_map/ppermute | solution.py:475
  18.4 6.2 %collective-permute-start.5 = (bf16[4,128,128]{2,1,0:T(8,128)(2,1)S(1)}, bf16[4,128,128]{2,1,0:T(8,128)(2,1)S(1)}, u32[]{:S(2)}, u32[]{:S(2)}) collective-permute-start(bf16[4,128,128]{2,1,0:T(8,128)(2,1)S(1)} %get-tuple-element.31), channel_id=1, source_target_pairs={{0,15},{1,2},{2,1},{3,4},{4,3},{5,6},{6,5},{7,8},{8,7},{9,10},{10,... | collective-permute-start | bytes 393224 | tf_op jit(solution)/shard_map/ppermute | solution.py:475
  19.6 5.0 %copy-start = (s32[1,1,2,8]{3,2,1,0:T(2,128)S(1)}, s32[1,1,2,8]{3,2,1,0:T(2,128)}, u32[]{:S(2)}) copy-start(s32[1,1,2,8]{3,2,1,0:T(2,128)} %pos_ref.1) | copy-start | bytes 196
  32.7 11.0 %collective-permute-start.6 = (bf16[64,16,128]{2,1,0:T(8,128)(2,1)S(1)}, bf16[64,16,128]{2,1,0:T(8,128)(2,1)S(1)}, u32[]{:S(2)}, u32[]{:S(2)}) collective-permute-start(bf16[64,16,128]{2,1,0:T(8,128)(2,1)S(1)} %get-tuple-element.39), channel_id=1, source_target_pairs={{0,1},{1,0},{2,3},{3,2},{4,5},{5,4},{6,7},{7,6},{8,9},{9,8},{10,11... | collective-permute-start | bytes 786440 | tf_op jit(solution)/shard_map/ppermute | solution.py:475
  42.5 9.7 %collective-permute-start.7 = (bf16[2,768,128]{2,1,0:T(8,128)(2,1)}, bf16[2,768,128]{2,1,0:T(8,128)(2,1)S(1)}, u32[]{:S(2)}, u32[]{:S(2)}) collective-permute-start(bf16[2,768,128]{2,1,0:T(8,128)(2,1)} %get-tuple-element.42), channel_id=1, source_target_pairs={{0,1},{1,0},{2,3},{3,2},{4,5},{5,4},{6,7},{7,6},{8,9},{9,8},{10,11... | collective-permute-start | bytes 1179656 | tf_op jit(solution)/shard_map/ppermute | solution.py:475
  42.6 10.7 %collective-permute-start.8 = (bf16[2,768,128]{2,1,0:T(8,128)(2,1)}, bf16[2,768,128]{2,1,0:T(8,128)(2,1)S(1)}, u32[]{:S(2)}, u32[]{:S(2)}) collective-permute-start(bf16[2,768,128]{2,1,0:T(8,128)(2,1)} %get-tuple-element.43), channel_id=1, source_target_pairs={{0,15},{1,2},{2,1},{3,4},{4,3},{5,6},{6,5},{7,8},{8,7},{9,10},{10,... | collective-permute-start | bytes 1179656 | tf_op jit(solution)/shard_map/ppermute | solution.py:475
  44.5 17.3 %all-to-all-start = ((bf16[64,16,128]{2,1,0:T(8,128)(2,1)}), bf16[64,16,128]{2,1,0:T(8,128)(2,1)S(1)}, u32[]{:S(2)}, u32[]{:S(2)}) async-start(bf16[64,16,128]{2,1,0:T(8,128)(2,1)} %add_convert_fusion), calls=%async_computation | async-start | bytes 524288 | tf_op jit(solution)/shard_map/all_to_all | solution.py:496
  54.6 12.8 %collective-permute-start.9 = (bf16[2,4,128,128]{3,2,1,0:T(8,128)(2,1)S(1)}, bf16[2,4,128,128]{3,2,1,0:T(8,128)(2,1)S(1)}, u32[]{:S(2)}, u32[]{:S(2)}) collective-permute-start(bf16[2,4,128,128]{3,2,1,0:T(8,128)(2,1)S(1)} %get-tuple-element.44), channel_id=1, source_target_pairs={{0,16},{16,0},{32,48},{48,32},{64,80},{80,64},{96,112},{112,96},{1... | collective-permute-start | bytes 786440 | tf_op jit(solution)/shard_map/ppermute | solution.py:475
  54.7 12.8 %collective-permute-start.10 = (bf16[2,4,128,128]{3,2,1,0:T(8,128)(2,1)S(1)}, bf16[2,4,128,128]{3,2,1,0:T(8,128)(2,1)S(1)}, u32[]{:S(2)}, u32[]{:S(2)}) collective-permute-start(bf16[2,4,128,128]{3,2,1,0:T(8,128)(2,1)S(1)} %get-tuple-element.45), channel_id=1, source_target_pairs={{0,112},{16,32},{32,16},{48,64},{64,48},{80,96},{96,80},{112,0},{1... | collective-permute-start | bytes 786440 | tf_op jit(solution)/shard_map/ppermute | solution.py:475
  62.6 14.1 %all-to-all-start.1 = ((bf16[64,16,128]{2,1,0:T(8,128)(2,1)}), bf16[64,16,128]{2,1,0:T(8,128)(2,1)S(1)}, u32[]{:S(2)}, u32[]{:S(2)}) async-start(bf16[64,16,128]{2,1,0:T(8,128)(2,1)} %peer_sum.1), calls=%async_computation.1 | async-start | bytes 524288 | tf_op jit(solution)/shard_map/all_to_all | solution.py:501
  76.7 4.5 %collective-permute-start.11 = (bf16[64,16,128]{2,1,0:T(8,128)(2,1)S(1)}, bf16[64,16,128]{2,1,0:T(8,128)(2,1)S(1)}, u32[]{:S(2)}, u32[]{:S(2)}) collective-permute-start(bf16[64,16,128]{2,1,0:T(8,128)(2,1)S(1)} %all-to-all-done.1.mine_ref), channel_id=1, source_target_pairs={{0,1},{1,0},{2,3},{3,2},{4,5},{5,4},{6,7},{7,6},{8,9},{9,8},{10,11... | collective-permute-start | bytes 786440 | tf_op jit(solution)/shard_map/ppermute | solution.py:475

commit v6 on v5

--- a/solution.py
+++ b/solution.py
@@ -47,7 +47,7 @@
     return jnp.dot(a, b, preferred_element_type=F32)
 
 
-def margins_kernel(obj, row_a, row_b, col_a, col_b, sems):
+def margins_kernel(obj, row_a, edge_b, row_b, col_a, col_b, sems):
     tile = obj.shape[1]
     row_odd, core = place()
     copies = []
@@ -56,8 +56,11 @@
         copies.append(pltpu.make_async_copy(src, dst, sems.at[len(copies)]))
         copies[-1].start()
 
-    for row, at in ((row_b, row_odd), (row_a, 1 - row_odd)):
-        put(obj.at[:, pl.ds(pl.multiple_of(at * (tile - HALO), HALO), HALO), :], row)
+    rows_b = pl.ds(pl.multiple_of(row_odd * (tile - HALO), HALO), HALO)
+    put(obj.at[:, rows_b, 0:HALO], edge_b.at[0:2])
+    put(obj.at[:, rows_b, tile - HALO :], edge_b.at[2:4])
+    put(obj.at[:, pl.ds(pl.multiple_of((1 - row_odd) * (tile - HALO), HALO), HALO), :], row_a)
+    put(obj.at[:, rows_b, HALO : tile - HALO], row_b)
     for col, at in ((col_b, core), (col_a, 1 - core)):
         put(obj.at[:, :, pl.ds(pl.multiple_of(at * (tile - HALO), HALO), HALO)], col)
     for copy in copies:
@@ -67,27 +70,29 @@
 def margins(obj):
     tile = obj.shape[1]
     row = jax.ShapeDtypeStruct((2, HALO, tile), BF16)
+    edge = jax.ShapeDtypeStruct((4, HALO, HALO), BF16)
+    inside = jax.ShapeDtypeStruct((2, HALO, tile - 2 * HALO), BF16)
     col = jax.ShapeDtypeStruct((2, tile, HALO), BF16)
     return pl.pallas_call(
         margins_kernel,
-        out_shape=(row, row, col, col),
+        out_shape=(row, edge, inside, col, col),
         in_specs=[pl.BlockSpec(memory_space=pltpu.HBM)],
-        out_specs=(VM,) * 4,
-        scratch_shapes=[pltpu.SemaphoreType.DMA((4,))],
+        out_specs=(VM,) * 5,
+        scratch_shapes=[pltpu.SemaphoreType.DMA((6,))],
         compiler_params=pltpu.CompilerParams(vmem_limit_bytes=8 * 1024 * 1024),
         name="margins",
     )(pltpu.with_memory_space_constraint(obj, pltpu.HBM))
 
 
-def corners_kernel(row_a, row_b, cor_a, cor_b):
+def corners_kernel(row_a, edge_b, cor_a, cor_b):
     tile = row_a.shape[2]
     core = lax.axis_index("core")
 
-    def emit(cor, cols):
-        cor[0:2] = row_a[:, :, cols]
-        cor[2:4] = row_b[:, :, cols]
-
-    low, high = slice(0, HALO), slice(tile - HALO, tile)
+    def emit(cor, side):
+        cor[0:2] = row_a[:, :, side * (tile - HALO) : side * (tile - HALO) + HALO]
+        cor[2:4] = edge_b[2 * side : 2 * side + 2]
+
+    low, high = 0, 1
 
     @pl.when(core == 0)
     def _():
@@ -100,8 +105,8 @@
         emit(cor_b, high)
 
 
-def corners(row_a, row_b):
-    shape = jax.ShapeDtypeStruct((4, HALO, HALO), BF16)
+def corners(row_a, edge_b):
+    shape = jax.ShapeDtypeStruct(edge_b.shape, BF16)
     return pl.pallas_call(
         corners_kernel,
         out_shape=(shape, shape),
@@ -109,11 +114,11 @@
         out_specs=(VM, VM),
         compiler_params=pltpu.CompilerParams(vmem_limit_bytes=8 * 1024 * 1024),
         name="corners",
-    )(row_a, row_b)
+    )(row_a, edge_b)
 
 
 def frames_kernel(
-    count_ref, pos_ref, row_a_ref, row_b_ref, col_a_ref, col_b_ref, cor_a_ref, cor_b_ref,
+    count_ref, pos_ref, row_a_ref, edge_b_ref, row_b_ref, col_a_ref, col_b_ref, cor_a_ref, cor_b_ref,
     ext_ref, grad_ref, pgrad_ref, probe_ref, amp_ref, tables_ref,
     ext, grad, pgrad, obj_hbm, strip_a_hbm, strip_b_hbm, out_a_hbm, out_b_hbm, keep_out, send,
     patch, waves, chi, firsts, backs, out_a, out_b, sems,
@@ -134,7 +139,11 @@
         for b in range(nblk):
             cols = slice(b * LANES, (b + 1) * LANES)
             ext[c, b + 1, pl.ds(row_a, HALO), :] = row_a_ref[c, :, cols].astype(F32)
-            ext[c, b + 1, pl.ds(row_b, HALO), :] = live(row_in, row_b_ref[c, :, cols].astype(F32))
+            if b in (0, nblk - 1):
+                part = edge_b_ref[c + 2 * min(b, 1)]
+            else:
+                part = row_b_ref[c, :, (b - 1) * LANES : b * LANES]
+            ext[c, b + 1, pl.ds(row_b, HALO), :] = live(row_in, part.astype(F32))
         ext[c, col_a, pl.ds(row_a, HALO), :] = cor_a_ref[c].astype(F32)
         ext[c, col_a, HALO : HALO + tile, :] = col_a_ref[c].astype(F32)
         ext[c, col_a, pl.ds(row_b, HALO), :] = live(row_in, cor_a_ref[2 + c].astype(F32))
@@ -477,17 +486,18 @@
 
 def shards(object_field, probe_modes, measured_amp, scan_positions, frame_counts):
     slots = measured_amp.shape[2]
-    to_row_a, to_row_b, to_col_a, to_col_b = margins(object_field)
+    to_row_a, to_edge_b, to_row_b, to_col_a, to_col_b = margins(object_field)
+    edge_b = trade(to_edge_b, "row", 1)
+    row_a = trade(to_row_a, "row", 0)
     row_b = trade(to_row_b, "row", 1)
-    row_a = trade(to_row_a, "row", 0)
     col_b = trade(to_col_b, COL, 1)
     col_a = trade(to_col_a, COL, 0)
-    to_cor_a, to_cor_b = corners(row_a, row_b)
+    to_cor_a, to_cor_b = corners(row_a, edge_b)
     cor_b = trade(to_cor_b, COL, 1)
     cor_a = trade(to_cor_a, COL, 0)
     prepared = prepare(object_field, probe_modes, measured_amp[0, 0], fourier_tables(probe_modes.shape[-1]))
     _, _, _, part, strip_a, strip_b, out_a, out_b, keep, send = run_frames(
-        frame_counts, scan_positions, (row_a, row_b, col_a, col_b, cor_a, cor_b), prepared
+        frame_counts, scan_positions, (row_a, edge_b, row_b, col_a, col_b, cor_a, cor_b), prepared
     )
     scale = 1.0 / math.sqrt(lax.axis_size("row") * lax.axis_size(COL) * slots)
     pair = (keep + trade(send, COL, 0).astype(F32)).astype(BF16)

time: 81.9 us -> 81.4 us (level)
  starting transfers between devices: 43.7 us -> 37 us
  Pallas kernels: 17.3 us -> 22 us
  waiting for transfers between devices: 19.1 us -> 20 us
    ppermute x12 -> x13, starting transfers between devices: 31 us -> 23.9 us  [trade(): lax.ppermute(value, axis, [(i, ((i + phase ^ 1) - phase) % n) for i in ra...]
    pallas_call x1, Pallas kernels: 8.2 us -> 12.8 us  [run_frames(): pl.pallas_call(frames_kernel, out_shape=(pltpu.VMEM(ext.shape, F32), pltp...]
    all_to_all x1, starting transfers between devices: 4.88 us -> 7.22 us  [shards(): mine = lax.all_to_all(peer_sum(peers, scale), PEERS, 0, 0, tiled=True)]
    all_to_all x1, starting transfers between devices: 7.78 us -> 5.91 us  [shards(): peers = lax.all_to_all(pair, PEERS, 0, 0, tiled=True)]
    ppermute x12 -> x13, waiting for transfers between devices: 9.69 us -> 10.9 us  [trade(): lax.ppermute(value, axis, [(i, ((i + phase ^ 1) - phase) % n) for i in ra...]
  transfers between devices with their start and end apart: 14 -> 15, of which waited for: 7 -> 6; matrix products, arithmetic and copies ran while one was open for 1% -> 1% of each run, Pallas kernels for 8% -> 8%
where the time goes in v6:
time: 81.4 us; the launch traced here: 81.2 us
  starting transfers between devices  37 us (45%)
  Pallas kernels  22 us (27%)
  waiting for transfers between devices  20 us (25%)
  between operations  1.41 us (2%)
    ppermute x13, starting transfers between devices, trade(): lax.ppermute(value, axis, [(i, ((i + phase ^ 1) - phase) % n) for i in ra...  23.9 us
    pallas_call x1, Pallas kernels, run_frames(): pl.pallas_call(frames_kernel, out_shape=(pltpu.VMEM(ext.shape, F32), pltp...  12.8 us
    ppermute x13, waiting for transfers between devices, trade(): lax.ppermute(value, axis, [(i, ((i + phase ^ 1) - phase) % n) for i in ra...  10.9 us
    all_to_all x1, starting transfers between devices, shards(): mine = lax.all_to_all(peer_sum(peers, scale), PEERS, 0, 0, tiled=True)  7.22 us
    all_to_all x1, waiting for transfers between devices, shards(): mine = lax.all_to_all(peer_sum(peers, scale), PEERS, 0, 0, tiled=True)  6.7 us
    all_to_all x1, starting transfers between devices, shards(): peers = lax.all_to_all(pair, PEERS, 0, 0, tiled=True)  5.91 us
    pallas_call x1, Pallas kernels, finish_object(): pl.pallas_call(object_kernel, out_shape=pltpu.HBM(part.shape, F32), in_sp...  2.48 us
    all_to_all x1, waiting for transfers between devices, shards(): peers = lax.all_to_all(pair, PEERS, 0, 0, tiled=True)  2.4 us
  transfers between devices with their start and end apart: 15, of which 6 were waited for; matrix products, arithmetic and copies ran while one was open for 1% of the time, Pallas kernels for 8%

profile of v6, /device:TPU:1, one launch (start us, length us, event | category | flops | bytes accessed | tf_op | source)
XLA Modules:
  0.0 81.2 jit_solution(2264371814476814306)
XLA Ops:
  0.6 1.3 %margins.1 = (bf16[2,128,512]{2,1,0:T(8,128)(2,1)S(1)}, bf16[4,128,128]{2,1,0:T(8,128)(2,1)S(1)}, bf16[2,128,256]{2,1,0:T(8,128)(2,1)S(1)}, bf16[2,512,128]{2,1,0:T(8,128)(2,1)S(1)}, bf16[2,512,128]{2,1,0:T(8,128)(2,1)S(1)}) custom-call(bf16[2,512,512]{2,1,0:T(8,128)(2,1)} %mid_hbm.1), custom_call_target="tpu_custom_call" | custom-call | tf_op jit(solution)/shard_map/margins/pallas_call | solution.py:76
  2.0 2.5 %collective-permute-start = (bf16[2,128,512]{2,1,0:T(8,128)(2,1)S(1)}, bf16[2,128,512]{2,1,0:T(8,128)(2,1)S(1)}, u32[]{:S(2)}, u32[]{:S(2)}) collective-permute-start(bf16[2,128,512]{2,1,0:T(8,128)(2,1)S(1)} %get-tuple-element.27), channel_id=1, source_target_pairs={{0,16},{16,0},{32,48},{48,32},{64,80},{80,64},{96,112},{112,96},{1... | collective-permute-start | bytes 786440 | tf_op jit(solution)/shard_map/ppermute | solution.py:484
  4.5 4.7 %collective-permute-start.1 = (bf16[4,128,128]{2,1,0:T(8,128)(2,1)S(1)}, bf16[4,128,128]{2,1,0:T(8,128)(2,1)S(1)}, u32[]{:S(2)}, u32[]{:S(2)}) collective-permute-start(bf16[4,128,128]{2,1,0:T(8,128)(2,1)S(1)} %get-tuple-element.28), channel_id=1, source_target_pairs={{0,112},{16,32},{32,16},{48,64},{64,48},{80,96},{96,80},{112,0},{1... | collective-permute-start | bytes 393224 | tf_op jit(solution)/shard_map/ppermute | solution.py:484
  9.6 1.5 %collective-permute-start.3 = (bf16[2,512,128]{2,1,0:T(8,128)(2,1)S(1)}, bf16[2,512,128]{2,1,0:T(8,128)(2,1)S(1)}, u32[]{:S(2)}, u32[]{:S(2)}) collective-permute-start(bf16[2,512,128]{2,1,0:T(8,128)(2,1)S(1)} %get-tuple-element.30), channel_id=1, source_target_pairs={{0,1},{1,0},{2,3},{3,2},{4,5},{5,4},{6,7},{7,6},{8,9},{9,8},{10,11... | collective-permute-start | bytes 786440 | tf_op jit(solution)/shard_map/ppermute | solution.py:484
  11.1 1.1 %collective-permute-start.4 = (bf16[2,512,128]{2,1,0:T(8,128)(2,1)S(1)}, bf16[2,512,128]{2,1,0:T(8,128)(2,1)S(1)}, u32[]{:S(2)}, u32[]{:S(2)}) collective-permute-start(bf16[2,512,128]{2,1,0:T(8,128)(2,1)S(1)} %get-tuple-element.31), channel_id=1, source_target_pairs={{0,15},{1,2},{2,1},{3,4},{4,3},{5,6},{6,5},{7,8},{8,7},{9,10},{10,... | collective-permute-start | bytes 786440 | tf_op jit(solution)/shard_map/ppermute | solution.py:484
  12.3 3.0 %collective-permute-start.5 = (bf16[4,128,128]{2,1,0:T(8,128)(2,1)S(1)}, bf16[4,128,128]{2,1,0:T(8,128)(2,1)S(1)}, u32[]{:S(2)}, u32[]{:S(2)}) collective-permute-start(bf16[4,128,128]{2,1,0:T(8,128)(2,1)S(1)} %get-tuple-element.32), channel_id=1, source_target_pairs={{0,1},{1,0},{2,3},{3,2},{4,5},{5,4},{6,7},{7,6},{8,9},{9,8},{10,11... | collective-permute-start | bytes 393224 | tf_op jit(solution)/shard_map/ppermute | solution.py:484
  15.4 2.2 %prepare.1 = (f32[2,6,768,128]{3,2,1,0:T(8,128)S(1)}, f32[2,6,768,128]{3,2,1,0:T(8,128)S(1)}, f32[2,2,256,256]{3,2,1,0:T(8,128)S(1)}, f32[2,2,256,256]{3,2,1,0:T...) custom-call(bf16[2,512,512]{2,1,0:T(8,128)(2,1)} %mid_hbm.1, ...), custom_call_target="tpu_custom_call" | custom-call | flops 5000000000 | tf_op jit(solution)/shard_map/prepare/pallas_call | solution.py:289
  18.3 5.1 %collective-permute-done.4.col_b_ref = bf16[2,512,128]{2,1,0:T(8,128)(2,1)S(1)} collective-permute-done((bf16[2,512,128]{2,1,0:T(8,128)(2,1)S(1)}, bf16[2,512,128]{2,1,0:T(8,128)(2,1)S(1)}, u32[]{:S(2)}, u32[]{:S(2)}) %collective-permute-start.4) | collective-permute-done | bytes 262176 | tf_op jit(solution)/shard_map/ppermute | solution.py:484
  23.4 1.4 %collective-permute-done.6.cor_b_ref = bf16[4,128,128]{2,1,0:T(8,128)(2,1)S(1)} collective-permute-done((bf16[4,128,128]{2,1,0:T(8,128)(2,1)S(1)}, bf16[4,128,128]{2,1,0:T(8,128)(2,1)S(1)}, u32[]{:S(2)}, u32[]{:S(2)}) %collective-permute-start.6) | collective-permute-done | bytes 131104 | tf_op jit(solution)/shard_map/ppermute | solution.py:484
  24.8 12.8 %frames.1 = (f32[2,6,768,128]{3,2,1,0:T(8,128)S(1)}, f32[2,6,768,128]{3,2,1,0:T(8,128)S(1)}, f32[2,2,256,256]{3,2,1,0:T(8,128)S(1)}, f32[2,512,512]{2,1,0:T(8,12...) custom-call(s32[1,1]{1,0:T(1,128)S(6)} %copy.15.count_ref, ...), custom_call_target="tpu_custom_call", output_to_operand_aliasing={{0}: (9, {}), {1}: (10, {}), {2}: (11, {})} | custom-call | tf_op jit(solution)/shard_map/frames/pallas_call | solution.py:311
  38.2 5.0 %collective-permute-start.9 = (bf16[2,768,128]{2,1,0:T(8,128)(2,1)}, bf16[2,768,128]{2,1,0:T(8,128)(2,1)S(1)}, u32[]{:S(2)}, u32[]{:S(2)}) collective-permute-start(bf16[2,768,128]{2,1,0:T(8,128)(2,1)} %get-tuple-element.45), channel_id=1, source_target_pairs={{0,15},{1,2},{2,1},{3,4},{4,3},{5,6},{6,5},{7,8},{8,7},{9,10},{10,... | collective-permute-start | bytes 1179656 | tf_op jit(solution)/shard_map/ppermute | solution.py:484
  43.2 0.8 add_convert_fusion
  44.0 5.9 %all-to-all-start = ((bf16[64,16,128]{2,1,0:T(8,128)(2,1)}), bf16[64,16,128]{2,1,0:T(8,128)(2,1)S(1)}, u32[]{:S(2)}, u32[]{:S(2)}) async-start(bf16[64,16,128]{2,1,0:T(8,128)(2,1)} %add_convert_fusion), calls=%async_computation | async-start | bytes 524288 | tf_op jit(solution)/shard_map/all_to_all | solution.py:506
  49.9 3.2 %collective-permute-done.9.got_b_ref.col_b_ref = bf16[2,768,128]{2,1,0:T(8,128)(2,1)S(1)} collective-permute-done((bf16[2,768,128]{2,1,0:T(8,128)(2,1)}, bf16[2,768,128]{2,1,0:T(8,128)(2,1)S(1)}, u32[]{:S(2)}, u32[]{:S(2)}) %collective-permute-start.9) | collective-permute-done | bytes 393248 | tf_op jit(solution)/shard_map/ppermute | solution.py:484
  53.1 1.3 %row_margins.1 = (bf16[2,4,128,128]{3,2,1,0:T(8,128)(2,1)S(1)}, bf16[2,4,128,128]{3,2,1,0:T(8,128)(2,1)S(1)}) custom-call(f32[2,4,128,128]{3,2,1,0:T(8,128)} %get-tuple-element.42.strip_a_hbm, f32[2,4,128,128]{3,2,1,0:T(8,128)} %get-tuple-element.43.strip_b_hbm, bf16[2,768,128]{2,1,0:T(8,128)(2,1)S(1)} %collective-permute-done.8.got_a_ref.col_a_ref, ...), custom_call_target="tpu_custom_call" | custom-call | flops 5000000000 | tf_op jit(solution)/shard_map/row_margins/pallas_call | solution.py:378
  54.5 2.2 %collective-permute-start.11 = (bf16[2,4,128,128]{3,2,1,0:T(8,128)(2,1)S(1)}, bf16[2,4,128,128]{3,2,1,0:T(8,128)(2,1)S(1)}, u32[]{:S(2)}, u32[]{:S(2)}) collective-permute-start(bf16[2,4,128,128]{3,2,1,0:T(8,128)(2,1)S(1)} %get-tuple-element.47), channel_id=1, source_target_pairs={{0,112},{16,32},{32,16},{48,64},{64,48},{80,96},{96,80},{112,0},{1... | collective-permute-start | bytes 786440 | tf_op jit(solution)/shard_map/ppermute | solution.py:484
  56.7 2.4 %all-to-all-done.got_ref = bf16[64,16,128]{2,1,0:T(8,128)(2,1)S(1)} async-done(((bf16[64,16,128]{2,1,0:T(8,128)(2,1)}), bf16[64,16,128]{2,1,0:T(8,128)(2,1)S(1)}, u32[]{:S(2)}, u32[]{:S(2)}) %all-to-all-start) | async-done | bytes 262176 | tf_op jit(solution)/shard_map/all_to_all | solution.py:506
  59.1 0.8 peer_sum.1
  59.9 7.2 %all-to-all-start.1 = ((bf16[64,16,128]{2,1,0:T(8,128)(2,1)}), bf16[64,16,128]{2,1,0:T(8,128)(2,1)S(1)}, u32[]{:S(2)}, u32[]{:S(2)}) async-start(bf16[64,16,128]{2,1,0:T(8,128)(2,1)} %peer_sum.1), calls=%async_computation.1 | async-start | bytes 524288 | tf_op jit(solution)/shard_map/all_to_all | solution.py:511
  67.2 2.5 %finish_object.1 = f32[2,512,512]{2,1,0:T(8,128)} custom-call(f32[2,512,512]{2,1,0:T(8,128)} %get-tuple-element.49.part_hbm, bf16[2,768,128]{2,1,0:T(8,128)(2,1)S(1)} %collective-permute-done.8.got_a_ref.col_a_ref, bf16[2,768,128]{2,1,0:T(8,128)(2,1)S(1)} %collective-permute-done.9.got_b_ref.col_b_ref, ...), custom_call_target="tpu_custom_call" | custom-call | flops 5000000000 | tf_op jit(solution)/shard_map/finish_object/pallas_call | solution.py:444
  69.7 6.7 %all-to-all-done.1.mine_ref = bf16[64,16,128]{2,1,0:T(8,128)(2,1)S(1)} async-done(((bf16[64,16,128]{2,1,0:T(8,128)(2,1)}), bf16[64,16,128]{2,1,0:T(8,128)(2,1)S(1)}, u32[]{:S(2)}, u32[]{:S(2)}) %all-to-all-start.1) | async-done | bytes 262176 | tf_op jit(solution)/shard_map/all_to_all | solution.py:511
  76.4 2.7 %collective-permute-start.12 = (bf16[64,16,128]{2,1,0:T(8,128)(2,1)S(1)}, bf16[64,16,128]{2,1,0:T(8,128)(2,1)S(1)}, u32[]{:S(2)}, u32[]{:S(2)}) collective-permute-start(bf16[64,16,128]{2,1,0:T(8,128)(2,1)S(1)} %all-to-all-done.1.mine_ref), channel_id=1, source_target_pairs={{0,1},{1,0},{2,3},{3,2},{4,5},{5,4},{6,7},{7,6},{8,9},{9,8},{10,11... | collective-permute-start | bytes 786440 | tf_op jit(solution)/shard_map/ppermute | solution.py:484
  79.0 1.2 %collective-permute-done.12.theirs_ref = bf16[64,16,128]{2,1,0:T(8,128)(2,1)S(1)} collective-permute-done((bf16[64,16,128]{2,1,0:T(8,128)(2,1)S(1)}, bf16[64,16,128]{2,1,0:T(8,128)(2,1)S(1)}, u32[]{:S(2)}, u32[]{:S(2)}) %collective-permute-start.12) | collective-permute-done | bytes 262176 | tf_op jit(solution)/shard_map/ppermute | solution.py:484
  80.2 1.0 %finish_probe.1 = f32[2,2,256,256]{3,2,1,0:T(8,128)} custom-call(bf16[64,16,128]{2,1,0:T(8,128)(2,1)S(1)} %all-to-all-done.1.mine_ref, bf16[64,16,128]{2,1,0:T(8,128)(2,1)S(1)} %collective-permute-done.12.theirs_ref), custom_call_target="tpu_custom_call" | custom-call | tf_op jit(solution)/shard_map/finish_probe/pallas_call | solution.py:472
  (17 shorter events, 1.2 us)
Async XLA Ops:
  2.0 10.2 %collective-permute-start = (bf16[2,128,512]{2,1,0:T(8,128)(2,1)S(1)}, bf16[2,128,512]{2,1,0:T(8,128)(2,1)S(1)}, u32[]{:S(2)}, u32[]{:S(2)}) collective-permute-start(bf16[2,128,512]{2,1,0:T(8,128)(2,1)S(1)} %get-tuple-element.27), channel_id=1, source_target_pairs={{0,16},{16,0},{32,48},{48,32},{64,80},{80,64},{96,112},{112,96},{1... | collective-permute-start | bytes 786440 | tf_op jit(solution)/shard_map/ppermute | solution.py:484
  4.5 7.7 %collective-permute-start.1 = (bf16[4,128,128]{2,1,0:T(8,128)(2,1)S(1)}, bf16[4,128,128]{2,1,0:T(8,128)(2,1)S(1)}, u32[]{:S(2)}, u32[]{:S(2)}) collective-permute-start(bf16[4,128,128]{2,1,0:T(8,128)(2,1)S(1)} %get-tuple-element.28), channel_id=1, source_target_pairs={{0,112},{16,32},{32,16},{48,64},{64,48},{80,96},{96,80},{112,0},{1... | collective-permute-start | bytes 393224 | tf_op jit(solution)/shard_map/ppermute | solution.py:484
  9.2 9.0 %collective-permute-start.2 = (bf16[2,128,256]{2,1,0:T(8,128)(2,1)S(1)}, bf16[2,128,256]{2,1,0:T(8,128)(2,1)S(1)}, u32[]{:S(2)}, u32[]{:S(2)}) collective-permute-start(bf16[2,128,256]{2,1,0:T(8,128)(2,1)S(1)} %get-tuple-element.29), channel_id=1, source_target_pairs={{0,112},{16,32},{32,16},{48,64},{64,48},{80,96},{96,80},{112,0},{1... | collective-permute-start | bytes 393224 | tf_op jit(solution)/shard_map/ppermute | solution.py:484
  9.6 8.7 %collective-permute-start.3 = (bf16[2,512,128]{2,1,0:T(8,128)(2,1)S(1)}, bf16[2,512,128]{2,1,0:T(8,128)(2,1)S(1)}, u32[]{:S(2)}, u32[]{:S(2)}) collective-permute-start(bf16[2,512,128]{2,1,0:T(8,128)(2,1)S(1)} %get-tuple-element.30), channel_id=1, source_target_pairs={{0,1},{1,0},{2,3},{3,2},{4,5},{5,4},{6,7},{7,6},{8,9},{9,8},{10,11... | collective-permute-start | bytes 786440 | tf_op jit(solution)/shard_map/ppermute | solution.py:484
  11.1 12.3 %collective-permute-start.4 = (bf16[2,512,128]{2,1,0:T(8,128)(2,1)S(1)}, bf16[2,512,128]{2,1,0:T(8,128)(2,1)S(1)}, u32[]{:S(2)}, u32[]{:S(2)}) collective-permute-start(bf16[2,512,128]{2,1,0:T(8,128)(2,1)S(1)} %get-tuple-element.31), channel_id=1, source_target_pairs={{0,15},{1,2},{2,1},{3,4},{4,3},{5,6},{6,5},{7,8},{8,7},{9,10},{10,... | collective-permute-start | bytes 786440 | tf_op jit(solution)/shard_map/ppermute | solution.py:484
  12.3 11.2 %collective-permute-start.5 = (bf16[4,128,128]{2,1,0:T(8,128)(2,1)S(1)}, bf16[4,128,128]{2,1,0:T(8,128)(2,1)S(1)}, u32[]{:S(2)}, u32[]{:S(2)}) collective-permute-start(bf16[4,128,128]{2,1,0:T(8,128)(2,1)S(1)} %get-tuple-element.32), channel_id=1, source_target_pairs={{0,1},{1,0},{2,3},{3,2},{4,5},{5,4},{6,7},{7,6},{8,9},{9,8},{10,11... | collective-permute-start | bytes 393224 | tf_op jit(solution)/shard_map/ppermute | solution.py:484
  15.3 9.5 %collective-permute-start.6 = (bf16[4,128,128]{2,1,0:T(8,128)(2,1)S(1)}, bf16[4,128,128]{2,1,0:T(8,128)(2,1)S(1)}, u32[]{:S(2)}, u32[]{:S(2)}) collective-permute-start(bf16[4,128,128]{2,1,0:T(8,128)(2,1)S(1)} %get-tuple-element.33), channel_id=1, source_target_pairs={{0,15},{1,2},{2,1},{3,4},{4,3},{5,6},{6,5},{7,8},{8,7},{9,10},{10,... | collective-permute-start | bytes 393224 | tf_op jit(solution)/shard_map/ppermute | solution.py:484
  15.4 9.5 %copy-start = (s32[1,1,2,8]{3,2,1,0:T(2,128)S(1)}, s32[1,1,2,8]{3,2,1,0:T(2,128)}, u32[]{:S(2)}) copy-start(s32[1,1,2,8]{3,2,1,0:T(2,128)} %pos_ref.1) | copy-start | bytes 196
  37.6 5.6 %collective-permute-start.7 = (bf16[64,16,128]{2,1,0:T(8,128)(2,1)S(1)}, bf16[64,16,128]{2,1,0:T(8,128)(2,1)S(1)}, u32[]{:S(2)}, u32[]{:S(2)}) collective-permute-start(bf16[64,16,128]{2,1,0:T(8,128)(2,1)S(1)} %get-tuple-element.41), channel_id=1, source_target_pairs={{0,1},{1,0},{2,3},{3,2},{4,5},{5,4},{6,7},{7,6},{8,9},{9,8},{10,11... | collective-permute-start | bytes 786440 | tf_op jit(solution)/shard_map/ppermute | solution.py:484
  37.7 12.2 %collective-permute-start.8 = (bf16[2,768,128]{2,1,0:T(8,128)(2,1)}, bf16[2,768,128]{2,1,0:T(8,128)(2,1)S(1)}, u32[]{:S(2)}, u32[]{:S(2)}) collective-permute-start(bf16[2,768,128]{2,1,0:T(8,128)(2,1)} %get-tuple-element.44), channel_id=1, source_target_pairs={{0,1},{1,0},{2,3},{3,2},{4,5},{5,4},{6,7},{7,6},{8,9},{9,8},{10,11... | collective-permute-start | bytes 1179656 | tf_op jit(solution)/shard_map/ppermute | solution.py:484
  38.2 14.9 %collective-permute-start.9 = (bf16[2,768,128]{2,1,0:T(8,128)(2,1)}, bf16[2,768,128]{2,1,0:T(8,128)(2,1)S(1)}, u32[]{:S(2)}, u32[]{:S(2)}) collective-permute-start(bf16[2,768,128]{2,1,0:T(8,128)(2,1)} %get-tuple-element.45), channel_id=1, source_target_pairs={{0,15},{1,2},{2,1},{3,4},{4,3},{5,6},{6,5},{7,8},{8,7},{9,10},{10,... | collective-permute-start | bytes 1179656 | tf_op jit(solution)/shard_map/ppermute | solution.py:484
  44.0 15.2 %all-to-all-start = ((bf16[64,16,128]{2,1,0:T(8,128)(2,1)}), bf16[64,16,128]{2,1,0:T(8,128)(2,1)S(1)}, u32[]{:S(2)}, u32[]{:S(2)}) async-start(bf16[64,16,128]{2,1,0:T(8,128)(2,1)} %add_convert_fusion), calls=%async_computation | async-start | bytes 524288 | tf_op jit(solution)/shard_map/all_to_all | solution.py:506
  54.4 12.7 %collective-permute-start.10 = (bf16[2,4,128,128]{3,2,1,0:T(8,128)(2,1)S(1)}, bf16[2,4,128,128]{3,2,1,0:T(8,128)(2,1)S(1)}, u32[]{:S(2)}, u32[]{:S(2)}) collective-permute-start(bf16[2,4,128,128]{3,2,1,0:T(8,128)(2,1)S(1)} %get-tuple-element.46), channel_id=1, source_target_pairs={{0,16},{16,0},{32,48},{48,32},{64,80},{80,64},{96,112},{112,96},{1... | collective-permute-start | bytes 786440 | tf_op jit(solution)/shard_map/ppermute | solution.py:484
  54.5 12.7 %collective-permute-start.11 = (bf16[2,4,128,128]{3,2,1,0:T(8,128)(2,1)S(1)}, bf16[2,4,128,128]{3,2,1,0:T(8,128)(2,1)S(1)}, u32[]{:S(2)}, u32[]{:S(2)}) collective-permute-start(bf16[2,4,128,128]{3,2,1,0:T(8,128)(2,1)S(1)} %get-tuple-element.47), channel_id=1, source_target_pairs={{0,112},{16,32},{32,16},{48,64},{64,48},{80,96},{96,80},{112,0},{1... | collective-permute-start | bytes 786440 | tf_op jit(solution)/shard_map/ppermute | solution.py:484
  59.9 16.4 %all-to-all-start.1 = ((bf16[64,16,128]{2,1,0:T(8,128)(2,1)}), bf16[64,16,128]{2,1,0:T(8,128)(2,1)S(1)}, u32[]{:S(2)}, u32[]{:S(2)}) async-start(bf16[64,16,128]{2,1,0:T(8,128)(2,1)} %peer_sum.1), calls=%async_computation.1 | async-start | bytes 524288 | tf_op jit(solution)/shard_map/all_to_all | solution.py:511
  76.4 3.8 %collective-permute-start.12 = (bf16[64,16,128]{2,1,0:T(8,128)(2,1)S(1)}, bf16[64,16,128]{2,1,0:T(8,128)(2,1)S(1)}, u32[]{:S(2)}, u32[]{:S(2)}) collective-permute-start(bf16[64,16,128]{2,1,0:T(8,128)(2,1)S(1)} %all-to-all-done.1.mine_ref), channel_id=1, source_target_pairs={{0,1},{1,0},{2,3},{3,2},{4,5},{5,4},{6,7},{7,6},{8,9},{9,8},{10,11... | collective-permute-start | bytes 786440 | tf_op jit(solution)/shard_map/ppermute | solution.py:484

commit v7 on v6

--- a/solution.py
+++ b/solution.py
@@ -480,8 +480,18 @@
 
 
 def trade(value, axis, phase):
-    n = lax.axis_size(axis)
-    return lax.ppermute(value, axis, [(i, (((i + phase) ^ 1) - phase) % n) for i in range(n)])
+    n_row, n_col = lax.axis_size("row"), lax.axis_size(COL)
+    pairs = []
+    for r in range(n_row):
+        for c in range(n_col):
+            if axis == "row":
+                at = ((r + phase) ^ 1) - phase
+                to = (at, c) if 0 <= at < n_row else (r, c ^ 1)
+            else:
+                at = ((c + phase) ^ 1) - phase
+                to = (r, at) if 0 <= at < n_col else (r ^ 1, c)
+            pairs.append((r * n_col + c, to[0] * n_col + to[1]))
+    return lax.ppermute(value, ("row",) + COL, pairs)
 
 
 def shards(object_field, probe_modes, measured_amp, scan_positions, frame_counts):

time: 81.4 us -> 79.8 us (0.980)
  starting transfers between devices: 37 us -> 32.1 us
  Pallas kernels: 22 us -> 25.1 us
    ppermute x13, starting transfers between devices: 23.9 us -> 13.4 us  [trade(): return lax.ppermute(value, ('row',) + COL, pairs)]
    all_to_all x1, starting transfers between devices: 5.91 us -> 13.9 us  [shards(): peers = lax.all_to_all(pair, PEERS, 0, 0, tiled=True)]
    ppermute x13, waiting for transfers between devices: 10.9 us -> 7 us  [trade(): return lax.ppermute(value, ('row',) + COL, pairs)]
    all_to_all x1, waiting for transfers between devices: 2.4 us -> 6.29 us  [shards(): peers = lax.all_to_all(pair, PEERS, 0, 0, tiled=True)]
    pallas_call x1, Pallas kernels: 12.8 us -> 15.9 us  [run_frames(): pl.pallas_call(frames_kernel, out_shape=(pltpu.VMEM(ext.shape, F32), pltp...]
    all_to_all x1, starting transfers between devices: 7.22 us -> 4.8 us  [shards(): mine = lax.all_to_all(peer_sum(peers, scale), PEERS, 0, 0, tiled=True)]
  transfers between devices with their start and end apart: 15 -> 15, of which waited for: 6 -> 6; matrix products, arithmetic and copies ran while one was open for 1% -> 1% of each run, Pallas kernels for 8% -> 9%
where the time goes in v7:
time: 79.8 us; the launch traced here: 79.3 us
  starting transfers between devices  32.1 us (40%)
  Pallas kernels  25.1 us (31%)
  waiting for transfers between devices  20 us (25%)
  between operations  1.42 us (2%)
    pallas_call x1, Pallas kernels, run_frames(): pl.pallas_call(frames_kernel, out_shape=(pltpu.VMEM(ext.shape, F32), pltp...  15.9 us
    all_to_all x1, starting transfers between devices, shards(): peers = lax.all_to_all(pair, PEERS, 0, 0, tiled=True)  13.9 us
    ppermute x13, starting transfers between devices, trade(): return lax.ppermute(value, ('row',) + COL, pairs)  13.4 us
    ppermute x13, waiting for transfers between devices, trade(): return lax.ppermute(value, ('row',) + COL, pairs)  7 us
    all_to_all x1, waiting for transfers between devices, shards(): mine = lax.all_to_all(peer_sum(peers, scale), PEERS, 0, 0, tiled=True)  6.7 us
    all_to_all x1, waiting for transfers between devices, shards(): peers = lax.all_to_all(pair, PEERS, 0, 0, tiled=True)  6.29 us
    all_to_all x1, starting transfers between devices, shards(): mine = lax.all_to_all(peer_sum(peers, scale), PEERS, 0, 0, tiled=True)  4.8 us
    pallas_call x1, Pallas kernels, finish_object(): pl.pallas_call(object_kernel, out_shape=pltpu.HBM(part.shape, F32), in_sp...  2.48 us
  transfers between devices with their start and end apart: 15, of which 6 were waited for; matrix products, arithmetic and copies ran while one was open for 1% of the time, Pallas kernels for 9%

profile of v7, /device:TPU:1, one launch (start us, length us, event | category | flops | bytes accessed | tf_op | source)
XLA Modules:
  0.0 79.3 jit_solution(12087256479533638762)
XLA Ops:
  0.6 1.3 %margins.1 = (bf16[2,128,512]{2,1,0:T(8,128)(2,1)S(1)}, bf16[4,128,128]{2,1,0:T(8,128)(2,1)S(1)}, bf16[2,128,256]{2,1,0:T(8,128)(2,1)S(1)}, bf16[2,512,128]{2,1,0:T(8,128)(2,1)S(1)}, bf16[2,512,128]{2,1,0:T(8,128)(2,1)S(1)}) custom-call(bf16[2,512,512]{2,1,0:T(8,128)(2,1)} %mid_hbm.1), custom_call_target="tpu_custom_call" | custom-call | tf_op jit(solution)/shard_map/margins/pallas_call | solution.py:76
  2.0 2.5 %collective-permute-start = (bf16[2,128,512]{2,1,0:T(8,128)(2,1)S(1)}, bf16[2,128,512]{2,1,0:T(8,128)(2,1)S(1)}, u32[]{:S(2)}, u32[]{:S(2)}) collective-permute-start(bf16[2,128,512]{2,1,0:T(8,128)(2,1)S(1)} %get-tuple-element.27), channel_id=1, source_target_pairs={{0,16},{1,17},{2,18},{3,19},{4,20},{5,21},{6,22},{7,23},{8,24},{9,... | collective-permute-start | bytes 786440 | tf_op jit(solution)/shard_map/ppermute | solution.py:494
  4.5 1.0 %collective-permute-start.1 = (bf16[4,128,128]{2,1,0:T(8,128)(2,1)S(1)}, bf16[4,128,128]{2,1,0:T(8,128)(2,1)S(1)}, u32[]{:S(2)}, u32[]{:S(2)}) collective-permute-start(bf16[4,128,128]{2,1,0:T(8,128)(2,1)S(1)} %get-tuple-element.28), channel_id=1, source_target_pairs={{0,1},{1,0},{2,3},{3,2},{4,5},{5,4},{6,7},{7,6},{8,9},{9,8},{10,11... | collective-permute-start | bytes 393224 | tf_op jit(solution)/shard_map/ppermute | solution.py:494
  6.0 1.1 %collective-permute-start.4 = (bf16[2,512,128]{2,1,0:T(8,128)(2,1)S(1)}, bf16[2,512,128]{2,1,0:T(8,128)(2,1)S(1)}, u32[]{:S(2)}, u32[]{:S(2)}) collective-permute-start(bf16[2,512,128]{2,1,0:T(8,128)(2,1)S(1)} %get-tuple-element.31), channel_id=1, source_target_pairs={{0,16},{1,2},{2,1},{3,4},{4,3},{5,6},{6,5},{7,8},{8,7},{9,10},{10,... | collective-permute-start | bytes 786440 | tf_op jit(solution)/shard_map/ppermute | solution.py:494
  7.1 3.4 %collective-permute-done.row_a.row_a_ref = bf16[2,128,512]{2,1,0:T(8,128)(2,1)S(1)} collective-permute-done((bf16[2,128,512]{2,1,0:T(8,128)(2,1)S(1)}, bf16[2,128,512]{2,1,0:T(8,128)(2,1)S(1)}, u32[]{:S(2)}, u32[]{:S(2)}) %collective-permute-start) | collective-permute-done | bytes 262176 | tf_op jit(solution)/shard_map/ppermute | solution.py:494
  10.6 1.3 %collective-permute-start.5 = (bf16[4,128,128]{2,1,0:T(8,128)(2,1)S(1)}, bf16[4,128,128]{2,1,0:T(8,128)(2,1)S(1)}, u32[]{:S(2)}, u32[]{:S(2)}) collective-permute-start(bf16[4,128,128]{2,1,0:T(8,128)(2,1)S(1)} %get-tuple-element.32), channel_id=1, source_target_pairs={{0,1},{1,0},{2,3},{3,2},{4,5},{5,4},{6,7},{7,6},{8,9},{9,8},{10,11... | collective-permute-start | bytes 393224 | tf_op jit(solution)/shard_map/ppermute | solution.py:494
  11.9 1.2 %collective-permute-start.6 = (bf16[4,128,128]{2,1,0:T(8,128)(2,1)S(1)}, bf16[4,128,128]{2,1,0:T(8,128)(2,1)S(1)}, u32[]{:S(2)}, u32[]{:S(2)}) collective-permute-start(bf16[4,128,128]{2,1,0:T(8,128)(2,1)S(1)} %get-tuple-element.33), channel_id=1, source_target_pairs={{0,16},{1,2},{2,1},{3,4},{4,3},{5,6},{6,5},{7,8},{8,7},{9,10},{10,... | collective-permute-start | bytes 393224 | tf_op jit(solution)/shard_map/ppermute | solution.py:494
  13.1 2.2 %prepare.1 = (f32[2,6,768,128]{3,2,1,0:T(8,128)S(1)}, f32[2,6,768,128]{3,2,1,0:T(8,128)S(1)}, f32[2,2,256,256]{3,2,1,0:T(8,128)S(1)}, f32[2,2,256,256]{3,2,1,0:T...) custom-call(bf16[2,512,512]{2,1,0:T(8,128)(2,1)} %mid_hbm.1, ...), custom_call_target="tpu_custom_call" | custom-call | flops 5000000000 | tf_op jit(solution)/shard_map/prepare/pallas_call | solution.py:289
  16.0 1.4 %collective-permute-done.6.cor_b_ref = bf16[4,128,128]{2,1,0:T(8,128)(2,1)S(1)} collective-permute-done((bf16[4,128,128]{2,1,0:T(8,128)(2,1)S(1)}, bf16[4,128,128]{2,1,0:T(8,128)(2,1)S(1)}, u32[]{:S(2)}, u32[]{:S(2)}) %collective-permute-start.6) | collective-permute-done | bytes 131104 | tf_op jit(solution)/shard_map/ppermute | solution.py:494
  17.4 15.9 %frames.1 = (f32[2,6,768,128]{3,2,1,0:T(8,128)S(1)}, f32[2,6,768,128]{3,2,1,0:T(8,128)S(1)}, f32[2,2,256,256]{3,2,1,0:T(8,128)S(1)}, f32[2,512,512]{2,1,0:T(8,12...) custom-call(s32[1,1]{1,0:T(1,128)S(6)} %copy.15.count_ref, ...), custom_call_target="tpu_custom_call", output_to_operand_aliasing={{0}: (9, {}), {1}: (10, {}), {2}: (11, {})} | custom-call | tf_op jit(solution)/shard_map/frames/pallas_call | solution.py:311
  33.8 1.0 %collective-permute-done.7 = bf16[64,16,128]{2,1,0:T(8,128)(2,1)S(1)} collective-permute-done((bf16[64,16,128]{2,1,0:T(8,128)(2,1)S(1)}, bf16[64,16,128]{2,1,0:T(8,128)(2,1)S(1)}, u32[]{:S(2)}, u32[]{:S(2)}) %collective-permute-start.7) | collective-permute-done | bytes 262176 | tf_op jit(solution)/shard_map/ppermute | solution.py:494
  34.9 0.8 add_convert_fusion
  35.6 13.9 %all-to-all-start = ((bf16[64,16,128]{2,1,0:T(8,128)(2,1)}), bf16[64,16,128]{2,1,0:T(8,128)(2,1)S(1)}, u32[]{:S(2)}, u32[]{:S(2)}) async-start(bf16[64,16,128]{2,1,0:T(8,128)(2,1)} %add_convert_fusion), calls=%async_computation | async-start | bytes 524288 | tf_op jit(solution)/shard_map/all_to_all | solution.py:516
  49.5 1.3 %row_margins.1 = (bf16[2,4,128,128]{3,2,1,0:T(8,128)(2,1)S(1)}, bf16[2,4,128,128]{3,2,1,0:T(8,128)(2,1)S(1)}) custom-call(f32[2,4,128,128]{3,2,1,0:T(8,128)} %get-tuple-element.42.strip_a_hbm, f32[2,4,128,128]{3,2,1,0:T(8,128)} %get-tuple-element.43.strip_b_hbm, bf16[2,768,128]{2,1,0:T(8,128)(2,1)S(1)} %collective-permute-done.8.got_a_ref.col_a_ref, ...), custom_call_target="tpu_custom_call" | custom-call | flops 5000000000 | tf_op jit(solution)/shard_map/row_margins/pallas_call | solution.py:378
  50.8 1.1 %collective-permute-start.10 = (bf16[2,4,128,128]{3,2,1,0:T(8,128)(2,1)S(1)}, bf16[2,4,128,128]{3,2,1,0:T(8,128)(2,1)S(1)}, u32[]{:S(2)}, u32[]{:S(2)}) collective-permute-start(bf16[2,4,128,128]{3,2,1,0:T(8,128)(2,1)S(1)} %get-tuple-element.46), channel_id=1, source_target_pairs={{0,16},{1,17},{2,18},{3,19},{4,20},{5,21},{6,22},{7,23},{8,24},{9,... | collective-permute-start | bytes 786440 | tf_op jit(solution)/shard_map/ppermute | solution.py:494
  51.9 1.0 %collective-permute-start.11 = (bf16[2,4,128,128]{3,2,1,0:T(8,128)(2,1)S(1)}, bf16[2,4,128,128]{3,2,1,0:T(8,128)(2,1)S(1)}, u32[]{:S(2)}, u32[]{:S(2)}) collective-permute-start(bf16[2,4,128,128]{3,2,1,0:T(8,128)(2,1)S(1)} %get-tuple-element.47), channel_id=1, source_target_pairs={{0,1},{1,0},{2,3},{3,2},{4,5},{5,4},{6,7},{7,6},{8,9},{9,8},{10,11... | collective-permute-start | bytes 786440 | tf_op jit(solution)/shard_map/ppermute | solution.py:494
  52.9 6.3 %all-to-all-done.got_ref = bf16[64,16,128]{2,1,0:T(8,128)(2,1)S(1)} async-done(((bf16[64,16,128]{2,1,0:T(8,128)(2,1)}), bf16[64,16,128]{2,1,0:T(8,128)(2,1)S(1)}, u32[]{:S(2)}, u32[]{:S(2)}) %all-to-all-start) | async-done | bytes 262176 | tf_op jit(solution)/shard_map/all_to_all | solution.py:516
  59.2 0.8 peer_sum.1
  60.0 4.8 %all-to-all-start.1 = ((bf16[64,16,128]{2,1,0:T(8,128)(2,1)}), bf16[64,16,128]{2,1,0:T(8,128)(2,1)S(1)}, u32[]{:S(2)}, u32[]{:S(2)}) async-start(bf16[64,16,128]{2,1,0:T(8,128)(2,1)} %peer_sum.1), calls=%async_computation.1 | async-start | bytes 524288 | tf_op jit(solution)/shard_map/all_to_all | solution.py:521
  64.8 2.5 %finish_object.1 = f32[2,512,512]{2,1,0:T(8,128)} custom-call(f32[2,512,512]{2,1,0:T(8,128)} %get-tuple-element.49.part_hbm, bf16[2,768,128]{2,1,0:T(8,128)(2,1)S(1)} %collective-permute-done.8.got_a_ref.col_a_ref, bf16[2,768,128]{2,1,0:T(8,128)(2,1)S(1)} %collective-permute-done.9.got_b_ref.col_b_ref, ...), custom_call_target="tpu_custom_call" | custom-call | flops 5000000000 | tf_op jit(solution)/shard_map/finish_object/pallas_call | solution.py:444
  67.3 6.7 %all-to-all-done.1.mine_ref = bf16[64,16,128]{2,1,0:T(8,128)(2,1)S(1)} async-done(((bf16[64,16,128]{2,1,0:T(8,128)(2,1)}), bf16[64,16,128]{2,1,0:T(8,128)(2,1)S(1)}, u32[]{:S(2)}, u32[]{:S(2)}) %all-to-all-start.1) | async-done | bytes 262176 | tf_op jit(solution)/shard_map/all_to_all | solution.py:521
  74.0 3.1 %collective-permute-start.12 = (bf16[64,16,128]{2,1,0:T(8,128)(2,1)S(1)}, bf16[64,16,128]{2,1,0:T(8,128)(2,1)S(1)}, u32[]{:S(2)}, u32[]{:S(2)}) collective-permute-start(bf16[64,16,128]{2,1,0:T(8,128)(2,1)S(1)} %all-to-all-done.1.mine_ref), channel_id=1, source_target_pairs={{0,1},{1,0},{2,3},{3,2},{4,5},{5,4},{6,7},{7,6},{8,9},{9,8},{10,11... | collective-permute-start | bytes 786440 | tf_op jit(solution)/shard_map/ppermute | solution.py:494
  77.1 1.2 %collective-permute-done.12.theirs_ref = bf16[64,16,128]{2,1,0:T(8,128)(2,1)S(1)} collective-permute-done((bf16[64,16,128]{2,1,0:T(8,128)(2,1)S(1)}, bf16[64,16,128]{2,1,0:T(8,128)(2,1)S(1)}, u32[]{:S(2)}, u32[]{:S(2)}) %collective-permute-start.12) | collective-permute-done | bytes 262176 | tf_op jit(solution)/shard_map/ppermute | solution.py:494
  78.3 1.0 %finish_probe.1 = f32[2,2,256,256]{3,2,1,0:T(8,128)} custom-call(bf16[64,16,128]{2,1,0:T(8,128)(2,1)S(1)} %all-to-all-done.1.mine_ref, bf16[64,16,128]{2,1,0:T(8,128)(2,1)S(1)} %collective-permute-done.12.theirs_ref), custom_call_target="tpu_custom_call" | custom-call | tf_op jit(solution)/shard_map/finish_probe/pallas_call | solution.py:472
  (17 shorter events, 1.2 us)
Async XLA Ops:
  2.0 8.6 %collective-permute-start = (bf16[2,128,512]{2,1,0:T(8,128)(2,1)S(1)}, bf16[2,128,512]{2,1,0:T(8,128)(2,1)S(1)}, u32[]{:S(2)}, u32[]{:S(2)}) collective-permute-start(bf16[2,128,512]{2,1,0:T(8,128)(2,1)S(1)} %get-tuple-element.27), channel_id=1, source_target_pairs={{0,16},{1,17},{2,18},{3,19},{4,20},{5,21},{6,22},{7,23},{8,24},{9,... | collective-permute-start | bytes 786440 | tf_op jit(solution)/shard_map/ppermute | solution.py:494
  4.5 2.6 %collective-permute-start.1 = (bf16[4,128,128]{2,1,0:T(8,128)(2,1)S(1)}, bf16[4,128,128]{2,1,0:T(8,128)(2,1)S(1)}, u32[]{:S(2)}, u32[]{:S(2)}) collective-permute-start(bf16[4,128,128]{2,1,0:T(8,128)(2,1)S(1)} %get-tuple-element.28), channel_id=1, source_target_pairs={{0,1},{1,0},{2,3},{3,2},{4,5},{5,4},{6,7},{7,6},{8,9},{9,8},{10,11... | collective-permute-start | bytes 393224 | tf_op jit(solution)/shard_map/ppermute | solution.py:494
  5.5 10.5 %collective-permute-start.2 = (bf16[2,128,256]{2,1,0:T(8,128)(2,1)S(1)}, bf16[2,128,256]{2,1,0:T(8,128)(2,1)S(1)}, u32[]{:S(2)}, u32[]{:S(2)}) collective-permute-start(bf16[2,128,256]{2,1,0:T(8,128)(2,1)S(1)} %get-tuple-element.29), channel_id=1, source_target_pairs={{0,1},{1,0},{2,3},{3,2},{4,5},{5,4},{6,7},{7,6},{8,9},{9,8},{10,11... | collective-permute-start | bytes 393224 | tf_op jit(solution)/shard_map/ppermute | solution.py:494
  5.5 10.5 %collective-permute-start.3 = (bf16[2,512,128]{2,1,0:T(8,128)(2,1)S(1)}, bf16[2,512,128]{2,1,0:T(8,128)(2,1)S(1)}, u32[]{:S(2)}, u32[]{:S(2)}) collective-permute-start(bf16[2,512,128]{2,1,0:T(8,128)(2,1)S(1)} %get-tuple-element.30), channel_id=1, source_target_pairs={{0,1},{1,0},{2,3},{3,2},{4,5},{5,4},{6,7},{7,6},{8,9},{9,8},{10,11... | collective-permute-start | bytes 786440 | tf_op jit(solution)/shard_map/ppermute | solution.py:494
  6.0 10.0 %collective-permute-start.4 = (bf16[2,512,128]{2,1,0:T(8,128)(2,1)S(1)}, bf16[2,512,128]{2,1,0:T(8,128)(2,1)S(1)}, u32[]{:S(2)}, u32[]{:S(2)}) collective-permute-start(bf16[2,512,128]{2,1,0:T(8,128)(2,1)S(1)} %get-tuple-element.31), channel_id=1, source_target_pairs={{0,16},{1,2},{2,1},{3,4},{4,3},{5,6},{6,5},{7,8},{8,7},{9,10},{10,... | collective-permute-start | bytes 786440 | tf_op jit(solution)/shard_map/ppermute | solution.py:494
  10.6 5.4 %collective-permute-start.5 = (bf16[4,128,128]{2,1,0:T(8,128)(2,1)S(1)}, bf16[4,128,128]{2,1,0:T(8,128)(2,1)S(1)}, u32[]{:S(2)}, u32[]{:S(2)}) collective-permute-start(bf16[4,128,128]{2,1,0:T(8,128)(2,1)S(1)} %get-tuple-element.32), channel_id=1, source_target_pairs={{0,1},{1,0},{2,3},{3,2},{4,5},{5,4},{6,7},{7,6},{8,9},{9,8},{10,11... | collective-permute-start | bytes 393224 | tf_op jit(solution)/shard_map/ppermute | solution.py:494
  11.9 5.5 %collective-permute-start.6 = (bf16[4,128,128]{2,1,0:T(8,128)(2,1)S(1)}, bf16[4,128,128]{2,1,0:T(8,128)(2,1)S(1)}, u32[]{:S(2)}, u32[]{:S(2)}) collective-permute-start(bf16[4,128,128]{2,1,0:T(8,128)(2,1)S(1)} %get-tuple-element.33), channel_id=1, source_target_pairs={{0,16},{1,2},{2,1},{3,4},{4,3},{5,6},{6,5},{7,8},{8,7},{9,10},{10,... | collective-permute-start | bytes 393224 | tf_op jit(solution)/shard_map/ppermute | solution.py:494
  13.1 4.3 %copy-start = (s32[1,1,2,8]{3,2,1,0:T(2,128)S(1)}, s32[1,1,2,8]{3,2,1,0:T(2,128)}, u32[]{:S(2)}) copy-start(s32[1,1,2,8]{3,2,1,0:T(2,128)} %pos_ref.1) | copy-start | bytes 196
  33.3 1.6 %collective-permute-start.7 = (bf16[64,16,128]{2,1,0:T(8,128)(2,1)S(1)}, bf16[64,16,128]{2,1,0:T(8,128)(2,1)S(1)}, u32[]{:S(2)}, u32[]{:S(2)}) collective-permute-start(bf16[64,16,128]{2,1,0:T(8,128)(2,1)S(1)} %get-tuple-element.41), channel_id=1, source_target_pairs={{0,1},{1,0},{2,3},{3,2},{4,5},{5,4},{6,7},{7,6},{8,9},{9,8},{10,11... | collective-permute-start | bytes 786440 | tf_op jit(solution)/shard_map/ppermute | solution.py:494
  33.3 16.2 %collective-permute-start.8 = (bf16[2,768,128]{2,1,0:T(8,128)(2,1)}, bf16[2,768,128]{2,1,0:T(8,128)(2,1)S(1)}, u32[]{:S(2)}, u32[]{:S(2)}) collective-permute-start(bf16[2,768,128]{2,1,0:T(8,128)(2,1)} %get-tuple-element.44), channel_id=1, source_target_pairs={{0,1},{1,0},{2,3},{3,2},{4,5},{5,4},{6,7},{7,6},{8,9},{9,8},{10,11... | collective-permute-start | bytes 1179656 | tf_op jit(solution)/shard_map/ppermute | solution.py:494
  33.8 15.7 %collective-permute-start.9 = (bf16[2,768,128]{2,1,0:T(8,128)(2,1)}, bf16[2,768,128]{2,1,0:T(8,128)(2,1)S(1)}, u32[]{:S(2)}, u32[]{:S(2)}) collective-permute-start(bf16[2,768,128]{2,1,0:T(8,128)(2,1)} %get-tuple-element.45), channel_id=1, source_target_pairs={{0,16},{1,2},{2,1},{3,4},{4,3},{5,6},{6,5},{7,8},{8,7},{9,10},{10,... | collective-permute-start | bytes 1179656 | tf_op jit(solution)/shard_map/ppermute | solution.py:494
  35.6 23.6 %all-to-all-start = ((bf16[64,16,128]{2,1,0:T(8,128)(2,1)}), bf16[64,16,128]{2,1,0:T(8,128)(2,1)S(1)}, u32[]{:S(2)}, u32[]{:S(2)}) async-start(bf16[64,16,128]{2,1,0:T(8,128)(2,1)} %add_convert_fusion), calls=%async_computation | async-start | bytes 524288 | tf_op jit(solution)/shard_map/all_to_all | solution.py:516
  50.8 14.0 %collective-permute-start.10 = (bf16[2,4,128,128]{3,2,1,0:T(8,128)(2,1)S(1)}, bf16[2,4,128,128]{3,2,1,0:T(8,128)(2,1)S(1)}, u32[]{:S(2)}, u32[]{:S(2)}) collective-permute-start(bf16[2,4,128,128]{3,2,1,0:T(8,128)(2,1)S(1)} %get-tuple-element.46), channel_id=1, source_target_pairs={{0,16},{1,17},{2,18},{3,19},{4,20},{5,21},{6,22},{7,23},{8,24},{9,... | collective-permute-start | bytes 786440 | tf_op jit(solution)/shard_map/ppermute | solution.py:494
  51.9 12.9 %collective-permute-start.11 = (bf16[2,4,128,128]{3,2,1,0:T(8,128)(2,1)S(1)}, bf16[2,4,128,128]{3,2,1,0:T(8,128)(2,1)S(1)}, u32[]{:S(2)}, u32[]{:S(2)}) collective-permute-start(bf16[2,4,128,128]{3,2,1,0:T(8,128)(2,1)S(1)} %get-tuple-element.47), channel_id=1, source_target_pairs={{0,1},{1,0},{2,3},{3,2},{4,5},{5,4},{6,7},{7,6},{8,9},{9,8},{10,11... | collective-permute-start | bytes 786440 | tf_op jit(solution)/shard_map/ppermute | solution.py:494
  60.0 14.0 %all-to-all-start.1 = ((bf16[64,16,128]{2,1,0:T(8,128)(2,1)}), bf16[64,16,128]{2,1,0:T(8,128)(2,1)S(1)}, u32[]{:S(2)}, u32[]{:S(2)}) async-start(bf16[64,16,128]{2,1,0:T(8,128)(2,1)} %peer_sum.1), calls=%async_computation.1 | async-start | bytes 524288 | tf_op jit(solution)/shard_map/all_to_all | solution.py:521
  74.0 4.3 %collective-permute-start.12 = (bf16[64,16,128]{2,1,0:T(8,128)(2,1)S(1)}, bf16[64,16,128]{2,1,0:T(8,128)(2,1)S(1)}, u32[]{:S(2)}, u32[]{:S(2)}) collective-permute-start(bf16[64,16,128]{2,1,0:T(8,128)(2,1)S(1)} %all-to-all-done.1.mine_ref), channel_id=1, source_target_pairs={{0,1},{1,0},{2,3},{3,2},{4,5},{5,4},{6,7},{7,6},{8,9},{9,8},{10,11... | collective-permute-start | bytes 786440 | tf_op jit(solution)/shard_map/ppermute | solution.py:494

commit v8 on v7

--- a/solution.py
+++ b/solution.py
@@ -245,7 +245,7 @@
 
     for c in range(2):
         for b in range(nblk):
-            put(grad.at[c, b + 1, HALO : HALO + tile, :], obj_hbm.at[c, :, b * LANES : (b + 1) * LANES])
+            put(grad.at[c, b + 1, HALO : HALO + tile, :], obj_hbm.at[c, b])
         put(grad.at[c, 1 : nblk + 1, pl.ds(row_a, HALO), :], strip_a_hbm.at[c])
         put(grad.at[c, 1 : nblk + 1, pl.ds(row_b, HALO), :], strip_b_hbm.at[c])
     for c in range(2):
@@ -314,7 +314,7 @@
             pltpu.VMEM(ext.shape, F32),
             pltpu.VMEM(grad.shape, F32),
             pltpu.VMEM(pgrad.shape, F32),
-            pltpu.HBM((2, tile, tile), F32),
+            pltpu.HBM((2, nblk, tile, LANES), F32),
             pltpu.HBM((2, nblk, HALO, LANES), F32),
             pltpu.HBM((2, nblk, HALO, LANES), F32),
             pltpu.HBM((2, rows, LANES), BF16),
@@ -420,7 +420,7 @@
     fetches, copies = [], []
     for i, (c, b) in enumerate(blocks):
         cols = slice(b * LANES, (b + 1) * LANES)
-        fetches.append(pltpu.make_async_copy(part_hbm.at[c, :, cols], acc.at[c, b], in_sems.at[i]))
+        fetches.append(pltpu.make_async_copy(part_hbm.at[c, b], acc.at[c, b], in_sems.at[i]))
         copies.append(pltpu.make_async_copy(acc.at[c, b], obj_hbm.at[c, :, cols], out_sems.at[i]))
         fetches[i].start()
     for i, (c, b) in enumerate(blocks):
@@ -439,11 +439,10 @@
 
 
 def finish_object(part, col_a, col_b, row_a, row_b):
-    tile = part.shape[1]
-    nblk = part.shape[2] // LANES
+    nblk, tile = part.shape[1:3]
     return pl.pallas_call(
         object_kernel,
-        out_shape=pltpu.HBM(part.shape, F32),
+        out_shape=pltpu.HBM((2, tile, nblk * LANES), F32),
         in_specs=[pl.BlockSpec(memory_space=pltpu.HBM)] + [VM] * 4,
         out_specs=pl.BlockSpec(memory_space=pltpu.HBM),
         scratch_shapes=[
@@ -457,26 +456,56 @@
     )(pltpu.with_memory_space_constraint(part, pltpu.HBM), col_a, col_b, row_a, row_b)
 
 
-def probe_kernel(mine_ref, theirs_ref, out_ref):
-    core = lax.axis_index("core")
-    modes, side = out_ref.shape[1], out_ref.shape[2]
-    for part_ref, at in ((mine_ref, core), (theirs_ref, 1 - core)):
-        for m in range(modes):
-            for i in range(side // CHUNK):
-                for j in range(side // LANES):
-                    k = (m * (side // CHUNK) + i) * (side // LANES) + j
-                    out_ref[at, m, i * CHUNK : (i + 1) * CHUNK, j * LANES : (j + 1) * LANES] = part_ref[k].astype(F32)
-
-
-def finish_probe(mine, theirs, shape):
-    return pl.pallas_call(
-        probe_kernel,
-        out_shape=jax.ShapeDtypeStruct(shape, F32),
-        in_specs=[VM, VM],
-        out_specs=VM,
-        compiler_params=pltpu.CompilerParams(vmem_limit_bytes=16 * 1024 * 1024),
-        name="finish_probe",
-    )(mine, theirs)
+def put_half(part_ref, half):
+    modes, side = half.shape[0], half.shape[1]
+    for m in range(modes):
+        for i in range(side // CHUNK):
+            for j in range(side // LANES):
+                k = (m * (side // CHUNK) + i) * (side // LANES) + j
+                half[m, i * CHUNK : (i + 1) * CHUNK, j * LANES : (j + 1) * LANES] = part_ref[k].astype(F32)
+
+
+def mine_kernel(part_ref, out_hbm, half, sem):
+    put_half(part_ref, half)
+    copy = pltpu.make_async_copy(half, out_hbm.at[lax.axis_index("core")], sem)
+    copy.start()
+    copy.wait()
+
+
+def theirs_kernel(part_ref, so_far_hbm, out_hbm, half, sem):
+    del so_far_hbm
+    put_half(part_ref, half)
+    copy = pltpu.make_async_copy(half, out_hbm.at[1 - lax.axis_index("core")], sem)
+    copy.start()
+    copy.wait()
+
+
+def finish_mine(mine, shape):
+    hbm = pl.BlockSpec(memory_space=pltpu.HBM)
+    return pl.pallas_call(
+        mine_kernel,
+        out_shape=pltpu.HBM(shape, F32),
+        in_specs=[VM],
+        out_specs=hbm,
+        scratch_shapes=[pltpu.VMEM(shape[1:], F32), pltpu.SemaphoreType.DMA(())],
+        compiler_params=pltpu.CompilerParams(vmem_limit_bytes=8 * 1024 * 1024),
+        cost_estimate=pl.CostEstimate(flops=5000000000, transcendentals=0, bytes_accessed=0),
+        name="finish_mine",
+    )(mine)
+
+
+def finish_theirs(theirs, so_far):
+    hbm = pl.BlockSpec(memory_space=pltpu.HBM)
+    return pl.pallas_call(
+        theirs_kernel,
+        out_shape=pltpu.HBM(so_far.shape, F32),
+        in_specs=[VM, hbm],
+        out_specs=hbm,
+        input_output_aliases={1: 0},
+        scratch_shapes=[pltpu.VMEM(so_far.shape[1:], F32), pltpu.SemaphoreType.DMA(())],
+        compiler_params=pltpu.CompilerParams(vmem_limit_bytes=8 * 1024 * 1024),
+        name="finish_theirs",
+    )(theirs, so_far)
 
 
 def trade(value, axis, phase):
@@ -521,7 +550,8 @@
     mine = lax.all_to_all(peer_sum(peers, scale), PEERS, 0, 0, tiled=True)
     obj = finish_object(part, got_a, got_b, back_a, back_b)
     mine, obj = lax.optimization_barrier((mine, obj))
-    return obj, finish_probe(mine, trade(mine, COL, 0), probe_modes.shape)
+    theirs = trade(mine, COL, 0)
+    return obj, finish_theirs(theirs, finish_mine(mine, probe_modes.shape))
 
 
 def solution(mesh):

time: 79.8 us -> 79.6 us (level)
  waiting for transfers between devices: 20 us -> 19.2 us
    ppermute x13, waiting for transfers between devices: 7 us -> 6.16 us  [trade(): return lax.ppermute(value, ('row',) + COL, pairs)]
    pallas_call x2 -> x3, Pallas kernels: 3.53 us -> 4.15 us  [the longest x1 2.48 us: finish_object(): pl.pallas_call(object_kernel, out_shape=pltpu.HBM((2, tile, nblk * LANES)...]
  transfers between devices with their start and end apart: 15 -> 15, of which waited for: 6 -> 6; matrix products, arithmetic and copies ran while one was open for 1% -> 1% of each run, Pallas kernels for 9% -> 10%
where the time goes in v8:
time: 79.6 us; the launch traced here: 79.4 us
  starting transfers between devices  32.3 us (41%)
  Pallas kernels  25.7 us (32%)
  waiting for transfers between devices  19.2 us (24%)
  between operations  1.43 us (2%)
    pallas_call x1, Pallas kernels, run_frames(): pl.pallas_call(frames_kernel, out_shape=(pltpu.VMEM(ext.shape, F32), pltp...  15.9 us
    all_to_all x1, starting transfers between devices, shards(): peers = lax.all_to_all(pair, PEERS, 0, 0, tiled=True)  14.1 us
    ppermute x13, starting transfers between devices, trade(): return lax.ppermute(value, ('row',) + COL, pairs)  13.4 us
    all_to_all x1, waiting for transfers between devices, shards(): mine = lax.all_to_all(peer_sum(peers, scale), PEERS, 0, 0, tiled=True)  6.7 us
    all_to_all x1, waiting for transfers between devices, shards(): peers = lax.all_to_all(pair, PEERS, 0, 0, tiled=True)  6.29 us
    ppermute x13, waiting for transfers between devices, trade(): return lax.ppermute(value, ('row',) + COL, pairs)  6.16 us
    all_to_all x1, starting transfers between devices, shards(): mine = lax.all_to_all(peer_sum(peers, scale), PEERS, 0, 0, tiled=True)  4.8 us
    pallas_call x1, Pallas kernels, finish_object(): pl.pallas_call(object_kernel, out_shape=pltpu.HBM((2, tile, nblk * LANES)...  2.48 us
  transfers between devices with their start and end apart: 15, of which 6 were waited for; matrix products, arithmetic and copies ran while one was open for 1% of the time, Pallas kernels for 10%

profile of v8, /device:TPU:1, one launch (start us, length us, event | category | flops | bytes accessed | tf_op | source)
XLA Modules:
  0.0 79.4 jit_solution(16444467011558569169)
XLA Ops:
  0.6 1.3 %margins.1 = (bf16[2,128,512]{2,1,0:T(8,128)(2,1)S(1)}, bf16[4,128,128]{2,1,0:T(8,128)(2,1)S(1)}, bf16[2,128,256]{2,1,0:T(8,128)(2,1)S(1)}, bf16[2,512,128]{2,1,0:T(8,128)(2,1)S(1)}, bf16[2,512,128]{2,1,0:T(8,128)(2,1)S(1)}) custom-call(bf16[2,512,512]{2,1,0:T(8,128)(2,1)} %mid_hbm.1), custom_call_target="tpu_custom_call" | custom-call | tf_op jit(solution)/shard_map/margins/pallas_call | solution.py:76
  2.0 2.5 %collective-permute-start = (bf16[2,128,512]{2,1,0:T(8,128)(2,1)S(1)}, bf16[2,128,512]{2,1,0:T(8,128)(2,1)S(1)}, u32[]{:S(2)}, u32[]{:S(2)}) collective-permute-start(bf16[2,128,512]{2,1,0:T(8,128)(2,1)S(1)} %get-tuple-element.27), channel_id=1, source_target_pairs={{0,16},{1,17},{2,18},{3,19},{4,20},{5,21},{6,22},{7,23},{8,24},{9,... | collective-permute-start | bytes 786440 | tf_op jit(solution)/shard_map/ppermute | solution.py:523
  4.5 1.0 %collective-permute-start.1 = (bf16[4,128,128]{2,1,0:T(8,128)(2,1)S(1)}, bf16[4,128,128]{2,1,0:T(8,128)(2,1)S(1)}, u32[]{:S(2)}, u32[]{:S(2)}) collective-permute-start(bf16[4,128,128]{2,1,0:T(8,128)(2,1)S(1)} %get-tuple-element.28), channel_id=1, source_target_pairs={{0,1},{1,0},{2,3},{3,2},{4,5},{5,4},{6,7},{7,6},{8,9},{9,8},{10,11... | collective-permute-start | bytes 393224 | tf_op jit(solution)/shard_map/ppermute | solution.py:523
  6.0 1.1 %collective-permute-start.4 = (bf16[2,512,128]{2,1,0:T(8,128)(2,1)S(1)}, bf16[2,512,128]{2,1,0:T(8,128)(2,1)S(1)}, u32[]{:S(2)}, u32[]{:S(2)}) collective-permute-start(bf16[2,512,128]{2,1,0:T(8,128)(2,1)S(1)} %get-tuple-element.31), channel_id=1, source_target_pairs={{0,16},{1,2},{2,1},{3,4},{4,3},{5,6},{6,5},{7,8},{8,7},{9,10},{10,... | collective-permute-start | bytes 786440 | tf_op jit(solution)/shard_map/ppermute | solution.py:523
  7.1 3.4 %collective-permute-done.row_a.row_a_ref = bf16[2,128,512]{2,1,0:T(8,128)(2,1)S(1)} collective-permute-done((bf16[2,128,512]{2,1,0:T(8,128)(2,1)S(1)}, bf16[2,128,512]{2,1,0:T(8,128)(2,1)S(1)}, u32[]{:S(2)}, u32[]{:S(2)}) %collective-permute-start) | collective-permute-done | bytes 262176 | tf_op jit(solution)/shard_map/ppermute | solution.py:523
  10.6 1.3 %collective-permute-start.5 = (bf16[4,128,128]{2,1,0:T(8,128)(2,1)S(1)}, bf16[4,128,128]{2,1,0:T(8,128)(2,1)S(1)}, u32[]{:S(2)}, u32[]{:S(2)}) collective-permute-start(bf16[4,128,128]{2,1,0:T(8,128)(2,1)S(1)} %get-tuple-element.32), channel_id=1, source_target_pairs={{0,1},{1,0},{2,3},{3,2},{4,5},{5,4},{6,7},{7,6},{8,9},{9,8},{10,11... | collective-permute-start | bytes 393224 | tf_op jit(solution)/shard_map/ppermute | solution.py:523
  11.9 1.2 %collective-permute-start.6 = (bf16[4,128,128]{2,1,0:T(8,128)(2,1)S(1)}, bf16[4,128,128]{2,1,0:T(8,128)(2,1)S(1)}, u32[]{:S(2)}, u32[]{:S(2)}) collective-permute-start(bf16[4,128,128]{2,1,0:T(8,128)(2,1)S(1)} %get-tuple-element.33), channel_id=1, source_target_pairs={{0,16},{1,2},{2,1},{3,4},{4,3},{5,6},{6,5},{7,8},{8,7},{9,10},{10,... | collective-permute-start | bytes 393224 | tf_op jit(solution)/shard_map/ppermute | solution.py:523
  13.1 2.2 %prepare.1 = (f32[2,6,768,128]{3,2,1,0:T(8,128)S(1)}, f32[2,6,768,128]{3,2,1,0:T(8,128)S(1)}, f32[2,2,256,256]{3,2,1,0:T(8,128)S(1)}, f32[2,2,256,256]{3,2,1,0:T...) custom-call(bf16[2,512,512]{2,1,0:T(8,128)(2,1)} %mid_hbm.1, ...), custom_call_target="tpu_custom_call" | custom-call | flops 5000000000 | tf_op jit(solution)/shard_map/prepare/pallas_call | solution.py:289
  16.0 1.4 %collective-permute-done.6.cor_b_ref = bf16[4,128,128]{2,1,0:T(8,128)(2,1)S(1)} collective-permute-done((bf16[4,128,128]{2,1,0:T(8,128)(2,1)S(1)}, bf16[4,128,128]{2,1,0:T(8,128)(2,1)S(1)}, u32[]{:S(2)}, u32[]{:S(2)}) %collective-permute-start.6) | collective-permute-done | bytes 131104 | tf_op jit(solution)/shard_map/ppermute | solution.py:523
  17.4 15.9 %frames.1 = (f32[2,6,768,128]{3,2,1,0:T(8,128)S(1)}, f32[2,6,768,128]{3,2,1,0:T(8,128)S(1)}, f32[2,2,256,256]{3,2,1,0:T(8,128)S(1)}, f32[2,4,512,128]{3,2,1,0:T(...) custom-call(s32[1,1]{1,0:T(1,128)S(6)} %copy.17.count_ref, ...), custom_call_target="tpu_custom_call", output_to_operand_aliasing={{0}: (9, {}), {1}: (10, {}), {2}: (11, {})} | custom-call | tf_op jit(solution)/shard_map/frames/pallas_call | solution.py:311
  33.8 1.0 %collective-permute-done.7 = bf16[64,16,128]{2,1,0:T(8,128)(2,1)S(1)} collective-permute-done((bf16[64,16,128]{2,1,0:T(8,128)(2,1)S(1)}, bf16[64,16,128]{2,1,0:T(8,128)(2,1)S(1)}, u32[]{:S(2)}, u32[]{:S(2)}) %collective-permute-start.7) | collective-permute-done | bytes 262176 | tf_op jit(solution)/shard_map/ppermute | solution.py:523
  34.9 0.8 add_convert_fusion
  35.6 14.1 %all-to-all-start = ((bf16[64,16,128]{2,1,0:T(8,128)(2,1)}), bf16[64,16,128]{2,1,0:T(8,128)(2,1)S(1)}, u32[]{:S(2)}, u32[]{:S(2)}) async-start(bf16[64,16,128]{2,1,0:T(8,128)(2,1)} %add_convert_fusion), calls=%async_computation | async-start | bytes 524288 | tf_op jit(solution)/shard_map/all_to_all | solution.py:545
  49.8 1.3 %row_margins.1 = (bf16[2,4,128,128]{3,2,1,0:T(8,128)(2,1)S(1)}, bf16[2,4,128,128]{3,2,1,0:T(8,128)(2,1)S(1)}) custom-call(f32[2,4,128,128]{3,2,1,0:T(8,128)} %get-tuple-element.42.strip_a_hbm, f32[2,4,128,128]{3,2,1,0:T(8,128)} %get-tuple-element.43.strip_b_hbm, bf16[2,768,128]{2,1,0:T(8,128)(2,1)S(1)} %collective-permute-done.8.got_a_ref.col_a_ref, ...), custom_call_target="tpu_custom_call" | custom-call | flops 5000000000 | tf_op jit(solution)/shard_map/row_margins/pallas_call | solution.py:378
  51.1 1.1 %collective-permute-start.10 = (bf16[2,4,128,128]{3,2,1,0:T(8,128)(2,1)S(1)}, bf16[2,4,128,128]{3,2,1,0:T(8,128)(2,1)S(1)}, u32[]{:S(2)}, u32[]{:S(2)}) collective-permute-start(bf16[2,4,128,128]{3,2,1,0:T(8,128)(2,1)S(1)} %get-tuple-element.46), channel_id=1, source_target_pairs={{0,16},{1,17},{2,18},{3,19},{4,20},{5,21},{6,22},{7,23},{8,24},{9,... | collective-permute-start | bytes 786440 | tf_op jit(solution)/shard_map/ppermute | solution.py:523
  52.2 1.0 %collective-permute-start.11 = (bf16[2,4,128,128]{3,2,1,0:T(8,128)(2,1)S(1)}, bf16[2,4,128,128]{3,2,1,0:T(8,128)(2,1)S(1)}, u32[]{:S(2)}, u32[]{:S(2)}) collective-permute-start(bf16[2,4,128,128]{3,2,1,0:T(8,128)(2,1)S(1)} %get-tuple-element.47), channel_id=1, source_target_pairs={{0,1},{1,0},{2,3},{3,2},{4,5},{5,4},{6,7},{7,6},{8,9},{9,8},{10,11... | collective-permute-start | bytes 786440 | tf_op jit(solution)/shard_map/ppermute | solution.py:523
  53.2 6.3 %all-to-all-done.got_ref = bf16[64,16,128]{2,1,0:T(8,128)(2,1)S(1)} async-done(((bf16[64,16,128]{2,1,0:T(8,128)(2,1)}), bf16[64,16,128]{2,1,0:T(8,128)(2,1)S(1)}, u32[]{:S(2)}, u32[]{:S(2)}) %all-to-all-start) | async-done | bytes 262176 | tf_op jit(solution)/shard_map/all_to_all | solution.py:545
  59.5 0.8 peer_sum.1
  60.3 4.8 %all-to-all-start.1 = ((bf16[64,16,128]{2,1,0:T(8,128)(2,1)}), bf16[64,16,128]{2,1,0:T(8,128)(2,1)S(1)}, u32[]{:S(2)}, u32[]{:S(2)}) async-start(bf16[64,16,128]{2,1,0:T(8,128)(2,1)} %peer_sum.1), calls=%async_computation.1 | async-start | bytes 524288 | tf_op jit(solution)/shard_map/all_to_all | solution.py:550
  65.1 2.5 %finish_object.1 = f32[2,512,512]{2,1,0:T(8,128)} custom-call(f32[2,4,512,128]{3,2,1,0:T(8,128)} %get-tuple-element.49.part_hbm, bf16[2,768,128]{2,1,0:T(8,128)(2,1)S(1)} %collective-permute-done.8.got_a_ref.col_a_ref, bf16[2,768,128]{2,1,0:T(8,128)(2,1)S(1)} %collective-permute-done.9.got_b_ref.col_b_ref, ...), custom_call_target="tpu_custom_call" | custom-call | flops 5000000000 | tf_op jit(solution)/shard_map/finish_object/pallas_call | solution.py:443
  67.6 6.7 %all-to-all-done.1.part_ref = bf16[64,16,128]{2,1,0:T(8,128)(2,1)S(1)} async-done(((bf16[64,16,128]{2,1,0:T(8,128)(2,1)}), bf16[64,16,128]{2,1,0:T(8,128)(2,1)S(1)}, u32[]{:S(2)}, u32[]{:S(2)}) %all-to-all-start.1) | async-done | bytes 262176 | tf_op jit(solution)/shard_map/all_to_all | solution.py:550
  74.3 3.1 %collective-permute-start.12 = (bf16[64,16,128]{2,1,0:T(8,128)(2,1)S(1)}, bf16[64,16,128]{2,1,0:T(8,128)(2,1)S(1)}, u32[]{:S(2)}, u32[]{:S(2)}) collective-permute-start(bf16[64,16,128]{2,1,0:T(8,128)(2,1)S(1)} %all-to-all-done.1.part_ref), channel_id=1, source_target_pairs={{0,1},{1,0},{2,3},{3,2},{4,5},{5,4},{6,7},{7,6},{8,9},{9,8},{10,11... | collective-permute-start | bytes 786440 | tf_op jit(solution)/shard_map/ppermute | solution.py:523
  77.4 0.8 %finish_mine.1.so_far_hbm = f32[2,2,256,256]{3,2,1,0:T(8,128)} custom-call(bf16[64,16,128]{2,1,0:T(8,128)(2,1)S(1)} %all-to-all-done.1.part_ref), custom_call_target="tpu_custom_call" | custom-call | flops 5000000000 | tf_op jit(solution)/shard_map/finish_mine/pallas_call | solution.py:485
  78.5 0.8 %finish_theirs.1 = f32[2,2,256,256]{3,2,1,0:T(8,128)} custom-call(bf16[64,16,128]{2,1,0:T(8,128)(2,1)S(1)} %collective-permute-done.12.part_ref, f32[2,2,256,256]{3,2,1,0:T(8,128)} %finish_mine.1.so_far_hbm), custom_call_target="tpu_custom_call", output_to_operand_aliasing={{}: (1, {})} | custom-call | tf_op jit(solution)/shard_map/finish_theirs/pallas_call | solution.py:499
  (18 shorter events, 1.5 us)
Async XLA Ops:
  2.0 8.6 %collective-permute-start = (bf16[2,128,512]{2,1,0:T(8,128)(2,1)S(1)}, bf16[2,128,512]{2,1,0:T(8,128)(2,1)S(1)}, u32[]{:S(2)}, u32[]{:S(2)}) collective-permute-start(bf16[2,128,512]{2,1,0:T(8,128)(2,1)S(1)} %get-tuple-element.27), channel_id=1, source_target_pairs={{0,16},{1,17},{2,18},{3,19},{4,20},{5,21},{6,22},{7,23},{8,24},{9,... | collective-permute-start | bytes 786440 | tf_op jit(solution)/shard_map/ppermute | solution.py:523
  4.5 2.6 %collective-permute-start.1 = (bf16[4,128,128]{2,1,0:T(8,128)(2,1)S(1)}, bf16[4,128,128]{2,1,0:T(8,128)(2,1)S(1)}, u32[]{:S(2)}, u32[]{:S(2)}) collective-permute-start(bf16[4,128,128]{2,1,0:T(8,128)(2,1)S(1)} %get-tuple-element.28), channel_id=1, source_target_pairs={{0,1},{1,0},{2,3},{3,2},{4,5},{5,4},{6,7},{7,6},{8,9},{9,8},{10,11... | collective-permute-start | bytes 393224 | tf_op jit(solution)/shard_map/ppermute | solution.py:523
  5.5 10.5 %collective-permute-start.2 = (bf16[2,128,256]{2,1,0:T(8,128)(2,1)S(1)}, bf16[2,128,256]{2,1,0:T(8,128)(2,1)S(1)}, u32[]{:S(2)}, u32[]{:S(2)}) collective-permute-start(bf16[2,128,256]{2,1,0:T(8,128)(2,1)S(1)} %get-tuple-element.29), channel_id=1, source_target_pairs={{0,1},{1,0},{2,3},{3,2},{4,5},{5,4},{6,7},{7,6},{8,9},{9,8},{10,11... | collective-permute-start | bytes 393224 | tf_op jit(solution)/shard_map/ppermute | solution.py:523
  5.5 10.5 %collective-permute-start.3 = (bf16[2,512,128]{2,1,0:T(8,128)(2,1)S(1)}, bf16[2,512,128]{2,1,0:T(8,128)(2,1)S(1)}, u32[]{:S(2)}, u32[]{:S(2)}) collective-permute-start(bf16[2,512,128]{2,1,0:T(8,128)(2,1)S(1)} %get-tuple-element.30), channel_id=1, source_target_pairs={{0,1},{1,0},{2,3},{3,2},{4,5},{5,4},{6,7},{7,6},{8,9},{9,8},{10,11... | collective-permute-start | bytes 786440 | tf_op jit(solution)/shard_map/ppermute | solution.py:523
  6.0 10.0 %collective-permute-start.4 = (bf16[2,512,128]{2,1,0:T(8,128)(2,1)S(1)}, bf16[2,512,128]{2,1,0:T(8,128)(2,1)S(1)}, u32[]{:S(2)}, u32[]{:S(2)}) collective-permute-start(bf16[2,512,128]{2,1,0:T(8,128)(2,1)S(1)} %get-tuple-element.31), channel_id=1, source_target_pairs={{0,16},{1,2},{2,1},{3,4},{4,3},{5,6},{6,5},{7,8},{8,7},{9,10},{10,... | collective-permute-start | bytes 786440 | tf_op jit(solution)/shard_map/ppermute | solution.py:523
  10.6 5.4 %collective-permute-start.5 = (bf16[4,128,128]{2,1,0:T(8,128)(2,1)S(1)}, bf16[4,128,128]{2,1,0:T(8,128)(2,1)S(1)}, u32[]{:S(2)}, u32[]{:S(2)}) collective-permute-start(bf16[4,128,128]{2,1,0:T(8,128)(2,1)S(1)} %get-tuple-element.32), channel_id=1, source_target_pairs={{0,1},{1,0},{2,3},{3,2},{4,5},{5,4},{6,7},{7,6},{8,9},{9,8},{10,11... | collective-permute-start | bytes 393224 | tf_op jit(solution)/shard_map/ppermute | solution.py:523
  11.9 5.5 %collective-permute-start.6 = (bf16[4,128,128]{2,1,0:T(8,128)(2,1)S(1)}, bf16[4,128,128]{2,1,0:T(8,128)(2,1)S(1)}, u32[]{:S(2)}, u32[]{:S(2)}) collective-permute-start(bf16[4,128,128]{2,1,0:T(8,128)(2,1)S(1)} %get-tuple-element.33), channel_id=1, source_target_pairs={{0,16},{1,2},{2,1},{3,4},{4,3},{5,6},{6,5},{7,8},{8,7},{9,10},{10,... | collective-permute-start | bytes 393224 | tf_op jit(solution)/shard_map/ppermute | solution.py:523
  13.1 4.3 %copy-start = (s32[1,1,2,8]{3,2,1,0:T(2,128)S(1)}, s32[1,1,2,8]{3,2,1,0:T(2,128)}, u32[]{:S(2)}) copy-start(s32[1,1,2,8]{3,2,1,0:T(2,128)} %pos_ref.1) | copy-start | bytes 196
  33.3 1.6 %collective-permute-start.7 = (bf16[64,16,128]{2,1,0:T(8,128)(2,1)S(1)}, bf16[64,16,128]{2,1,0:T(8,128)(2,1)S(1)}, u32[]{:S(2)}, u32[]{:S(2)}) collective-permute-start(bf16[64,16,128]{2,1,0:T(8,128)(2,1)S(1)} %get-tuple-element.41), channel_id=1, source_target_pairs={{0,1},{1,0},{2,3},{3,2},{4,5},{5,4},{6,7},{7,6},{8,9},{9,8},{10,11... | collective-permute-start | bytes 786440 | tf_op jit(solution)/shard_map/ppermute | solution.py:523
  33.3 16.4 %collective-permute-start.8 = (bf16[2,768,128]{2,1,0:T(8,128)(2,1)}, bf16[2,768,128]{2,1,0:T(8,128)(2,1)S(1)}, u32[]{:S(2)}, u32[]{:S(2)}) collective-permute-start(bf16[2,768,128]{2,1,0:T(8,128)(2,1)} %get-tuple-element.44), channel_id=1, source_target_pairs={{0,1},{1,0},{2,3},{3,2},{4,5},{5,4},{6,7},{7,6},{8,9},{9,8},{10,11... | collective-permute-start | bytes 1179656 | tf_op jit(solution)/shard_map/ppermute | solution.py:523
  33.8 15.9 %collective-permute-start.9 = (bf16[2,768,128]{2,1,0:T(8,128)(2,1)}, bf16[2,768,128]{2,1,0:T(8,128)(2,1)S(1)}, u32[]{:S(2)}, u32[]{:S(2)}) collective-permute-start(bf16[2,768,128]{2,1,0:T(8,128)(2,1)} %get-tuple-element.45), channel_id=1, source_target_pairs={{0,16},{1,2},{2,1},{3,4},{4,3},{5,6},{6,5},{7,8},{8,7},{9,10},{10,... | collective-permute-start | bytes 1179656 | tf_op jit(solution)/shard_map/ppermute | solution.py:523
  35.6 23.8 %all-to-all-start = ((bf16[64,16,128]{2,1,0:T(8,128)(2,1)}), bf16[64,16,128]{2,1,0:T(8,128)(2,1)S(1)}, u32[]{:S(2)}, u32[]{:S(2)}) async-start(bf16[64,16,128]{2,1,0:T(8,128)(2,1)} %add_convert_fusion), calls=%async_computation | async-start | bytes 524288 | tf_op jit(solution)/shard_map/all_to_all | solution.py:545
  51.1 14.0 %collective-permute-start.10 = (bf16[2,4,128,128]{3,2,1,0:T(8,128)(2,1)S(1)}, bf16[2,4,128,128]{3,2,1,0:T(8,128)(2,1)S(1)}, u32[]{:S(2)}, u32[]{:S(2)}) collective-permute-start(bf16[2,4,128,128]{3,2,1,0:T(8,128)(2,1)S(1)} %get-tuple-element.46), channel_id=1, source_target_pairs={{0,16},{1,17},{2,18},{3,19},{4,20},{5,21},{6,22},{7,23},{8,24},{9,... | collective-permute-start | bytes 786440 | tf_op jit(solution)/shard_map/ppermute | solution.py:523
  52.2 12.9 %collective-permute-start.11 = (bf16[2,4,128,128]{3,2,1,0:T(8,128)(2,1)S(1)}, bf16[2,4,128,128]{3,2,1,0:T(8,128)(2,1)S(1)}, u32[]{:S(2)}, u32[]{:S(2)}) collective-permute-start(bf16[2,4,128,128]{3,2,1,0:T(8,128)(2,1)S(1)} %get-tuple-element.47), channel_id=1, source_target_pairs={{0,1},{1,0},{2,3},{3,2},{4,5},{5,4},{6,7},{7,6},{8,9},{9,8},{10,11... | collective-permute-start | bytes 786440 | tf_op jit(solution)/shard_map/ppermute | solution.py:523
  60.3 14.0 %all-to-all-start.1 = ((bf16[64,16,128]{2,1,0:T(8,128)(2,1)}), bf16[64,16,128]{2,1,0:T(8,128)(2,1)S(1)}, u32[]{:S(2)}, u32[]{:S(2)}) async-start(bf16[64,16,128]{2,1,0:T(8,128)(2,1)} %peer_sum.1), calls=%async_computation.1 | async-start | bytes 524288 | tf_op jit(solution)/shard_map/all_to_all | solution.py:550
  74.3 4.3 %collective-permute-start.12 = (bf16[64,16,128]{2,1,0:T(8,128)(2,1)S(1)}, bf16[64,16,128]{2,1,0:T(8,128)(2,1)S(1)}, u32[]{:S(2)}, u32[]{:S(2)}) collective-permute-start(bf16[64,16,128]{2,1,0:T(8,128)(2,1)S(1)} %all-to-all-done.1.part_ref), channel_id=1, source_target_pairs={{0,1},{1,0},{2,3},{3,2},{4,5},{5,4},{6,7},{7,6},{8,9},{9,8},{10,11... | collective-permute-start | bytes 786440 | tf_op jit(solution)/shard_map/ppermute | solution.py:523

commit v9 on v8

--- a/solution.py
+++ b/solution.py
@@ -47,7 +47,7 @@
     return jnp.dot(a, b, preferred_element_type=F32)
 
 
-def margins_kernel(obj, row_a, edge_b, row_b, col_a, col_b, sems):
+def margins_kernel(obj, edge_b, row_a, col_b, col_a, row_b, sems):
     tile = obj.shape[1]
     row_odd, core = place()
     copies = []
@@ -75,7 +75,7 @@
     col = jax.ShapeDtypeStruct((2, tile, HALO), BF16)
     return pl.pallas_call(
         margins_kernel,
-        out_shape=(row, edge, inside, col, col),
+        out_shape=(edge, row, col, col, inside),
         in_specs=[pl.BlockSpec(memory_space=pltpu.HBM)],
         out_specs=(VM,) * 5,
         scratch_shapes=[pltpu.SemaphoreType.DMA((6,))],
@@ -118,7 +118,7 @@
 
 
 def frames_kernel(
-    count_ref, pos_ref, row_a_ref, edge_b_ref, row_b_ref, col_a_ref, col_b_ref, cor_a_ref, cor_b_ref,
+    count_ref, pos_ref, edge_b_ref, row_a_ref, col_b_ref, col_a_ref, row_b_ref, cor_b_ref, cor_a_ref,
     ext_ref, grad_ref, pgrad_ref, probe_ref, amp_ref, tables_ref,
     ext, grad, pgrad, obj_hbm, strip_a_hbm, strip_b_hbm, out_a_hbm, out_b_hbm, keep_out, send,
     patch, waves, chi, firsts, backs, out_a, out_b, sems,
@@ -525,18 +525,19 @@
 
 def shards(object_field, probe_modes, measured_amp, scan_positions, frame_counts):
     slots = measured_amp.shape[2]
-    to_row_a, to_edge_b, to_row_b, to_col_a, to_col_b = margins(object_field)
+    to_edge_b, to_row_a, to_col_b, to_col_a, to_row_b = margins(object_field)
     edge_b = trade(to_edge_b, "row", 1)
     row_a = trade(to_row_a, "row", 0)
-    row_b = trade(to_row_b, "row", 1)
     col_b = trade(to_col_b, COL, 1)
     col_a = trade(to_col_a, COL, 0)
+    to_row_b, col_a = lax.optimization_barrier((to_row_b, col_a))
+    row_b = trade(to_row_b, "row", 1)
     to_cor_a, to_cor_b = corners(row_a, edge_b)
     cor_b = trade(to_cor_b, COL, 1)
     cor_a = trade(to_cor_a, COL, 0)
     prepared = prepare(object_field, probe_modes, measured_amp[0, 0], fourier_tables(probe_modes.shape[-1]))
     _, _, _, part, strip_a, strip_b, out_a, out_b, keep, send = run_frames(
-        frame_counts, scan_positions, (row_a, edge_b, row_b, col_a, col_b, cor_a, cor_b), prepared
+        frame_counts, scan_positions, (edge_b, row_a, col_b, col_a, row_b, cor_b, cor_a), prepared
     )
     scale = 1.0 / math.sqrt(lax.axis_size("row") * lax.axis_size(COL) * slots)
     pair = (keep + trade(send, COL, 0).astype(F32)).astype(BF16)

time: 79.6 us -> 81.9 us (1.029)
  starting transfers between devices: 32.3 us -> 36.4 us
  waiting for transfers between devices: 19.2 us -> 17.2 us
    all_to_all x1, starting transfers between devices: 14.1 us -> 17 us  [shards(): peers = lax.all_to_all(pair, PEERS, 0, 0, tiled=True)]
    ppermute x13, waiting for transfers between devices: 6.16 us -> 3.97 us  [trade(): return lax.ppermute(value, ('row',) + COL, pairs)]
    ppermute x13, starting transfers between devices: 13.4 us -> 14.6 us  [trade(): return lax.ppermute(value, ('row',) + COL, pairs)]
  transfers between devices with their start and end apart: 15 -> 15, of which waited for: 6 -> 5; matrix products, arithmetic and copies ran while one was open for 1% -> 1% of each run, Pallas kernels for 10% -> 9%
where the time goes in v9:
time: 81.9 us; the launch traced here: 81.7 us
  starting transfers between devices  36.4 us (44%)
  Pallas kernels  25.8 us (32%)
  waiting for transfers between devices  17.2 us (21%)
  between operations  1.43 us (2%)
    all_to_all x1, starting transfers between devices, shards(): peers = lax.all_to_all(pair, PEERS, 0, 0, tiled=True)  17 us
    pallas_call x1, Pallas kernels, run_frames(): pl.pallas_call(frames_kernel, out_shape=(pltpu.VMEM(ext.shape, F32), pltp...  15.9 us
    ppermute x13, starting transfers between devices, trade(): return lax.ppermute(value, ('row',) + COL, pairs)  14.6 us
    all_to_all x1, waiting for transfers between devices, shards(): mine = lax.all_to_all(peer_sum(peers, scale), PEERS, 0, 0, tiled=True)  6.7 us
    all_to_all x1, waiting for transfers between devices, shards(): peers = lax.all_to_all(pair, PEERS, 0, 0, tiled=True)  6.57 us
    all_to_all x1, starting transfers between devices, shards(): mine = lax.all_to_all(peer_sum(peers, scale), PEERS, 0, 0, tiled=True)  4.93 us
    ppermute x13, waiting for transfers between devices, trade(): return lax.ppermute(value, ('row',) + COL, pairs)  3.97 us
    pallas_call x1, Pallas kernels, finish_object(): pl.pallas_call(object_kernel, out_shape=pltpu.HBM((2, tile, nblk * LANES)...  2.48 us
  transfers between devices with their start and end apart: 15, of which 5 were waited for; matrix products, arithmetic and copies ran while one was open for 1% of the time, Pallas kernels for 9%

profile of v9, /device:TPU:1, one launch (start us, length us, event | category | flops | bytes accessed | tf_op | source)
XLA Modules:
  0.0 81.7 jit_solution(7549651928362935011)
XLA Ops:
  0.6 1.3 %margins.1 = (bf16[4,128,128]{2,1,0:T(8,128)(2,1)S(1)}, bf16[2,128,512]{2,1,0:T(8,128)(2,1)S(1)}, bf16[2,512,128]{2,1,0:T(8,128)(2,1)S(1)}, bf16[2,512,128]{2,1,0:T(8,128)(2,1)S(1)}, bf16[2,128,256]{2,1,0:T(8,128)(2,1)S(1)}) custom-call(bf16[2,512,512]{2,1,0:T(8,128)(2,1)} %mid_hbm.1), custom_call_target="tpu_custom_call" | custom-call | tf_op jit(solution)/shard_map/margins/pallas_call | solution.py:76
  2.0 2.5 %collective-permute-start.1 = (bf16[2,128,512]{2,1,0:T(8,128)(2,1)S(1)}, bf16[2,128,512]{2,1,0:T(8,128)(2,1)S(1)}, u32[]{:S(2)}, u32[]{:S(2)}) collective-permute-start(bf16[2,128,512]{2,1,0:T(8,128)(2,1)S(1)} %get-tuple-element.30), channel_id=1, source_target_pairs={{0,16},{1,17},{2,18},{3,19},{4,20},{5,21},{6,22},{7,23},{8,24},{9,... | collective-permute-start | bytes 786440 | tf_op jit(solution)/shard_map/ppermute | solution.py:523
  4.5 1.0 %collective-permute-start.3 = (bf16[2,512,128]{2,1,0:T(8,128)(2,1)S(1)}, bf16[2,512,128]{2,1,0:T(8,128)(2,1)S(1)}, u32[]{:S(2)}, u32[]{:S(2)}) collective-permute-start(bf16[2,512,128]{2,1,0:T(8,128)(2,1)S(1)} %get-tuple-element.33), channel_id=1, source_target_pairs={{0,1},{1,0},{2,3},{3,2},{4,5},{5,4},{6,7},{7,6},{8,9},{9,8},{10,11... | collective-permute-start | bytes 786440 | tf_op jit(solution)/shard_map/ppermute | solution.py:523
  5.5 1.6 %collective-permute-start.2 = (bf16[2,512,128]{2,1,0:T(8,128)(2,1)S(1)}, bf16[2,512,128]{2,1,0:T(8,128)(2,1)S(1)}, u32[]{:S(2)}, u32[]{:S(2)}) collective-permute-start(bf16[2,512,128]{2,1,0:T(8,128)(2,1)S(1)} %get-tuple-element.31), channel_id=1, source_target_pairs={{0,16},{1,2},{2,1},{3,4},{4,3},{5,6},{6,5},{7,8},{8,7},{9,10},{10,... | collective-permute-start | bytes 786440 | tf_op jit(solution)/shard_map/ppermute | solution.py:523
  7.1 3.4 %collective-permute-done.1.row_a.row_a_ref = bf16[2,128,512]{2,1,0:T(8,128)(2,1)S(1)} collective-permute-done((bf16[2,128,512]{2,1,0:T(8,128)(2,1)S(1)}, bf16[2,128,512]{2,1,0:T(8,128)(2,1)S(1)}, u32[]{:S(2)}, u32[]{:S(2)}) %collective-permute-start.1) | collective-permute-done | bytes 262176 | tf_op jit(solution)/shard_map/ppermute | solution.py:523
  10.6 2.4 %collective-permute-start.5 = (bf16[4,128,128]{2,1,0:T(8,128)(2,1)S(1)}, bf16[4,128,128]{2,1,0:T(8,128)(2,1)S(1)}, u32[]{:S(2)}, u32[]{:S(2)}) collective-permute-start(bf16[4,128,128]{2,1,0:T(8,128)(2,1)S(1)} %get-tuple-element.36), channel_id=1, source_target_pairs={{0,16},{1,2},{2,1},{3,4},{4,3},{5,6},{6,5},{7,8},{8,7},{9,10},{10,... | collective-permute-start | bytes 393224 | tf_op jit(solution)/shard_map/ppermute | solution.py:523
  13.0 0.6 collective-permute-start.6
  13.6 2.2 %prepare.1 = (f32[2,6,768,128]{3,2,1,0:T(8,128)S(1)}, f32[2,6,768,128]{3,2,1,0:T(8,128)S(1)}, f32[2,2,256,256]{3,2,1,0:T(8,128)S(1)}, f32[2,2,256,256]{3,2,1,0:T...) custom-call(bf16[2,512,512]{2,1,0:T(8,128)(2,1)} %mid_hbm.1, ...), custom_call_target="tpu_custom_call" | custom-call | flops 5000000000 | tf_op jit(solution)/shard_map/prepare/pallas_call | solution.py:289
  16.6 15.9 %frames.1 = (f32[2,6,768,128]{3,2,1,0:T(8,128)S(1)}, f32[2,6,768,128]{3,2,1,0:T(8,128)S(1)}, f32[2,2,256,256]{3,2,1,0:T(8,128)S(1)}, f32[2,4,512,128]{3,2,1,0:T(...) custom-call(s32[1,1]{1,0:T(1,128)S(6)} %copy.17.count_ref, ...), custom_call_target="tpu_custom_call", output_to_operand_aliasing={{0}: (9, {}), {1}: (10, {}), {2}: (11, {})} | custom-call | tf_op jit(solution)/shard_map/frames/pallas_call | solution.py:311
  32.5 0.6 collective-permute-start.7
  33.2 0.9 %collective-permute-start.9 = (bf16[2,768,128]{2,1,0:T(8,128)(2,1)}, bf16[2,768,128]{2,1,0:T(8,128)(2,1)S(1)}, u32[]{:S(2)}, u32[]{:S(2)}) collective-permute-start(bf16[2,768,128]{2,1,0:T(8,128)(2,1)} %get-tuple-element.49), channel_id=1, source_target_pairs={{0,16},{1,2},{2,1},{3,4},{4,3},{5,6},{6,5},{7,8},{8,7},{9,10},{10,... | collective-permute-start | bytes 1179656 | tf_op jit(solution)/shard_map/ppermute | solution.py:523
  34.3 0.8 add_convert_fusion
  35.1 17.0 %all-to-all-start = ((bf16[64,16,128]{2,1,0:T(8,128)(2,1)}), bf16[64,16,128]{2,1,0:T(8,128)(2,1)S(1)}, u32[]{:S(2)}, u32[]{:S(2)}) async-start(bf16[64,16,128]{2,1,0:T(8,128)(2,1)} %add_convert_fusion), calls=%async_computation | async-start | bytes 524288 | tf_op jit(solution)/shard_map/all_to_all | solution.py:546
  52.1 1.3 %row_margins.1 = (bf16[2,4,128,128]{3,2,1,0:T(8,128)(2,1)S(1)}, bf16[2,4,128,128]{3,2,1,0:T(8,128)(2,1)S(1)}) custom-call(f32[2,4,128,128]{3,2,1,0:T(8,128)} %get-tuple-element.46.strip_a_hbm, f32[2,4,128,128]{3,2,1,0:T(8,128)} %get-tuple-element.47.strip_b_hbm, bf16[2,768,128]{2,1,0:T(8,128)(2,1)S(1)} %collective-permute-done.8.got_a_ref.col_a_ref, ...), custom_call_target="tpu_custom_call" | custom-call | flops 5000000000 | tf_op jit(solution)/shard_map/row_margins/pallas_call | solution.py:378
  53.4 1.1 %collective-permute-start.10 = (bf16[2,4,128,128]{3,2,1,0:T(8,128)(2,1)S(1)}, bf16[2,4,128,128]{3,2,1,0:T(8,128)(2,1)S(1)}, u32[]{:S(2)}, u32[]{:S(2)}) collective-permute-start(bf16[2,4,128,128]{3,2,1,0:T(8,128)(2,1)S(1)} %get-tuple-element.50), channel_id=1, source_target_pairs={{0,16},{1,17},{2,18},{3,19},{4,20},{5,21},{6,22},{7,23},{8,24},{9,... | collective-permute-start | bytes 786440 | tf_op jit(solution)/shard_map/ppermute | solution.py:523
  54.5 0.8 collective-permute-start.11
  55.3 6.6 %all-to-all-done.got_ref = bf16[64,16,128]{2,1,0:T(8,128)(2,1)S(1)} async-done(((bf16[64,16,128]{2,1,0:T(8,128)(2,1)}), bf16[64,16,128]{2,1,0:T(8,128)(2,1)S(1)}, u32[]{:S(2)}, u32[]{:S(2)}) %all-to-all-start) | async-done | bytes 262176 | tf_op jit(solution)/shard_map/all_to_all | solution.py:546
  61.8 0.8 peer_sum.1
  62.6 4.9 %all-to-all-start.1 = ((bf16[64,16,128]{2,1,0:T(8,128)(2,1)}), bf16[64,16,128]{2,1,0:T(8,128)(2,1)S(1)}, u32[]{:S(2)}, u32[]{:S(2)}) async-start(bf16[64,16,128]{2,1,0:T(8,128)(2,1)} %peer_sum.1), calls=%async_computation.1 | async-start | bytes 524288 | tf_op jit(solution)/shard_map/all_to_all | solution.py:551
  67.6 2.5 %finish_object.1 = f32[2,512,512]{2,1,0:T(8,128)} custom-call(f32[2,4,512,128]{3,2,1,0:T(8,128)} %get-tuple-element.53.part_hbm, bf16[2,768,128]{2,1,0:T(8,128)(2,1)S(1)} %collective-permute-done.8.got_a_ref.col_a_ref, bf16[2,768,128]{2,1,0:T(8,128)(2,1)S(1)} %collective-permute-done.9.got_b_ref.col_b_ref, ...), custom_call_target="tpu_custom_call" | custom-call | flops 5000000000 | tf_op jit(solution)/shard_map/finish_object/pallas_call | solution.py:443
  70.1 6.7 %all-to-all-done.1.part_ref = bf16[64,16,128]{2,1,0:T(8,128)(2,1)S(1)} async-done(((bf16[64,16,128]{2,1,0:T(8,128)(2,1)}), bf16[64,16,128]{2,1,0:T(8,128)(2,1)S(1)}, u32[]{:S(2)}, u32[]{:S(2)}) %all-to-all-start.1) | async-done | bytes 262176 | tf_op jit(solution)/shard_map/all_to_all | solution.py:551
  76.8 2.9 %collective-permute-start.12 = (bf16[64,16,128]{2,1,0:T(8,128)(2,1)S(1)}, bf16[64,16,128]{2,1,0:T(8,128)(2,1)S(1)}, u32[]{:S(2)}, u32[]{:S(2)}) collective-permute-start(bf16[64,16,128]{2,1,0:T(8,128)(2,1)S(1)} %all-to-all-done.1.part_ref), channel_id=1, source_target_pairs={{0,1},{1,0},{2,3},{3,2},{4,5},{5,4},{6,7},{7,6},{8,9},{9,8},{10,11... | collective-permute-start | bytes 786440 | tf_op jit(solution)/shard_map/ppermute | solution.py:523
  79.7 0.8 %finish_mine.1.so_far_hbm = f32[2,2,256,256]{3,2,1,0:T(8,128)} custom-call(bf16[64,16,128]{2,1,0:T(8,128)(2,1)S(1)} %all-to-all-done.1.part_ref), custom_call_target="tpu_custom_call" | custom-call | flops 5000000000 | tf_op jit(solution)/shard_map/finish_mine/pallas_call | solution.py:485
  80.8 0.8 %finish_theirs.1 = f32[2,2,256,256]{3,2,1,0:T(8,128)} custom-call(bf16[64,16,128]{2,1,0:T(8,128)(2,1)S(1)} %collective-permute-done.12.part_ref, f32[2,2,256,256]{3,2,1,0:T(8,128)} %finish_mine.1.so_far_hbm), custom_call_target="tpu_custom_call", output_to_operand_aliasing={{}: (1, {})} | custom-call | tf_op jit(solution)/shard_map/finish_theirs/pallas_call | solution.py:499
  (18 shorter events, 0.7 us)
Async XLA Ops:
  2.0 8.6 %collective-permute-start.1 = (bf16[2,128,512]{2,1,0:T(8,128)(2,1)S(1)}, bf16[2,128,512]{2,1,0:T(8,128)(2,1)S(1)}, u32[]{:S(2)}, u32[]{:S(2)}) collective-permute-start(bf16[2,128,512]{2,1,0:T(8,128)(2,1)S(1)} %get-tuple-element.30), channel_id=1, source_target_pairs={{0,16},{1,17},{2,18},{3,19},{4,20},{5,21},{6,22},{7,23},{8,24},{9,... | collective-permute-start | bytes 786440 | tf_op jit(solution)/shard_map/ppermute | solution.py:523
  4.5 9.1 %collective-permute-start.3 = (bf16[2,512,128]{2,1,0:T(8,128)(2,1)S(1)}, bf16[2,512,128]{2,1,0:T(8,128)(2,1)S(1)}, u32[]{:S(2)}, u32[]{:S(2)}) collective-permute-start(bf16[2,512,128]{2,1,0:T(8,128)(2,1)S(1)} %get-tuple-element.33), channel_id=1, source_target_pairs={{0,1},{1,0},{2,3},{3,2},{4,5},{5,4},{6,7},{7,6},{8,9},{9,8},{10,11... | collective-permute-start | bytes 786440 | tf_op jit(solution)/shard_map/ppermute | solution.py:523
  5.5 1.6 %collective-permute-start = (bf16[4,128,128]{2,1,0:T(8,128)(2,1)S(1)}, bf16[4,128,128]{2,1,0:T(8,128)(2,1)S(1)}, u32[]{:S(2)}, u32[]{:S(2)}) collective-permute-start(bf16[4,128,128]{2,1,0:T(8,128)(2,1)S(1)} %get-tuple-element.29), channel_id=1, source_target_pairs={{0,1},{1,0},{2,3},{3,2},{4,5},{5,4},{6,7},{7,6},{8,9},{9,8},{10,11... | collective-permute-start | bytes 393224 | tf_op jit(solution)/shard_map/ppermute | solution.py:523
  5.5 11.0 %collective-permute-start.2 = (bf16[2,512,128]{2,1,0:T(8,128)(2,1)S(1)}, bf16[2,512,128]{2,1,0:T(8,128)(2,1)S(1)}, u32[]{:S(2)}, u32[]{:S(2)}) collective-permute-start(bf16[2,512,128]{2,1,0:T(8,128)(2,1)S(1)} %get-tuple-element.31), channel_id=1, source_target_pairs={{0,16},{1,2},{2,1},{3,4},{4,3},{5,6},{6,5},{7,8},{8,7},{9,10},{10,... | collective-permute-start | bytes 786440 | tf_op jit(solution)/shard_map/ppermute | solution.py:523
  10.6 6.0 %collective-permute-start.5 = (bf16[4,128,128]{2,1,0:T(8,128)(2,1)S(1)}, bf16[4,128,128]{2,1,0:T(8,128)(2,1)S(1)}, u32[]{:S(2)}, u32[]{:S(2)}) collective-permute-start(bf16[4,128,128]{2,1,0:T(8,128)(2,1)S(1)} %get-tuple-element.36), channel_id=1, source_target_pairs={{0,16},{1,2},{2,1},{3,4},{4,3},{5,6},{6,5},{7,8},{8,7},{9,10},{10,... | collective-permute-start | bytes 393224 | tf_op jit(solution)/shard_map/ppermute | solution.py:523
  13.0 3.6 %collective-permute-start.6 = (bf16[4,128,128]{2,1,0:T(8,128)(2,1)S(1)}, bf16[4,128,128]{2,1,0:T(8,128)(2,1)S(1)}, u32[]{:S(2)}, u32[]{:S(2)}) collective-permute-start(bf16[4,128,128]{2,1,0:T(8,128)(2,1)S(1)} %get-tuple-element.37), channel_id=1, source_target_pairs={{0,1},{1,0},{2,3},{3,2},{4,5},{5,4},{6,7},{7,6},{8,9},{9,8},{10,11... | collective-permute-start | bytes 393224 | tf_op jit(solution)/shard_map/ppermute | solution.py:523
  13.6 2.9 %collective-permute-start.4 = (bf16[2,128,256]{2,1,0:T(8,128)(2,1)S(1)}, bf16[2,128,256]{2,1,0:T(8,128)(2,1)S(1)}, u32[]{:S(2)}, u32[]{:S(2)}) collective-permute-start(bf16[2,128,256]{2,1,0:T(8,128)(2,1)S(1)} %get-tuple-element.35), channel_id=1, source_target_pairs={{0,1},{1,0},{2,3},{3,2},{4,5},{5,4},{6,7},{7,6},{8,9},{9,8},{10,11... | collective-permute-start | bytes 393224 | tf_op jit(solution)/shard_map/ppermute | solution.py:523
  13.6 2.9 %copy-start = (s32[1,1,2,8]{3,2,1,0:T(2,128)S(1)}, s32[1,1,2,8]{3,2,1,0:T(2,128)}, u32[]{:S(2)}) copy-start(s32[1,1,2,8]{3,2,1,0:T(2,128)} %pos_ref.1) | copy-start | bytes 196
  32.5 1.8 %collective-permute-start.7 = (bf16[64,16,128]{2,1,0:T(8,128)(2,1)S(1)}, bf16[64,16,128]{2,1,0:T(8,128)(2,1)S(1)}, u32[]{:S(2)}, u32[]{:S(2)}) collective-permute-start(bf16[64,16,128]{2,1,0:T(8,128)(2,1)S(1)} %get-tuple-element.45), channel_id=1, source_target_pairs={{0,1},{1,0},{2,3},{3,2},{4,5},{5,4},{6,7},{7,6},{8,9},{9,8},{10,11... | collective-permute-start | bytes 786440 | tf_op jit(solution)/shard_map/ppermute | solution.py:523
  33.1 18.9 %collective-permute-start.8 = (bf16[2,768,128]{2,1,0:T(8,128)(2,1)}, bf16[2,768,128]{2,1,0:T(8,128)(2,1)S(1)}, u32[]{:S(2)}, u32[]{:S(2)}) collective-permute-start(bf16[2,768,128]{2,1,0:T(8,128)(2,1)} %get-tuple-element.48), channel_id=1, source_target_pairs={{0,1},{1,0},{2,3},{3,2},{4,5},{5,4},{6,7},{7,6},{8,9},{9,8},{10,11... | collective-permute-start | bytes 1179656 | tf_op jit(solution)/shard_map/ppermute | solution.py:523
  33.2 18.8 %collective-permute-start.9 = (bf16[2,768,128]{2,1,0:T(8,128)(2,1)}, bf16[2,768,128]{2,1,0:T(8,128)(2,1)S(1)}, u32[]{:S(2)}, u32[]{:S(2)}) collective-permute-start(bf16[2,768,128]{2,1,0:T(8,128)(2,1)} %get-tuple-element.49), channel_id=1, source_target_pairs={{0,16},{1,2},{2,1},{3,4},{4,3},{5,6},{6,5},{7,8},{8,7},{9,10},{10,... | collective-permute-start | bytes 1179656 | tf_op jit(solution)/shard_map/ppermute | solution.py:523
  35.1 26.8 %all-to-all-start = ((bf16[64,16,128]{2,1,0:T(8,128)(2,1)}), bf16[64,16,128]{2,1,0:T(8,128)(2,1)S(1)}, u32[]{:S(2)}, u32[]{:S(2)}) async-start(bf16[64,16,128]{2,1,0:T(8,128)(2,1)} %add_convert_fusion), calls=%async_computation | async-start | bytes 524288 | tf_op jit(solution)/shard_map/all_to_all | solution.py:546
  53.4 14.2 %collective-permute-start.10 = (bf16[2,4,128,128]{3,2,1,0:T(8,128)(2,1)S(1)}, bf16[2,4,128,128]{3,2,1,0:T(8,128)(2,1)S(1)}, u32[]{:S(2)}, u32[]{:S(2)}) collective-permute-start(bf16[2,4,128,128]{3,2,1,0:T(8,128)(2,1)S(1)} %get-tuple-element.50), channel_id=1, source_target_pairs={{0,16},{1,17},{2,18},{3,19},{4,20},{5,21},{6,22},{7,23},{8,24},{9,... | collective-permute-start | bytes 786440 | tf_op jit(solution)/shard_map/ppermute | solution.py:523
  54.5 13.1 %collective-permute-start.11 = (bf16[2,4,128,128]{3,2,1,0:T(8,128)(2,1)S(1)}, bf16[2,4,128,128]{3,2,1,0:T(8,128)(2,1)S(1)}, u32[]{:S(2)}, u32[]{:S(2)}) collective-permute-start(bf16[2,4,128,128]{3,2,1,0:T(8,128)(2,1)S(1)} %get-tuple-element.51), channel_id=1, source_target_pairs={{0,1},{1,0},{2,3},{3,2},{4,5},{5,4},{6,7},{7,6},{8,9},{9,8},{10,11... | collective-permute-start | bytes 786440 | tf_op jit(solution)/shard_map/ppermute | solution.py:523
  62.6 14.1 %all-to-all-start.1 = ((bf16[64,16,128]{2,1,0:T(8,128)(2,1)}), bf16[64,16,128]{2,1,0:T(8,128)(2,1)S(1)}, u32[]{:S(2)}, u32[]{:S(2)}) async-start(bf16[64,16,128]{2,1,0:T(8,128)(2,1)} %peer_sum.1), calls=%async_computation.1 | async-start | bytes 524288 | tf_op jit(solution)/shard_map/all_to_all | solution.py:551
  76.8 4.0 %collective-permute-start.12 = (bf16[64,16,128]{2,1,0:T(8,128)(2,1)S(1)}, bf16[64,16,128]{2,1,0:T(8,128)(2,1)S(1)}, u32[]{:S(2)}, u32[]{:S(2)}) collective-permute-start(bf16[64,16,128]{2,1,0:T(8,128)(2,1)S(1)} %all-to-all-done.1.part_ref), channel_id=1, source_target_pairs={{0,1},{1,0},{2,3},{3,2},{4,5},{5,4},{6,7},{7,6},{8,9},{9,8},{10,11... | collective-permute-start | bytes 786440 | tf_op jit(solution)/shard_map/ppermute | solution.py:523

commit v10 on v8

--- a/solution.py
+++ b/solution.py
@@ -47,40 +47,54 @@
     return jnp.dot(a, b, preferred_element_type=F32)
 
 
-def margins_kernel(obj, row_a, edge_b, row_b, col_a, col_b, sems):
-    tile = obj.shape[1]
-    row_odd, core = place()
-    copies = []
-
-    def put(src, dst):
-        copies.append(pltpu.make_async_copy(src, dst, sems.at[len(copies)]))
-        copies[-1].start()
-
-    rows_b = pl.ds(pl.multiple_of(row_odd * (tile - HALO), HALO), HALO)
-    put(obj.at[:, rows_b, 0:HALO], edge_b.at[0:2])
-    put(obj.at[:, rows_b, tile - HALO :], edge_b.at[2:4])
-    put(obj.at[:, pl.ds(pl.multiple_of((1 - row_odd) * (tile - HALO), HALO), HALO), :], row_a)
-    put(obj.at[:, rows_b, HALO : tile - HALO], row_b)
-    for col, at in ((col_b, core), (col_a, 1 - core)):
-        put(obj.at[:, :, pl.ds(pl.multiple_of(at * (tile - HALO), HALO), HALO)], col)
+def cut(pairs, sems):
+    copies = [pltpu.make_async_copy(src, dst, sems.at[i]) for i, (src, dst) in enumerate(pairs)]
+    for copy in copies:
+        copy.start()
     for copy in copies:
         copy.wait()
 
 
-def margins(obj):
+def start_at(tile, odd):
+    return pl.ds(pl.multiple_of(odd * (tile - HALO), HALO), HALO)
+
+
+def row_margins_kernel(obj, row_a, edge_b, row_b, sems):
     tile = obj.shape[1]
-    row = jax.ShapeDtypeStruct((2, HALO, tile), BF16)
-    edge = jax.ShapeDtypeStruct((4, HALO, HALO), BF16)
-    inside = jax.ShapeDtypeStruct((2, HALO, tile - 2 * HALO), BF16)
-    col = jax.ShapeDtypeStruct((2, tile, HALO), BF16)
-    return pl.pallas_call(
-        margins_kernel,
-        out_shape=(row, edge, inside, col, col),
+    row_odd = lax.axis_index("row") % 2
+    rows = start_at(tile, row_odd)
+    cut(
+        (
+            (obj.at[:, rows, 0:HALO], edge_b.at[0:2]),
+            (obj.at[:, rows, tile - HALO :], edge_b.at[2:4]),
+            (obj.at[:, rows, HALO : tile - HALO], row_b),
+            (obj.at[:, start_at(tile, 1 - row_odd), :], row_a),
+        ),
+        sems,
+    )
+
+
+def col_margins_kernel(obj, col_a, col_b, sems):
+    tile = obj.shape[1]
+    core = lax.axis_index("core")
+    cut(
+        (
+            (obj.at[:, :, start_at(tile, core)], col_b),
+            (obj.at[:, :, start_at(tile, 1 - core)], col_a),
+        ),
+        sems,
+    )
+
+
+def margins(kernel, name, obj, *shapes):
+    return pl.pallas_call(
+        kernel,
+        out_shape=tuple(jax.ShapeDtypeStruct(shape, BF16) for shape in shapes),
         in_specs=[pl.BlockSpec(memory_space=pltpu.HBM)],
-        out_specs=(VM,) * 5,
-        scratch_shapes=[pltpu.SemaphoreType.DMA((6,))],
-        compiler_params=pltpu.CompilerParams(vmem_limit_bytes=8 * 1024 * 1024),
-        name="margins",
+        out_specs=(VM,) * len(shapes),
+        scratch_shapes=[pltpu.SemaphoreType.DMA((4,))],
+        compiler_params=pltpu.CompilerParams(vmem_limit_bytes=8 * 1024 * 1024),
+        name=name,
     )(pltpu.with_memory_space_constraint(obj, pltpu.HBM))
 
 
@@ -525,7 +539,12 @@
 
 def shards(object_field, probe_modes, measured_amp, scan_positions, frame_counts):
     slots = measured_amp.shape[2]
-    to_row_a, to_edge_b, to_row_b, to_col_a, to_col_b = margins(object_field)
+    tile = object_field.shape[1]
+    to_row_a, to_edge_b, to_row_b = margins(
+        row_margins_kernel, "halo_rows", object_field, (2, HALO, tile), (4, HALO, HALO), (2, HALO, tile - 2 * HALO)
+    )
+    rest, to_row_a, to_edge_b, to_row_b = lax.optimization_barrier((object_field, to_row_a, to_edge_b, to_row_b))
+    to_col_a, to_col_b = margins(col_margins_kernel, "halo_cols", rest, (2, tile, HALO), (2, tile, HALO))
     edge_b = trade(to_edge_b, "row", 1)
     row_a = trade(to_row_a, "row", 0)
     row_b = trade(to_row_b, "row", 1)

time: 79.6 us -> 79.8 us (level)
  waiting for transfers between devices: 19.2 us -> 18 us
  Pallas kernels: 25.7 us -> 26.6 us
    all_to_all x1, starting transfers between devices: 14.1 us -> 13.1 us  [shards(): peers = lax.all_to_all(pair, PEERS, 0, 0, tiled=True)]
    pallas_call x1 -> x2, Pallas kernels: 1.33 us -> 2.22 us  [margins(): pl.pallas_call(kernel, out_shape=tuple((jax.ShapeDtypeStruct(shape, BF16)...]
  transfers between devices with their start and end apart: 15 -> 15, of which waited for: 6 -> 6; matrix products, arithmetic and copies ran while one was open for 1% -> 1% of each run, Pallas kernels for 10% -> 11%
where the time goes in v10:
time: 79.8 us; the launch traced here: 79.1 us
  starting transfers between devices  32.2 us (40%)
  Pallas kernels  26.6 us (33%)
  waiting for transfers between devices  18 us (23%)
  between operations  1.43 us (2%)
    pallas_call x1, Pallas kernels, run_frames(): pl.pallas_call(frames_kernel, out_shape=(pltpu.VMEM(ext.shape, F32), pltp...  15.9 us
    ppermute x13, starting transfers between devices, trade(): return lax.ppermute(value, ('row',) + COL, pairs)  13.9 us
    all_to_all x1, starting transfers between devices, shards(): peers = lax.all_to_all(pair, PEERS, 0, 0, tiled=True)  13.1 us
    all_to_all x1, waiting for transfers between devices, shards(): mine = lax.all_to_all(peer_sum(peers, scale), PEERS, 0, 0, tiled=True)  6.7 us
    ppermute x13, waiting for transfers between devices, trade(): return lax.ppermute(value, ('row',) + COL, pairs)  5.77 us
    all_to_all x1, waiting for transfers between devices, shards(): peers = lax.all_to_all(pair, PEERS, 0, 0, tiled=True)  5.56 us
    all_to_all x1, starting transfers between devices, shards(): mine = lax.all_to_all(peer_sum(peers, scale), PEERS, 0, 0, tiled=True)  5.17 us
    pallas_call x1, Pallas kernels, finish_object(): pl.pallas_call(object_kernel, out_shape=pltpu.HBM((2, tile, nblk * LANES)...  2.48 us
  transfers between devices with their start and end apart: 15, of which 6 were waited for; matrix products, arithmetic and copies ran while one was open for 1% of the time, Pallas kernels for 11%

profile of v10, /device:TPU:1, one launch (start us, length us, event | category | flops | bytes accessed | tf_op | source)
XLA Modules:
  0.0 79.1 jit_solution(10923939535434640537)
XLA Ops:
  0.6 1.1 %halo_rows.1 = (bf16[2,128,512]{2,1,0:T(8,128)(2,1)S(1)}, bf16[4,128,128]{2,1,0:T(8,128)(2,1)S(1)}, bf16[2,128,256]{2,1,0:T(8,128)(2,1)S(1)}) custom-call(bf16[2,512,512]{2,1,0:T(8,128)(2,1)} %mid_hbm.1), custom_call_target="tpu_custom_call" | custom-call | tf_op jit(solution)/shard_map/halo_rows/pallas_call | solution.py:90
  1.8 2.5 %collective-permute-start = (bf16[2,128,512]{2,1,0:T(8,128)(2,1)S(1)}, bf16[2,128,512]{2,1,0:T(8,128)(2,1)S(1)}, u32[]{:S(2)}, u32[]{:S(2)}) collective-permute-start(bf16[2,128,512]{2,1,0:T(8,128)(2,1)S(1)} %get-tuple-element.34), channel_id=1, source_target_pairs={{0,16},{1,17},{2,18},{3,19},{4,20},{5,21},{6,22},{7,23},{8,24},{9,... | collective-permute-start | bytes 786440 | tf_op jit(solution)/shard_map/ppermute | solution.py:537
  4.3 1.0 %collective-permute-start.1 = (bf16[4,128,128]{2,1,0:T(8,128)(2,1)S(1)}, bf16[4,128,128]{2,1,0:T(8,128)(2,1)S(1)}, u32[]{:S(2)}, u32[]{:S(2)}) collective-permute-start(bf16[4,128,128]{2,1,0:T(8,128)(2,1)S(1)} %get-tuple-element.35), channel_id=1, source_target_pairs={{0,1},{1,0},{2,3},{3,2},{4,5},{5,4},{6,7},{7,6},{8,9},{9,8},{10,11... | collective-permute-start | bytes 393224 | tf_op jit(solution)/shard_map/ppermute | solution.py:537
  5.3 1.1 %halo_cols.1 = (bf16[2,512,128]{2,1,0:T(8,128)(2,1)S(1)}, bf16[2,512,128]{2,1,0:T(8,128)(2,1)S(1)}) custom-call(bf16[2,512,512]{2,1,0:T(8,128)(2,1)} %mid_hbm.1), custom_call_target="tpu_custom_call" | custom-call | tf_op jit(solution)/shard_map/halo_cols/pallas_call | solution.py:90
  7.0 1.2 %collective-permute-start.4 = (bf16[2,512,128]{2,1,0:T(8,128)(2,1)S(1)}, bf16[2,512,128]{2,1,0:T(8,128)(2,1)S(1)}, u32[]{:S(2)}, u32[]{:S(2)}) collective-permute-start(bf16[2,512,128]{2,1,0:T(8,128)(2,1)S(1)} %get-tuple-element.39), channel_id=1, source_target_pairs={{0,16},{1,2},{2,1},{3,4},{4,3},{5,6},{6,5},{7,8},{8,7},{9,10},{10,... | collective-permute-start | bytes 786440 | tf_op jit(solution)/shard_map/ppermute | solution.py:537
  8.1 2.2 %collective-permute-done.row_a.row_a_ref = bf16[2,128,512]{2,1,0:T(8,128)(2,1)S(1)} collective-permute-done((bf16[2,128,512]{2,1,0:T(8,128)(2,1)S(1)}, bf16[2,128,512]{2,1,0:T(8,128)(2,1)S(1)}, u32[]{:S(2)}, u32[]{:S(2)}) %collective-permute-start) | collective-permute-done | bytes 262176 | tf_op jit(solution)/shard_map/ppermute | solution.py:537
  10.4 1.3 %collective-permute-start.5 = (bf16[4,128,128]{2,1,0:T(8,128)(2,1)S(1)}, bf16[4,128,128]{2,1,0:T(8,128)(2,1)S(1)}, u32[]{:S(2)}, u32[]{:S(2)}) collective-permute-start(bf16[4,128,128]{2,1,0:T(8,128)(2,1)S(1)} %get-tuple-element.40), channel_id=1, source_target_pairs={{0,1},{1,0},{2,3},{3,2},{4,5},{5,4},{6,7},{7,6},{8,9},{9,8},{10,11... | collective-permute-start | bytes 393224 | tf_op jit(solution)/shard_map/ppermute | solution.py:537
  11.7 1.2 %collective-permute-start.6 = (bf16[4,128,128]{2,1,0:T(8,128)(2,1)S(1)}, bf16[4,128,128]{2,1,0:T(8,128)(2,1)S(1)}, u32[]{:S(2)}, u32[]{:S(2)}) collective-permute-start(bf16[4,128,128]{2,1,0:T(8,128)(2,1)S(1)} %get-tuple-element.41), channel_id=1, source_target_pairs={{0,16},{1,2},{2,1},{3,4},{4,3},{5,6},{6,5},{7,8},{8,7},{9,10},{10,... | collective-permute-start | bytes 393224 | tf_op jit(solution)/shard_map/ppermute | solution.py:537
  12.9 2.2 %prepare.1 = (f32[2,6,768,128]{3,2,1,0:T(8,128)S(1)}, f32[2,6,768,128]{3,2,1,0:T(8,128)S(1)}, f32[2,2,256,256]{3,2,1,0:T(8,128)S(1)}, f32[2,2,256,256]{3,2,1,0:T...) custom-call(bf16[2,512,512]{2,1,0:T(8,128)(2,1)} %mid_hbm.1, ...), custom_call_target="tpu_custom_call" | custom-call | flops 5000000000 | tf_op jit(solution)/shard_map/prepare/pallas_call | solution.py:303
  15.8 2.2 %collective-permute-done.6.cor_b_ref = bf16[4,128,128]{2,1,0:T(8,128)(2,1)S(1)} collective-permute-done((bf16[4,128,128]{2,1,0:T(8,128)(2,1)S(1)}, bf16[4,128,128]{2,1,0:T(8,128)(2,1)S(1)}, u32[]{:S(2)}, u32[]{:S(2)}) %collective-permute-start.6) | collective-permute-done | bytes 131104 | tf_op jit(solution)/shard_map/ppermute | solution.py:537
  18.0 15.9 %frames.1 = (f32[2,6,768,128]{3,2,1,0:T(8,128)S(1)}, f32[2,6,768,128]{3,2,1,0:T(8,128)S(1)}, f32[2,2,256,256]{3,2,1,0:T(8,128)S(1)}, f32[2,4,512,128]{3,2,1,0:T(...) custom-call(s32[1,1]{1,0:T(1,128)S(6)} %copy.17.count_ref, ...), custom_call_target="tpu_custom_call", output_to_operand_aliasing={{0}: (9, {}), {1}: (10, {}), {2}: (11, {})} | custom-call | tf_op jit(solution)/shard_map/frames/pallas_call | solution.py:325
  34.5 1.0 %collective-permute-done.7 = bf16[64,16,128]{2,1,0:T(8,128)(2,1)S(1)} collective-permute-done((bf16[64,16,128]{2,1,0:T(8,128)(2,1)S(1)}, bf16[64,16,128]{2,1,0:T(8,128)(2,1)S(1)}, u32[]{:S(2)}, u32[]{:S(2)}) %collective-permute-start.7) | collective-permute-done | bytes 262176 | tf_op jit(solution)/shard_map/ppermute | solution.py:537
  36.3 13.1 %all-to-all-start = ((bf16[64,16,128]{2,1,0:T(8,128)(2,1)}), bf16[64,16,128]{2,1,0:T(8,128)(2,1)S(1)}, u32[]{:S(2)}, u32[]{:S(2)}) async-start(bf16[64,16,128]{2,1,0:T(8,128)(2,1)} %add_convert_fusion), calls=%async_computation | async-start | bytes 524288 | tf_op jit(solution)/shard_map/all_to_all | solution.py:564
  49.5 1.3 %row_margins.1 = (bf16[2,4,128,128]{3,2,1,0:T(8,128)(2,1)S(1)}, bf16[2,4,128,128]{3,2,1,0:T(8,128)(2,1)S(1)}) custom-call(f32[2,4,128,128]{3,2,1,0:T(8,128)} %get-tuple-element.50.strip_a_hbm, f32[2,4,128,128]{3,2,1,0:T(8,128)} %get-tuple-element.51.strip_b_hbm, bf16[2,768,128]{2,1,0:T(8,128)(2,1)S(1)} %collective-permute-done.8.got_a_ref.col_a_ref, ...), custom_call_target="tpu_custom_call" | custom-call | flops 5000000000 | tf_op jit(solution)/shard_map/row_margins/pallas_call | solution.py:392
  50.8 1.1 %collective-permute-start.10 = (bf16[2,4,128,128]{3,2,1,0:T(8,128)(2,1)S(1)}, bf16[2,4,128,128]{3,2,1,0:T(8,128)(2,1)S(1)}, u32[]{:S(2)}, u32[]{:S(2)}) collective-permute-start(bf16[2,4,128,128]{3,2,1,0:T(8,128)(2,1)S(1)} %get-tuple-element.54), channel_id=1, source_target_pairs={{0,16},{1,17},{2,18},{3,19},{4,20},{5,21},{6,22},{7,23},{8,24},{9,... | collective-permute-start | bytes 786440 | tf_op jit(solution)/shard_map/ppermute | solution.py:537
  51.9 1.3 %collective-permute-start.11 = (bf16[2,4,128,128]{3,2,1,0:T(8,128)(2,1)S(1)}, bf16[2,4,128,128]{3,2,1,0:T(8,128)(2,1)S(1)}, u32[]{:S(2)}, u32[]{:S(2)}) collective-permute-start(bf16[2,4,128,128]{3,2,1,0:T(8,128)(2,1)S(1)} %get-tuple-element.55), channel_id=1, source_target_pairs={{0,1},{1,0},{2,3},{3,2},{4,5},{5,4},{6,7},{7,6},{8,9},{9,8},{10,11... | collective-permute-start | bytes 786440 | tf_op jit(solution)/shard_map/ppermute | solution.py:537
  53.2 5.6 %all-to-all-done.got_ref = bf16[64,16,128]{2,1,0:T(8,128)(2,1)S(1)} async-done(((bf16[64,16,128]{2,1,0:T(8,128)(2,1)}), bf16[64,16,128]{2,1,0:T(8,128)(2,1)S(1)}, u32[]{:S(2)}, u32[]{:S(2)}) %all-to-all-start) | async-done | bytes 262176 | tf_op jit(solution)/shard_map/all_to_all | solution.py:564
  58.7 0.8 peer_sum.1
  59.5 5.2 %all-to-all-start.1 = ((bf16[64,16,128]{2,1,0:T(8,128)(2,1)}), bf16[64,16,128]{2,1,0:T(8,128)(2,1)S(1)}, u32[]{:S(2)}, u32[]{:S(2)}) async-start(bf16[64,16,128]{2,1,0:T(8,128)(2,1)} %peer_sum.1), calls=%async_computation.1 | async-start | bytes 524288 | tf_op jit(solution)/shard_map/all_to_all | solution.py:569
  64.7 2.5 %finish_object.1 = f32[2,512,512]{2,1,0:T(8,128)} custom-call(f32[2,4,512,128]{3,2,1,0:T(8,128)} %get-tuple-element.57.part_hbm, bf16[2,768,128]{2,1,0:T(8,128)(2,1)S(1)} %collective-permute-done.8.got_a_ref.col_a_ref, bf16[2,768,128]{2,1,0:T(8,128)(2,1)S(1)} %collective-permute-done.9.got_b_ref.col_b_ref, ...), custom_call_target="tpu_custom_call" | custom-call | flops 5000000000 | tf_op jit(solution)/shard_map/finish_object/pallas_call | solution.py:457
  67.2 6.7 %all-to-all-done.1.part_ref = bf16[64,16,128]{2,1,0:T(8,128)(2,1)S(1)} async-done(((bf16[64,16,128]{2,1,0:T(8,128)(2,1)}), bf16[64,16,128]{2,1,0:T(8,128)(2,1)S(1)}, u32[]{:S(2)}, u32[]{:S(2)}) %all-to-all-start.1) | async-done | bytes 262176 | tf_op jit(solution)/shard_map/all_to_all | solution.py:569
  73.9 3.2 %collective-permute-start.12 = (bf16[64,16,128]{2,1,0:T(8,128)(2,1)S(1)}, bf16[64,16,128]{2,1,0:T(8,128)(2,1)S(1)}, u32[]{:S(2)}, u32[]{:S(2)}) collective-permute-start(bf16[64,16,128]{2,1,0:T(8,128)(2,1)S(1)} %all-to-all-done.1.part_ref), channel_id=1, source_target_pairs={{0,1},{1,0},{2,3},{3,2},{4,5},{5,4},{6,7},{7,6},{8,9},{9,8},{10,11... | collective-permute-start | bytes 786440 | tf_op jit(solution)/shard_map/ppermute | solution.py:537
  77.1 0.8 %finish_mine.1.so_far_hbm = f32[2,2,256,256]{3,2,1,0:T(8,128)} custom-call(bf16[64,16,128]{2,1,0:T(8,128)(2,1)S(1)} %all-to-all-done.1.part_ref), custom_call_target="tpu_custom_call" | custom-call | flops 5000000000 | tf_op jit(solution)/shard_map/finish_mine/pallas_call | solution.py:499
  78.3 0.8 %finish_theirs.1 = f32[2,2,256,256]{3,2,1,0:T(8,128)} custom-call(bf16[64,16,128]{2,1,0:T(8,128)(2,1)S(1)} %collective-permute-done.12.part_ref, f32[2,2,256,256]{3,2,1,0:T(8,128)} %finish_mine.1.so_far_hbm), custom_call_target="tpu_custom_call", output_to_operand_aliasing={{}: (1, {})} | custom-call | tf_op jit(solution)/shard_map/finish_theirs/pallas_call | solution.py:513
  (19 shorter events, 2.3 us)
Async XLA Ops:
  1.8 8.6 %collective-permute-start = (bf16[2,128,512]{2,1,0:T(8,128)(2,1)S(1)}, bf16[2,128,512]{2,1,0:T(8,128)(2,1)S(1)}, u32[]{:S(2)}, u32[]{:S(2)}) collective-permute-start(bf16[2,128,512]{2,1,0:T(8,128)(2,1)S(1)} %get-tuple-element.34), channel_id=1, source_target_pairs={{0,16},{1,17},{2,18},{3,19},{4,20},{5,21},{6,22},{7,23},{8,24},{9,... | collective-permute-start | bytes 786440 | tf_op jit(solution)/shard_map/ppermute | solution.py:537
  4.3 3.8 %collective-permute-start.1 = (bf16[4,128,128]{2,1,0:T(8,128)(2,1)S(1)}, bf16[4,128,128]{2,1,0:T(8,128)(2,1)S(1)}, u32[]{:S(2)}, u32[]{:S(2)}) collective-permute-start(bf16[4,128,128]{2,1,0:T(8,128)(2,1)S(1)} %get-tuple-element.35), channel_id=1, source_target_pairs={{0,1},{1,0},{2,3},{3,2},{4,5},{5,4},{6,7},{7,6},{8,9},{9,8},{10,11... | collective-permute-start | bytes 393224 | tf_op jit(solution)/shard_map/ppermute | solution.py:537
  5.3 10.5 %collective-permute-start.2 = (bf16[2,128,256]{2,1,0:T(8,128)(2,1)S(1)}, bf16[2,128,256]{2,1,0:T(8,128)(2,1)S(1)}, u32[]{:S(2)}, u32[]{:S(2)}) collective-permute-start(bf16[2,128,256]{2,1,0:T(8,128)(2,1)S(1)} %get-tuple-element.36), channel_id=1, source_target_pairs={{0,1},{1,0},{2,3},{3,2},{4,5},{5,4},{6,7},{7,6},{8,9},{9,8},{10,11... | collective-permute-start | bytes 393224 | tf_op jit(solution)/shard_map/ppermute | solution.py:537
  6.4 9.4 %collective-permute-start.3 = (bf16[2,512,128]{2,1,0:T(8,128)(2,1)S(1)}, bf16[2,512,128]{2,1,0:T(8,128)(2,1)S(1)}, u32[]{:S(2)}, u32[]{:S(2)}) collective-permute-start(bf16[2,512,128]{2,1,0:T(8,128)(2,1)S(1)} %get-tuple-element.38), channel_id=1, source_target_pairs={{0,1},{1,0},{2,3},{3,2},{4,5},{5,4},{6,7},{7,6},{8,9},{9,8},{10,11... | collective-permute-start | bytes 786440 | tf_op jit(solution)/shard_map/ppermute | solution.py:537
  7.0 8.8 %collective-permute-start.4 = (bf16[2,512,128]{2,1,0:T(8,128)(2,1)S(1)}, bf16[2,512,128]{2,1,0:T(8,128)(2,1)S(1)}, u32[]{:S(2)}, u32[]{:S(2)}) collective-permute-start(bf16[2,512,128]{2,1,0:T(8,128)(2,1)S(1)} %get-tuple-element.39), channel_id=1, source_target_pairs={{0,16},{1,2},{2,1},{3,4},{4,3},{5,6},{6,5},{7,8},{8,7},{9,10},{10,... | collective-permute-start | bytes 786440 | tf_op jit(solution)/shard_map/ppermute | solution.py:537
  10.4 5.4 %collective-permute-start.5 = (bf16[4,128,128]{2,1,0:T(8,128)(2,1)S(1)}, bf16[4,128,128]{2,1,0:T(8,128)(2,1)S(1)}, u32[]{:S(2)}, u32[]{:S(2)}) collective-permute-start(bf16[4,128,128]{2,1,0:T(8,128)(2,1)S(1)} %get-tuple-element.40), channel_id=1, source_target_pairs={{0,1},{1,0},{2,3},{3,2},{4,5},{5,4},{6,7},{7,6},{8,9},{9,8},{10,11... | collective-permute-start | bytes 393224 | tf_op jit(solution)/shard_map/ppermute | solution.py:537
  11.7 6.3 %collective-permute-start.6 = (bf16[4,128,128]{2,1,0:T(8,128)(2,1)S(1)}, bf16[4,128,128]{2,1,0:T(8,128)(2,1)S(1)}, u32[]{:S(2)}, u32[]{:S(2)}) collective-permute-start(bf16[4,128,128]{2,1,0:T(8,128)(2,1)S(1)} %get-tuple-element.41), channel_id=1, source_target_pairs={{0,16},{1,2},{2,1},{3,4},{4,3},{5,6},{6,5},{7,8},{8,7},{9,10},{10,... | collective-permute-start | bytes 393224 | tf_op jit(solution)/shard_map/ppermute | solution.py:537
  12.9 5.1 %copy-start = (s32[1,1,2,8]{3,2,1,0:T(2,128)S(1)}, s32[1,1,2,8]{3,2,1,0:T(2,128)}, u32[]{:S(2)}) copy-start(s32[1,1,2,8]{3,2,1,0:T(2,128)} %pos_ref.1) | copy-start | bytes 196
  33.9 1.6 %collective-permute-start.7 = (bf16[64,16,128]{2,1,0:T(8,128)(2,1)S(1)}, bf16[64,16,128]{2,1,0:T(8,128)(2,1)S(1)}, u32[]{:S(2)}, u32[]{:S(2)}) collective-permute-start(bf16[64,16,128]{2,1,0:T(8,128)(2,1)S(1)} %get-tuple-element.49), channel_id=1, source_target_pairs={{0,1},{1,0},{2,3},{3,2},{4,5},{5,4},{6,7},{7,6},{8,9},{9,8},{10,11... | collective-permute-start | bytes 786440 | tf_op jit(solution)/shard_map/ppermute | solution.py:537
  34.0 15.4 %collective-permute-start.8 = (bf16[2,768,128]{2,1,0:T(8,128)(2,1)}, bf16[2,768,128]{2,1,0:T(8,128)(2,1)S(1)}, u32[]{:S(2)}, u32[]{:S(2)}) collective-permute-start(bf16[2,768,128]{2,1,0:T(8,128)(2,1)} %get-tuple-element.52), channel_id=1, source_target_pairs={{0,1},{1,0},{2,3},{3,2},{4,5},{5,4},{6,7},{7,6},{8,9},{9,8},{10,11... | collective-permute-start | bytes 1179656 | tf_op jit(solution)/shard_map/ppermute | solution.py:537
  34.5 14.9 %collective-permute-start.9 = (bf16[2,768,128]{2,1,0:T(8,128)(2,1)}, bf16[2,768,128]{2,1,0:T(8,128)(2,1)S(1)}, u32[]{:S(2)}, u32[]{:S(2)}) collective-permute-start(bf16[2,768,128]{2,1,0:T(8,128)(2,1)} %get-tuple-element.53), channel_id=1, source_target_pairs={{0,16},{1,2},{2,1},{3,4},{4,3},{5,6},{6,5},{7,8},{8,7},{9,10},{10,... | collective-permute-start | bytes 1179656 | tf_op jit(solution)/shard_map/ppermute | solution.py:537
  36.3 22.4 %all-to-all-start = ((bf16[64,16,128]{2,1,0:T(8,128)(2,1)}), bf16[64,16,128]{2,1,0:T(8,128)(2,1)S(1)}, u32[]{:S(2)}, u32[]{:S(2)}) async-start(bf16[64,16,128]{2,1,0:T(8,128)(2,1)} %add_convert_fusion), calls=%async_computation | async-start | bytes 524288 | tf_op jit(solution)/shard_map/all_to_all | solution.py:564
  50.8 13.9 %collective-permute-start.10 = (bf16[2,4,128,128]{3,2,1,0:T(8,128)(2,1)S(1)}, bf16[2,4,128,128]{3,2,1,0:T(8,128)(2,1)S(1)}, u32[]{:S(2)}, u32[]{:S(2)}) collective-permute-start(bf16[2,4,128,128]{3,2,1,0:T(8,128)(2,1)S(1)} %get-tuple-element.54), channel_id=1, source_target_pairs={{0,16},{1,17},{2,18},{3,19},{4,20},{5,21},{6,22},{7,23},{8,24},{9,... | collective-permute-start | bytes 786440 | tf_op jit(solution)/shard_map/ppermute | solution.py:537
  51.9 12.8 %collective-permute-start.11 = (bf16[2,4,128,128]{3,2,1,0:T(8,128)(2,1)S(1)}, bf16[2,4,128,128]{3,2,1,0:T(8,128)(2,1)S(1)}, u32[]{:S(2)}, u32[]{:S(2)}) collective-permute-start(bf16[2,4,128,128]{3,2,1,0:T(8,128)(2,1)S(1)} %get-tuple-element.55), channel_id=1, source_target_pairs={{0,1},{1,0},{2,3},{3,2},{4,5},{5,4},{6,7},{7,6},{8,9},{9,8},{10,11... | collective-permute-start | bytes 786440 | tf_op jit(solution)/shard_map/ppermute | solution.py:537
  59.5 14.4 %all-to-all-start.1 = ((bf16[64,16,128]{2,1,0:T(8,128)(2,1)}), bf16[64,16,128]{2,1,0:T(8,128)(2,1)S(1)}, u32[]{:S(2)}, u32[]{:S(2)}) async-start(bf16[64,16,128]{2,1,0:T(8,128)(2,1)} %peer_sum.1), calls=%async_computation.1 | async-start | bytes 524288 | tf_op jit(solution)/shard_map/all_to_all | solution.py:569
  73.9 4.4 %collective-permute-start.12 = (bf16[64,16,128]{2,1,0:T(8,128)(2,1)S(1)}, bf16[64,16,128]{2,1,0:T(8,128)(2,1)S(1)}, u32[]{:S(2)}, u32[]{:S(2)}) collective-permute-start(bf16[64,16,128]{2,1,0:T(8,128)(2,1)S(1)} %all-to-all-done.1.part_ref), channel_id=1, source_target_pairs={{0,1},{1,0},{2,3},{3,2},{4,5},{5,4},{6,7},{7,6},{8,9},{9,8},{10,11... | collective-permute-start | bytes 786440 | tf_op jit(solution)/shard_map/ppermute | solution.py:537
